TPU v7x, 512 devices: a whole 4x4x16 slice. The times are simulated.
512 devices in a mesh: tm: 128 (over y, z, core), rep: 4 (over x).
Axes of the slice: x: 4, y: 4, z: 16, core: 2. Of those that a mesh axis runs over, the one named last changes fastest.
Arguments:
- separator_inverse: bfloat16 [512, 384, 384], P(('rep', 'tm')), parts along dimension 0, may hold values from -1 to 3, as said below
- separator_lower: bfloat16 [512, 384, 384], P(('rep', 'tm')), parts along dimension 0, may hold values from -0.15625 to 0.15625
- separator_upper: bfloat16 [512, 384, 384], P(('rep', 'tm')), parts along dimension 0, may hold values from -0.15625 to 0.15625
- top_diagonal: bfloat16 [512, 384, 384], P(('rep', 'tm')), parts along dimension 0, may hold values from -1 to 3, as said below
- top_coupling: bfloat16 [512, 384, 384], P(('rep', 'tm')), parts along dimension 0, may hold values from -0.3125 to 0.3125
- interior_inverse: bfloat16 [512, 384, 384], P(('rep', 'tm')), parts along dimension 0, may hold values from -1 to 3, as said below
- interior_lower: bfloat16 [512, 384, 384], P(('rep', 'tm')), parts along dimension 0, may hold values from -0.15625 to 0.15625
- interior_upper: bfloat16 [512, 384, 384], P(('rep', 'tm')), parts along dimension 0, may hold values from -0.15625 to 0.15625
Outputs:
- inverse_diagonal: bfloat16 [1024, 384, 384], P(('rep', 'tm')), parts along dimension 0
- inverse_below: bfloat16 [1024, 384, 384], P(('rep', 'tm')), parts along dimension 0
There are 4 independent parts, one for each index of `rep`. A program takes and returns all parts, laid end to end along the dimension named above; each array names one. Nothing has to cross between parts.
Inputs may be any that keep to these rules, and one draw needn't show every extreme that they name: `separator_inverse`: every block is symmetric. `top_diagonal`: every block is symmetric. `interior_inverse`: every block is symmetric.
All inputs are finite; a program needn't handle non-finite values.
Results may differ from a plain program's by a relative error of at most 0.006.
Values may be sent and summed in bfloat16 or wider, within the bound.
No kernel may reach another device: no remote copies, remote signals or barrier semaphores. Data moves between devices by JAX's collectives and lax.ppermute only.
A program may use at most 64 MiB of HBM per device.

v0:
```python
import jax
import jax.numpy as jnp
from jax import lax
from jax.sharding import PartitionSpec as P


def shifted(value, axis, steps):
    count = lax.axis_size(axis)
    pairs = [(source, (source + steps) % count) for source in range(count)]
    return lax.ppermute(value, axis, pairs)


def product(left_op, right_op):
    return jnp.dot(left_op, right_op, preferred_element_type=jnp.float32)


def product_transposed(left_op, right_op):
    return lax.dot_general(
        left_op, right_op, (((1,), (1,)), ((), ())), preferred_element_type=jnp.float32
    )


def descend(inverse, lower_mult, upper_mult, lower_diagonal, coupling, upper_diagonal):
    toward_lower = (product(lower_mult, lower_diagonal) + product(upper_mult, coupling)).astype(
        jnp.bfloat16
    )
    toward_upper = (
        product_transposed(lower_mult, coupling) + product(upper_mult, upper_diagonal)
    ).astype(jnp.bfloat16)
    diagonal_new = (
        inverse.astype(jnp.float32)
        + product_transposed(toward_lower, lower_mult)
        + product_transposed(toward_upper, upper_mult)
    ).astype(jnp.bfloat16)
    return (toward_lower, toward_upper, diagonal_new)


def on_device(
    separator_inverse,
    separator_lower,
    separator_upper,
    top_diagonal,
    top_coupling,
    interior_inverse,
    interior_lower,
    interior_upper,
):
    devices = lax.axis_size("tm")
    levels_total = min(4, devices // 4)
    spacing = 2**levels_total
    position = (lax.axis_index("tm") + spacing // 2) % devices
    blank = jnp.zeros(separator_inverse.shape[1:], jnp.bfloat16)
    topmost = position % spacing == 0
    sigma_diagonal = jnp.where(topmost, top_diagonal[0], blank)
    sigma_upper = jnp.where(topmost, top_coupling[0], blank)
    sigma_lower = blank
    for height in range(levels_total, 0, -1):
        offset = 2 ** (height - 1)
        stride = 2 * offset
        lower_diagonal, lower_coupling = shifted((sigma_diagonal, sigma_upper), "tm", offset)
        upper_diagonal, upper_coupling = shifted((sigma_diagonal, sigma_lower), "tm", -offset)
        lower_holds = jnp.logical_or(height == levels_total, position // stride % 2 == 1)
        coupling = jnp.where(lower_holds, lower_coupling.T, upper_coupling)
        removed = position % stride == offset
        toward_lower, toward_upper, diagonal_new = descend(
            separator_inverse[0],
            separator_lower[0],
            separator_upper[0],
            lower_diagonal,
            coupling,
            upper_diagonal,
        )
        sigma_lower = jnp.where(removed, toward_lower, sigma_lower)
        sigma_upper = jnp.where(removed, toward_upper, sigma_upper)
        sigma_diagonal = jnp.where(removed, diagonal_new, sigma_diagonal)
    next_diagonal, next_lower = shifted((sigma_diagonal, sigma_lower), "tm", -1)
    coupling = jnp.where(position % 2 == 1, sigma_upper.T, next_lower)
    below_own, below_next, interior_diagonal = descend(
        interior_inverse[0],
        interior_lower[0],
        interior_upper[0],
        sigma_diagonal,
        coupling,
        next_diagonal,
    )
    return (jnp.stack([sigma_diagonal, interior_diagonal]), jnp.stack([below_own, below_next.T]))


def solution(mesh):
    in_specs = (
        P(("rep", "tm"), None, None),
        P(("rep", "tm"), None, None),
        P(("rep", "tm"), None, None),
        P(("rep", "tm"), None, None),
        P(("rep", "tm"), None, None),
        P(("rep", "tm"), None, None),
        P(("rep", "tm"), None, None),
        P(("rep", "tm"), None, None),
    )
    out_specs = (P(("rep", "tm"), None, None), P(("rep", "tm"), None, None))
    return jax.shard_map(
        on_device, mesh=mesh, in_specs=in_specs, out_specs=out_specs, check_vma=False
    )
```

profile of v0, /device:TPU:1, one launch (start us, length us, event | category | flops | bytes accessed | tf_op | source)
XLA Modules:
  0.0 162.0 jit_solution(13019431863252528924)
XLA Ops:
  0.8 9.8 %collective-permute-start.1 = (bf16[384,384]{1,0:T(8,128)(2,1)S(1)}, bf16[384,384]{1,0:T(8,128)(2,1)S(1)}, u32[]{:S(2)}, u32[]{:S(2)}) collective-permute-start(bf16[384,384]{1,0:T(8,128)(2,1)S(1)} %select_bitcast_fusion.1), channel_id=1, source_target_pairs={{0,32},{4,36},{8,40},{12,44},{16,48},{20,52},{24,56},{28,60},{32,6... | collective-permute-start | bytes 884744 | tf_op jit(solution)/shard_map/ppermute | solution.py:10
  10.6 8.8 %collective-permute-start = (bf16[384,384]{1,0:T(8,128)(2,1)S(1)}, bf16[384,384]{1,0:T(8,128)(2,1)S(1)}, u32[]{:S(2)}, u32[]{:S(2)}) collective-permute-start(bf16[384,384]{1,0:T(8,128)(2,1)S(1)} %select_bitcast_fusion.2), channel_id=1, source_target_pairs={{0,32},{4,36},{8,40},{12,44},{16,48},{20,52},{24,56},{28,60},{32,6... | collective-permute-start | bytes 884744 | tf_op jit(solution)/shard_map/ppermute | solution.py:10
  19.4 2.5 %collective-permute-start.2 = (bf16[384,384]{1,0:T(8,128)(2,1)S(1)}, bf16[384,384]{1,0:T(8,128)(2,1)S(1)}, u32[]{:S(2)}, u32[]{:S(2)}) collective-permute-start(bf16[384,384]{1,0:T(8,128)(2,1)S(1)} %select_bitcast_fusion.2), channel_id=1, source_target_pairs={{0,480},{4,484},{8,488},{12,492},{16,496},{20,500},{24,504},{28,50... | collective-permute-start | bytes 884744 | tf_op jit(solution)/shard_map/ppermute | solution.py:10
  21.9 2.2 %collective-permute-done.1 = bf16[384,384]{1,0:T(8,128)(2,1)S(1)} collective-permute-done((bf16[384,384]{1,0:T(8,128)(2,1)S(1)}, bf16[384,384]{1,0:T(8,128)(2,1)S(1)}, u32[]{:S(2)}, u32[]{:S(2)}) %collective-permute-start.1) | collective-permute-done | bytes 294944 | tf_op jit(solution)/shard_map/ppermute | solution.py:10
  24.5 12.0 %collective-permute-done = bf16[384,384]{1,0:T(8,128)(2,1)S(1)} collective-permute-done((bf16[384,384]{1,0:T(8,128)(2,1)S(1)}, bf16[384,384]{1,0:T(8,128)(2,1)S(1)}, u32[]{:S(2)}, u32[]{:S(2)}) %collective-permute-start) | collective-permute-done | bytes 294944 | tf_op jit(solution)/shard_map/ppermute | solution.py:10
  38.3 12.3 %collective-permute-done.2 = bf16[384,384]{1,0:T(8,128)(2,1)S(1)} collective-permute-done((bf16[384,384]{1,0:T(8,128)(2,1)S(1)}, bf16[384,384]{1,0:T(8,128)(2,1)S(1)}, u32[]{:S(2)}, u32[]{:S(2)}) %collective-permute-start.2) | collective-permute-done | bytes 294944 | tf_op jit(solution)/shard_map/ppermute | solution.py:10
  51.4 15.2 %collective-permute-start.4 = (bf16[384,384]{1,0:T(8,128)(2,1)S(1)}, bf16[384,384]{1,0:T(8,128)(2,1)S(1)}, u32[]{:S(2)}, u32[]{:S(2)}) collective-permute-start(bf16[384,384]{1,0:T(8,128)(2,1)S(1)} %get-tuple-element.4), channel_id=1, source_target_pairs={{0,16},{4,20},{8,24},{12,28},{16,32},{20,36},{24,40},{28,44},{32,4... | collective-permute-start | bytes 884744 | tf_op jit(solution)/shard_map/ppermute | solution.py:10
  66.6 6.1 %collective-permute-start.5 = (bf16[384,384]{0,1:T(8,128)(2,1)S(1)}, bf16[384,384]{0,1:T(8,128)(2,1)S(1)}, u32[]{:S(2)}, u32[]{:S(2)}) collective-permute-start(bf16[384,384]{0,1:T(8,128)(2,1)S(1)} %select_bitcast_fusion), channel_id=1, source_target_pairs={{0,496},{4,500},{8,504},{12,508},{16,0},{20,4},{24,8},{28,12},{32,... | collective-permute-start | bytes 884744 | tf_op jit(solution)/shard_map/ppermute | solution.py:10
  73.1 3.5 %collective-permute-start.3 = (bf16[384,384]{1,0:T(8,128)(2,1)S(1)}, bf16[384,384]{1,0:T(8,128)(2,1)S(1)}, u32[]{:S(2)}, u32[]{:S(2)}) collective-permute-start(bf16[384,384]{1,0:T(8,128)(2,1)S(1)} %fusion.19), channel_id=1, source_target_pairs={{0,16},{4,20},{8,24},{12,28},{16,32},{20,36},{24,40},{28,44},{32,4... | collective-permute-start | bytes 884744 | tf_op jit(solution)/shard_map/ppermute | solution.py:10
  76.6 6.0 %collective-permute-start.6 = (bf16[384,384]{1,0:T(8,128)(2,1)S(1)}, bf16[384,384]{1,0:T(8,128)(2,1)S(1)}, u32[]{:S(2)}, u32[]{:S(2)}) collective-permute-start(bf16[384,384]{1,0:T(8,128)(2,1)S(1)} %fusion.19), channel_id=1, source_target_pairs={{0,496},{4,500},{8,504},{12,508},{16,0},{20,4},{24,8},{28,12},{32,... | collective-permute-start | bytes 884744 | tf_op jit(solution)/shard_map/ppermute | solution.py:10
  83.0 13.0 %collective-permute-done.3 = bf16[384,384]{1,0:T(8,128)(2,1)S(1)} collective-permute-done((bf16[384,384]{1,0:T(8,128)(2,1)S(1)}, bf16[384,384]{1,0:T(8,128)(2,1)S(1)}, u32[]{:S(2)}, u32[]{:S(2)}) %collective-permute-start.3) | collective-permute-done | bytes 294944 | tf_op jit(solution)/shard_map/ppermute | solution.py:10
  96.8 1.4 collective-permute-done.6
  98.9 7.9 %collective-permute-start.8 = (bf16[384,384]{1,0:T(8,128)(2,1)S(1)}, bf16[384,384]{1,0:T(8,128)(2,1)S(1)}, u32[]{:S(2)}, u32[]{:S(2)}) collective-permute-start(bf16[384,384]{1,0:T(8,128)(2,1)S(1)} %get-tuple-element.8), channel_id=1, source_target_pairs={{0,8},{4,12},{8,16},{12,20},{16,24},{20,28},{24,32},{28,36},{32,40... | collective-permute-start | bytes 884744 | tf_op jit(solution)/shard_map/ppermute | solution.py:10
  106.9 1.9 %collective-permute-start.9 = (bf16[384,384]{0,1:T(8,128)(2,1)S(1)}, bf16[384,384]{0,1:T(8,128)(2,1)S(1)}, u32[]{:S(2)}, u32[]{:S(2)}) collective-permute-start(bf16[384,384]{0,1:T(8,128)(2,1)S(1)} %get-tuple-element.6), channel_id=1, source_target_pairs={{0,504},{4,508},{8,0},{12,4},{16,8},{20,12},{24,16},{28,20},{32,24... | collective-permute-start | bytes 884744 | tf_op jit(solution)/shard_map/ppermute | solution.py:10
  109.1 3.4 %collective-permute-start.7 = (bf16[384,384]{1,0:T(8,128)(2,1)S(1)}, bf16[384,384]{1,0:T(8,128)(2,1)S(1)}, u32[]{:S(2)}, u32[]{:S(2)}) collective-permute-start(bf16[384,384]{1,0:T(8,128)(2,1)S(1)} %fusion.18), channel_id=1, source_target_pairs={{0,8},{4,12},{8,16},{12,20},{16,24},{20,28},{24,32},{28,36},{32,40... | collective-permute-start | bytes 884744 | tf_op jit(solution)/shard_map/ppermute | solution.py:10
  112.6 5.2 %collective-permute-start.10 = (bf16[384,384]{1,0:T(8,128)(2,1)S(1)}, bf16[384,384]{1,0:T(8,128)(2,1)S(1)}, u32[]{:S(2)}, u32[]{:S(2)}) collective-permute-start(bf16[384,384]{1,0:T(8,128)(2,1)S(1)} %fusion.18), channel_id=1, source_target_pairs={{0,504},{4,508},{8,0},{12,4},{16,8},{20,12},{24,16},{28,20},{32,24... | collective-permute-start | bytes 884744 | tf_op jit(solution)/shard_map/ppermute | solution.py:10
  118.2 2.9 %collective-permute-done.7 = bf16[384,384]{1,0:T(8,128)(2,1)S(1)} collective-permute-done((bf16[384,384]{1,0:T(8,128)(2,1)S(1)}, bf16[384,384]{1,0:T(8,128)(2,1)S(1)}, u32[]{:S(2)}, u32[]{:S(2)}) %collective-permute-start.7) | collective-permute-done | bytes 294944 | tf_op jit(solution)/shard_map/ppermute | solution.py:10
  123.6 5.3 %collective-permute-start.12 = (bf16[384,384]{1,0:T(8,128)(2,1)S(1)}, bf16[384,384]{1,0:T(8,128)(2,1)S(1)}, u32[]{:S(2)}, u32[]{:S(2)}) collective-permute-start(bf16[384,384]{1,0:T(8,128)(2,1)S(1)} %get-tuple-element.12), channel_id=1, source_target_pairs={{0,4},{4,8},{8,12},{12,16},{16,20},{20,24},{24,28},{28,32},{32,36}... | collective-permute-start | bytes 884744 | tf_op jit(solution)/shard_map/ppermute | solution.py:10
  128.9 1.9 %collective-permute-start.13 = (bf16[384,384]{0,1:T(8,128)(2,1)S(1)}, bf16[384,384]{0,1:T(8,128)(2,1)S(1)}, u32[]{:S(2)}, u32[]{:S(2)}) collective-permute-start(bf16[384,384]{0,1:T(8,128)(2,1)S(1)} %get-tuple-element.10), channel_id=1, source_target_pairs={{0,508},{4,0},{8,4},{12,8},{16,12},{20,16},{24,20},{28,24},{32,28}... | collective-permute-start | bytes 884744 | tf_op jit(solution)/shard_map/ppermute | solution.py:10
  131.2 3.6 %collective-permute-start.11 = (bf16[384,384]{1,0:T(8,128)(2,1)S(1)}, bf16[384,384]{1,0:T(8,128)(2,1)S(1)}, u32[]{:S(2)}, u32[]{:S(2)}) collective-permute-start(bf16[384,384]{1,0:T(8,128)(2,1)S(1)} %fusion.17), channel_id=1, source_target_pairs={{0,4},{4,8},{8,12},{12,16},{16,20},{20,24},{24,28},{28,32},{32,36}... | collective-permute-start | bytes 884744 | tf_op jit(solution)/shard_map/ppermute | solution.py:10
  134.9 4.0 %collective-permute-start.14 = (bf16[384,384]{1,0:T(8,128)(2,1)S(1)}, bf16[384,384]{1,0:T(8,128)(2,1)S(1)}, u32[]{:S(2)}, u32[]{:S(2)}) collective-permute-start(bf16[384,384]{1,0:T(8,128)(2,1)S(1)} %fusion.17), channel_id=1, source_target_pairs={{0,508},{4,0},{8,4},{12,8},{16,12},{20,16},{24,20},{28,24},{32,28}... | collective-permute-start | bytes 884744 | tf_op jit(solution)/shard_map/ppermute | solution.py:10
  139.6 9.0 %collective-permute-start.15 = (bf16[384,384]{0,1:T(8,128)(2,1)S(1)}, bf16[384,384]{0,1:T(8,128)(2,1)S(1)}, u32[]{:S(2)}, u32[]{:S(2)}) collective-permute-start(bf16[384,384]{0,1:T(8,128)(2,1)S(1)} %get-tuple-element.14), channel_id=1, source_target_pairs={{0,508},{4,0},{8,4},{12,8},{16,12},{20,16},{24,20},{28,24},{32,28}... | collective-permute-start | bytes 884744 | tf_op jit(solution)/shard_map/ppermute | solution.py:10
  150.1 1.9 %collective-permute-start.16 = (bf16[384,384]{1,0:T(8,128)(2,1)S(1)}, bf16[384,384]{1,0:T(8,128)(2,1)S(1)}, u32[]{:S(2)}, u32[]{:S(2)}) collective-permute-start(bf16[384,384]{1,0:T(8,128)(2,1)S(1)} %fusion.16), channel_id=1, source_target_pairs={{0,508},{4,0},{8,4},{12,8},{16,12},{20,16},{24,20},{28,24},{32,28}... | collective-permute-start | bytes 884744 | tf_op jit(solution)/shard_map/ppermute | solution.py:10
  152.6 5.6 %collective-permute-done.16 = bf16[384,384]{1,0:T(8,128)(2,1)S(1)} collective-permute-done((bf16[384,384]{1,0:T(8,128)(2,1)S(1)}, bf16[384,384]{1,0:T(8,128)(2,1)S(1)}, u32[]{:S(2)}, u32[]{:S(2)}) %collective-permute-start.16) | collective-permute-done | bytes 294944 | tf_op jit(solution)/shard_map/ppermute | solution.py:10
  (61 shorter events, 15.0 us)
Async XLA Ops:
  0.6 35.9 %copy-start = (bf16[1,384,384]{2,1,0:T(8,128)(2,1)S(1)}, bf16[1,384,384]{2,1,0:T(8,128)(2,1)}, u32[]{:S(2)}) copy-start(bf16[1,384,384]{2,1,0:T(8,128)(2,1)} %param.9) | copy-start | bytes 884740
  0.7 9.8 %copy-start.5 = (bf16[1,384,384]{2,1,0:T(8,128)(2,1)S(1)}, bf16[1,384,384]{2,1,0:T(8,128)(2,1)}, u32[]{:S(2)}) copy-start(bf16[1,384,384]{2,1,0:T(8,128)(2,1)} %param.11) | copy-start | bytes 884740
  0.7 23.4 %copy-start.1 = (bf16[1,384,384]{2,1,0:T(8,128)(2,1)S(1)}, bf16[1,384,384]{2,1,0:T(8,128)(2,1)}, u32[]{:S(2)}) copy-start(bf16[1,384,384]{2,1,0:T(8,128)(2,1)} %param.10) | copy-start | bytes 884740
  0.8 23.4 %collective-permute-start.1 = (bf16[384,384]{1,0:T(8,128)(2,1)S(1)}, bf16[384,384]{1,0:T(8,128)(2,1)S(1)}, u32[]{:S(2)}, u32[]{:S(2)}) collective-permute-start(bf16[384,384]{1,0:T(8,128)(2,1)S(1)} %select_bitcast_fusion.1), channel_id=1, source_target_pairs={{0,32},{4,36},{8,40},{12,44},{16,48},{20,52},{24,56},{28,60},{32,6... | collective-permute-start | bytes 884744 | tf_op jit(solution)/shard_map/ppermute | solution.py:10
  10.6 26.0 %collective-permute-start = (bf16[384,384]{1,0:T(8,128)(2,1)S(1)}, bf16[384,384]{1,0:T(8,128)(2,1)S(1)}, u32[]{:S(2)}, u32[]{:S(2)}) collective-permute-start(bf16[384,384]{1,0:T(8,128)(2,1)S(1)} %select_bitcast_fusion.2), channel_id=1, source_target_pairs={{0,32},{4,36},{8,40},{12,44},{16,48},{20,52},{24,56},{28,60},{32,6... | collective-permute-start | bytes 884744 | tf_op jit(solution)/shard_map/ppermute | solution.py:10
  19.4 31.3 %collective-permute-start.2 = (bf16[384,384]{1,0:T(8,128)(2,1)S(1)}, bf16[384,384]{1,0:T(8,128)(2,1)S(1)}, u32[]{:S(2)}, u32[]{:S(2)}) collective-permute-start(bf16[384,384]{1,0:T(8,128)(2,1)S(1)} %select_bitcast_fusion.2), channel_id=1, source_target_pairs={{0,480},{4,484},{8,488},{12,492},{16,496},{20,500},{24,504},{28,50... | collective-permute-start | bytes 884744 | tf_op jit(solution)/shard_map/ppermute | solution.py:10
  36.9 1.0 copy-start.2
  51.4 31.3 %collective-permute-start.4 = (bf16[384,384]{1,0:T(8,128)(2,1)S(1)}, bf16[384,384]{1,0:T(8,128)(2,1)S(1)}, u32[]{:S(2)}, u32[]{:S(2)}) collective-permute-start(bf16[384,384]{1,0:T(8,128)(2,1)S(1)} %get-tuple-element.4), channel_id=1, source_target_pairs={{0,16},{4,20},{8,24},{12,28},{16,32},{20,36},{24,40},{28,44},{32,4... | collective-permute-start | bytes 884744 | tf_op jit(solution)/shard_map/ppermute | solution.py:10
  66.6 16.0 %collective-permute-start.5 = (bf16[384,384]{0,1:T(8,128)(2,1)S(1)}, bf16[384,384]{0,1:T(8,128)(2,1)S(1)}, u32[]{:S(2)}, u32[]{:S(2)}) collective-permute-start(bf16[384,384]{0,1:T(8,128)(2,1)S(1)} %select_bitcast_fusion), channel_id=1, source_target_pairs={{0,496},{4,500},{8,504},{12,508},{16,0},{20,4},{24,8},{28,12},{32,... | collective-permute-start | bytes 884744 | tf_op jit(solution)/shard_map/ppermute | solution.py:10
  73.1 23.0 %collective-permute-start.3 = (bf16[384,384]{1,0:T(8,128)(2,1)S(1)}, bf16[384,384]{1,0:T(8,128)(2,1)S(1)}, u32[]{:S(2)}, u32[]{:S(2)}) collective-permute-start(bf16[384,384]{1,0:T(8,128)(2,1)S(1)} %fusion.19), channel_id=1, source_target_pairs={{0,16},{4,20},{8,24},{12,28},{16,32},{20,36},{24,40},{28,44},{32,4... | collective-permute-start | bytes 884744 | tf_op jit(solution)/shard_map/ppermute | solution.py:10
  76.6 21.6 %collective-permute-start.6 = (bf16[384,384]{1,0:T(8,128)(2,1)S(1)}, bf16[384,384]{1,0:T(8,128)(2,1)S(1)}, u32[]{:S(2)}, u32[]{:S(2)}) collective-permute-start(bf16[384,384]{1,0:T(8,128)(2,1)S(1)} %fusion.19), channel_id=1, source_target_pairs={{0,496},{4,500},{8,504},{12,508},{16,0},{20,4},{24,8},{28,12},{32,... | collective-permute-start | bytes 884744 | tf_op jit(solution)/shard_map/ppermute | solution.py:10
  98.9 18.9 %collective-permute-start.8 = (bf16[384,384]{1,0:T(8,128)(2,1)S(1)}, bf16[384,384]{1,0:T(8,128)(2,1)S(1)}, u32[]{:S(2)}, u32[]{:S(2)}) collective-permute-start(bf16[384,384]{1,0:T(8,128)(2,1)S(1)} %get-tuple-element.8), channel_id=1, source_target_pairs={{0,8},{4,12},{8,16},{12,20},{16,24},{20,28},{24,32},{28,36},{32,40... | collective-permute-start | bytes 884744 | tf_op jit(solution)/shard_map/ppermute | solution.py:10
  106.9 11.0 %collective-permute-start.9 = (bf16[384,384]{0,1:T(8,128)(2,1)S(1)}, bf16[384,384]{0,1:T(8,128)(2,1)S(1)}, u32[]{:S(2)}, u32[]{:S(2)}) collective-permute-start(bf16[384,384]{0,1:T(8,128)(2,1)S(1)} %get-tuple-element.6), channel_id=1, source_target_pairs={{0,504},{4,508},{8,0},{12,4},{16,8},{20,12},{24,16},{28,20},{32,24... | collective-permute-start | bytes 884744 | tf_op jit(solution)/shard_map/ppermute | solution.py:10
  109.1 11.9 %collective-permute-start.7 = (bf16[384,384]{1,0:T(8,128)(2,1)S(1)}, bf16[384,384]{1,0:T(8,128)(2,1)S(1)}, u32[]{:S(2)}, u32[]{:S(2)}) collective-permute-start(bf16[384,384]{1,0:T(8,128)(2,1)S(1)} %fusion.18), channel_id=1, source_target_pairs={{0,8},{4,12},{8,16},{12,20},{16,24},{20,28},{24,32},{28,36},{32,40... | collective-permute-start | bytes 884744 | tf_op jit(solution)/shard_map/ppermute | solution.py:10
  112.6 10.3 %collective-permute-start.10 = (bf16[384,384]{1,0:T(8,128)(2,1)S(1)}, bf16[384,384]{1,0:T(8,128)(2,1)S(1)}, u32[]{:S(2)}, u32[]{:S(2)}) collective-permute-start(bf16[384,384]{1,0:T(8,128)(2,1)S(1)} %fusion.18), channel_id=1, source_target_pairs={{0,504},{4,508},{8,0},{12,4},{16,8},{20,12},{24,16},{28,20},{32,24... | collective-permute-start | bytes 884744 | tf_op jit(solution)/shard_map/ppermute | solution.py:10
  123.6 15.3 %collective-permute-start.12 = (bf16[384,384]{1,0:T(8,128)(2,1)S(1)}, bf16[384,384]{1,0:T(8,128)(2,1)S(1)}, u32[]{:S(2)}, u32[]{:S(2)}) collective-permute-start(bf16[384,384]{1,0:T(8,128)(2,1)S(1)} %get-tuple-element.12), channel_id=1, source_target_pairs={{0,4},{4,8},{8,12},{12,16},{16,20},{20,24},{24,28},{28,32},{32,36}... | collective-permute-start | bytes 884744 | tf_op jit(solution)/shard_map/ppermute | solution.py:10
  128.9 10.0 %collective-permute-start.13 = (bf16[384,384]{0,1:T(8,128)(2,1)S(1)}, bf16[384,384]{0,1:T(8,128)(2,1)S(1)}, u32[]{:S(2)}, u32[]{:S(2)}) collective-permute-start(bf16[384,384]{0,1:T(8,128)(2,1)S(1)} %get-tuple-element.10), channel_id=1, source_target_pairs={{0,508},{4,0},{8,4},{12,8},{16,12},{20,16},{24,20},{28,24},{32,28}... | collective-permute-start | bytes 884744 | tf_op jit(solution)/shard_map/ppermute | solution.py:10
  131.2 8.1 %collective-permute-start.11 = (bf16[384,384]{1,0:T(8,128)(2,1)S(1)}, bf16[384,384]{1,0:T(8,128)(2,1)S(1)}, u32[]{:S(2)}, u32[]{:S(2)}) collective-permute-start(bf16[384,384]{1,0:T(8,128)(2,1)S(1)} %fusion.17), channel_id=1, source_target_pairs={{0,4},{4,8},{8,12},{12,16},{16,20},{20,24},{24,28},{28,32},{32,36}... | collective-permute-start | bytes 884744 | tf_op jit(solution)/shard_map/ppermute | solution.py:10
  134.9 14.2 %collective-permute-start.14 = (bf16[384,384]{1,0:T(8,128)(2,1)S(1)}, bf16[384,384]{1,0:T(8,128)(2,1)S(1)}, u32[]{:S(2)}, u32[]{:S(2)}) collective-permute-start(bf16[384,384]{1,0:T(8,128)(2,1)S(1)} %fusion.17), channel_id=1, source_target_pairs={{0,508},{4,0},{8,4},{12,8},{16,12},{20,16},{24,20},{28,24},{32,28}... | collective-permute-start | bytes 884744 | tf_op jit(solution)/shard_map/ppermute | solution.py:10
  139.6 12.8 %collective-permute-start.15 = (bf16[384,384]{0,1:T(8,128)(2,1)S(1)}, bf16[384,384]{0,1:T(8,128)(2,1)S(1)}, u32[]{:S(2)}, u32[]{:S(2)}) collective-permute-start(bf16[384,384]{0,1:T(8,128)(2,1)S(1)} %get-tuple-element.14), channel_id=1, source_target_pairs={{0,508},{4,0},{8,4},{12,8},{16,12},{20,16},{24,20},{28,24},{32,28}... | collective-permute-start | bytes 884744 | tf_op jit(solution)/shard_map/ppermute | solution.py:10
  149.7 2.3 %copy-start.3 = (bf16[1,384,384]{2,1,0:T(8,128)(2,1)S(1)}, bf16[1,384,384]{2,1,0:T(8,128)(2,1)}, u32[]{:S(2)}) copy-start(bf16[1,384,384]{2,1,0:T(8,128)(2,1)} %param.14) | copy-start | bytes 884740
  150.1 8.0 %collective-permute-start.16 = (bf16[384,384]{1,0:T(8,128)(2,1)S(1)}, bf16[384,384]{1,0:T(8,128)(2,1)S(1)}, u32[]{:S(2)}, u32[]{:S(2)}) collective-permute-start(bf16[384,384]{1,0:T(8,128)(2,1)S(1)} %fusion.16), channel_id=1, source_target_pairs={{0,508},{4,0},{8,4},{12,8},{16,12},{20,16},{24,20},{28,24},{32,28}... | collective-permute-start | bytes 884744 | tf_op jit(solution)/shard_map/ppermute | solution.py:10
  152.5 5.7 %copy-start.4 = (bf16[1,384,384]{2,1,0:T(8,128)(2,1)S(1)}, bf16[1,384,384]{2,1,0:T(8,128)(2,1)}, u32[]{:S(2)}) copy-start(bf16[1,384,384]{2,1,0:T(8,128)(2,1)} %param.15) | copy-start | bytes 884740
  159.3 1.1 copy-start.6
where the time goes:
time: 164 us; the launch traced here: 162 us
  starting transfers between devices  96.1 us (59%)
  waiting for transfers between devices  50.5 us (31%)
  matrix products  10.9 us (7%)
  local copies, waits for them, and re-layouts  2.02 us (1%)
    ppermute x17, starting transfers between devices, shifted(): return lax.ppermute(value, axis, pairs)  96.1 us
    ppermute x17, waiting for transfers between devices, shifted(): return lax.ppermute(value, axis, pairs)  50.5 us
    dot_general x15, matrix products, product_transposed(): lax.dot_general(left_op, right_op, (((1,), (1,)), ((), ())), preferred_el...  5.51 us
    dot_general x15, matrix products, product(): return jnp.dot(left_op, right_op, preferred_element_type=jnp.float32)  5.41 us
  transfers between devices with their start and end apart: 17, of which 8 were waited for; matrix products, arithmetic and copies ran while one was open for 4% of the time, Pallas kernels for 0%

commit v1 on v0

v1 whole, which is shorter than its diff:
```python
import functools

import jax
import jax.numpy as jnp
from jax import lax
from jax.experimental import pallas as pl
from jax.experimental.pallas import tpu as pltpu
from jax.sharding import PartitionSpec as P

BF = jnp.bfloat16
F32 = jnp.float32
NT = (((1,), (1,)), ((), ()))


def mm(left_op, right_op):
    return jnp.dot(left_op, right_op, preferred_element_type=F32)


def mt(left_op, right_op):
    return lax.dot_general(left_op, right_op, NT, preferred_element_type=F32)


def level_kernel(height, holds_all, place, inv, low, up, from_low, from_up, own_up, own_down, out_up, out_down):
    n = low.shape[1]
    stride = 2**height
    removed = lax.rem(place[0], stride) == stride // 2
    holds = jnp.logical_or(holds_all, lax.rem(place[0], 2 * stride) >= stride)

    @pl.when(jnp.logical_not(removed))
    def _():
        out_up[...] = own_up[...]
        out_down[...] = own_down[...]

    def finish():
        diag = inv[0].astype(F32) + mt(out_down[n:, :], low[0]) + mt(out_up[n:, :], up[0])
        diag = diag.astype(BF)
        out_up[:n, :] = diag
        out_down[:n, :] = diag

    @pl.when(jnp.logical_and(removed, holds))
    def _():
        out_down[n:, :] = (mm(low[0], from_low[:n, :]) + mt(up[0], from_low[n:, :])).astype(BF)
        out_up[n:, :] = (mm(low[0], from_low[n:, :]) + mm(up[0], from_up[:n, :])).astype(BF)
        finish()

    @pl.when(jnp.logical_and(removed, jnp.logical_not(holds)))
    def _():
        out_down[n:, :] = (mm(low[0], from_low[:n, :]) + mm(up[0], from_up[n:, :])).astype(BF)
        out_up[n:, :] = (mt(low[0], from_up[n:, :]) + mm(up[0], from_up[:n, :])).astype(BF)
        finish()


def interior_kernel(place, inv, low, up, own_up, next_up, next_down, out_diag, out_below):
    n = low.shape[1]
    out_diag[0] = own_up[:n, :]

    def finish(below, above, next_diag):
        out_below[0] = below.astype(BF)
        above = above.astype(BF)
        out_below[1] = above.T
        diag = inv[0].astype(F32) + mt(out_below[0], low[0]) + mt(above, up[0])
        out_diag[1] = diag.astype(BF)

    @pl.when(lax.rem(place[0], 2) == 1)
    def _():
        finish(
            mm(low[0], own_up[:n, :]) + mt(up[0], own_up[n:, :]),
            mm(low[0], own_up[n:, :]) + mm(up[0], next_up[:n, :]),
            None,
        )

    @pl.when(lax.rem(place[0], 2) == 0)
    def _():
        finish(
            mm(low[0], own_up[:n, :]) + mm(up[0], next_down[n:, :]),
            mt(low[0], next_down[n:, :]) + mm(up[0], next_down[:n, :]),
            None,
        )


def on_device(
    separator_inverse,
    separator_lower,
    separator_upper,
    top_diagonal,
    top_coupling,
    interior_inverse,
    interior_lower,
    interior_upper,
):
    devices = lax.axis_size("tm")
    levels_total = min(4, devices // 4)
    spacing = 2**levels_total
    margin = spacing // 2
    n = separator_lower.shape[1]
    place = ((lax.axis_index("tm") + margin) % devices).astype(jnp.int32).reshape(1)

    def moved(value, places, step):
        pairs = [((p - margin) % devices, (p + step - margin) % devices) for p in places]
        return lax.ppermute(value, "tm", pairs)

    smem = pl.BlockSpec(memory_space=pltpu.SMEM)
    vmem = pl.BlockSpec(memory_space=pltpu.VMEM)
    message = pltpu.VMEM((2 * n, n), BF)

    def near(*values):
        return [pltpu.with_memory_space_constraint(v, pltpu.VMEM) for v in values]


    own_up = jnp.concatenate([top_diagonal[0], top_coupling[0]], axis=0)
    own_down = own_up
    from_up = None
    for height in range(levels_total, 0, -1):
        offset = 2 ** (height - 1)
        stride = 2 * offset
        middles = range(offset, devices, stride)
        from_low = moved(own_up, [m - offset for m in middles], offset)
        from_up = moved(own_down, [m + offset for m in middles], -offset)
        own_up, own_down = pl.pallas_call(
            functools.partial(level_kernel, height, height == levels_total),
            out_shape=(message, message),
            in_specs=[smem] + [vmem] * 7,
            out_specs=(vmem, vmem),
            compiler_params=pltpu.CompilerParams(vmem_limit_bytes=16 << 20),
            name=f"level{height}",
        )(
            place,
            separator_inverse,
            separator_lower,
            separator_upper,
            *near(from_low, from_up, own_up, own_down),
        )
    next_down = moved(own_down, range(1, devices, 2), -1)
    pair = jax.ShapeDtypeStruct((2, n, n), BF)
    return pl.pallas_call(
        interior_kernel,
        out_shape=(pair, pair),
        in_specs=[smem] + [vmem] * 6,
        out_specs=(vmem, vmem),
        compiler_params=pltpu.CompilerParams(vmem_limit_bytes=16 << 20),
        name="interior",
    )(place, interior_inverse, interior_lower, interior_upper, *near(own_up, from_up, next_down))


def solution(mesh):
    spec = P(("rep", "tm"), None, None)
    return jax.shard_map(
        on_device, mesh=mesh, in_specs=(spec,) * 8, out_specs=(spec, spec), check_vma=False
    )
```

time: 164 us -> 74.9 us (0.46); the launches traced: 162 us -> 74.7 us
  starting transfers between devices: 96.1 us -> 8.23 us
  matrix products: 10.9 us -> 0 us
  waiting for transfers between devices: 50.5 us -> 60.4 us
  Pallas kernels: 0 us -> 3.94 us
  local copies, waits for them, and re-layouts: 2.02 us -> 0.03 us
    ppermute x17 -> x9, starting transfers between devices: 96.1 us -> 8.23 us  [moved(): return lax.ppermute(value, 'tm', pairs)]
    dot_general x30 -> x0, matrix products: 10.9 us -> none  [the longest x15 5.51 us: product_transposed(): lax.dot_general(left_op, right_op, (((1,), (1,)), ((), ())), preferred_el...]
    ppermute x17 -> x9, waiting for transfers between devices: 50.5 us -> 60.4 us  [moved(): return lax.ppermute(value, 'tm', pairs)]
    pallas_call x0 -> x5, Pallas kernels: none -> 3.94 us  [the longest x1 2.32 us: on_device(): pl.pallas_call(interior_kernel, out_shape=(pair, pair), in_specs=[smem] +...]
    unnamed x15 -> x12, local copies, waits for them, and re-layouts: 2.02 us -> 0.03 us
  transfers between devices with their start and end apart: 17 -> 9, of which waited for: 8 -> 3; matrix products, arithmetic and copies ran while one was open for 4% -> 0% of each run, Pallas kernels for 0% -> 0%
where the time goes in v1:
time: 74.9 us; the launch traced here: 74.7 us
  waiting for transfers between devices  60.4 us (81%)
  starting transfers between devices  8.23 us (11%)
  Pallas kernels  3.94 us (5%)
  other arithmetic  1.19 us (2%)
  between operations  0.87 us (1%)
    ppermute x9, waiting for transfers between devices, moved(): return lax.ppermute(value, 'tm', pairs)  60.4 us
    ppermute x9, starting transfers between devices, moved(): return lax.ppermute(value, 'tm', pairs)  8.23 us
    pallas_call x1, Pallas kernels, on_device(): pl.pallas_call(interior_kernel, out_shape=(pair, pair), in_specs=[smem] +...  2.32 us
    pallas_call x4, Pallas kernels, on_device(): pl.pallas_call(functools.partial(level_kernel, height, height == levels_t...  1.62 us
  transfers between devices with their start and end apart: 9, of which 3 were waited for; matrix products, arithmetic and copies ran while one was open for 0% of the time, Pallas kernels for 0%

profile of v1, /device:TPU:1, one launch (start us, length us, event | category | flops | bytes accessed | tf_op | source)
XLA Modules:
  0.0 74.7 jit_solution(16371472051858503063)
XLA Ops:
  0.7 1.2 %pad_maximum_fusion.own_up.own_down = bf16[768,384]{1,0:T(8,128)(2,1)S(1)} fusion(bf16[384,384]{1,0:T(8,128)(2,1)} %bitcast.3, bf16[384,384]{1,0:T(8,128)(2,1)} %bitcast.4), kind=kLoop, calls=%fused_computation | loop fusion | flops 1179648 | bytes 1179648 | tf_op jit(solution)/shard_map/concatenate | solution.py:110
  1.8 0.7 collective-permute-start.1
  2.6 0.7 collective-permute-start
  3.3 0.0 collective-permute-done.from_low
  3.3 0.1 level4.1
  3.4 0.7 collective-permute-start.2
  4.2 0.7 collective-permute-start.3
  4.9 0.0 collective-permute-done.2.from_low
  4.9 0.0 collective-permute-done.3.from_up
  4.9 0.1 level3.1
  5.0 0.7 collective-permute-start.4
  5.7 0.7 collective-permute-start.5
  6.4 0.1 level2.1
  6.6 1.3 %collective-permute-start.6 = (bf16[768,384]{1,0:T(8,128)(2,1)S(1)}, bf16[768,384]{1,0:T(8,128)(2,1)S(1)}, u32[]{:S(2)}, u32[]{:S(2)}) collective-permute-start(bf16[768,384]{1,0:T(8,128)(2,1)S(1)} %get-tuple-element.14.own_up), channel_id=1, source_target_pairs={{480,484},{488,492},{496,500},{504,508},{0,4},{8,12},{16,20},{24,2... | collective-permute-start | bytes 1769480 | tf_op jit(solution)/shard_map/ppermute | solution.py:100
  7.9 0.0 copy-start.3
  7.9 0.0 copy-start.4
  7.9 0.0 copy-start.5
  7.9 1.4 %collective-permute-start.7 = (bf16[768,384]{1,0:T(8,128)(2,1)S(1)}, bf16[768,384]{1,0:T(8,128)(2,1)S(1)}, u32[]{:S(2)}, u32[]{:S(2)}) collective-permute-start(bf16[768,384]{1,0:T(8,128)(2,1)S(1)} %get-tuple-element.15.own_down), channel_id=1, source_target_pairs={{488,484},{496,492},{504,500},{0,508},{8,4},{16,12},{24,20},{32,28... | collective-permute-start | bytes 1769480 | tf_op jit(solution)/shard_map/ppermute | solution.py:100
  9.3 46.2 %collective-permute-done.6.from_low = bf16[768,384]{1,0:T(8,128)(2,1)S(1)} collective-permute-done((bf16[768,384]{1,0:T(8,128)(2,1)S(1)}, bf16[768,384]{1,0:T(8,128)(2,1)S(1)}, u32[]{:S(2)}, u32[]{:S(2)}) %collective-permute-start.6) | collective-permute-done | bytes 589856 | tf_op jit(solution)/shard_map/ppermute | solution.py:100
  55.6 12.6 %collective-permute-done.7.from_up.next_up = bf16[768,384]{1,0:T(8,128)(2,1)S(1)} collective-permute-done((bf16[768,384]{1,0:T(8,128)(2,1)S(1)}, bf16[768,384]{1,0:T(8,128)(2,1)S(1)}, u32[]{:S(2)}, u32[]{:S(2)}) %collective-permute-start.7) | collective-permute-done | bytes 589856 | tf_op jit(solution)/shard_map/ppermute | solution.py:100
  68.1 1.3 %level1.1 = (bf16[768,384]{1,0:T(8,128)(2,1)S(1)}, bf16[768,384]{1,0:T(8,128)(2,1)S(1)}) custom-call(s32[1]{0:T(128)} %bitcast.place, bf16[1,384,384]{2,1,0:T(8,128)(2,1)S(1)} %copy-done, bf16[1,384,384]{2,1,0:T(8,128)(2,1)S(1)} %copy-done.1, bf16[1,384,384]{2,1,0:T(8,128)(2,1)S(1)} %copy-done.2, bf16[768,384]{1,0:T(8,128)(2,1)S(1)} %collective-permute-done.6.from_low, ...), custom_call_target="tpu_custom_call" | custom-call | tf_op jit(solution)/shard_map/level1/pallas_call | solution.py:119
  69.4 1.3 %collective-permute-start.8 = (bf16[768,384]{1,0:T(8,128)(2,1)S(1)}, bf16[768,384]{1,0:T(8,128)(2,1)S(1)}, u32[]{:S(2)}, u32[]{:S(2)}) collective-permute-start(bf16[768,384]{1,0:T(8,128)(2,1)S(1)} %get-tuple-element.17), channel_id=1, source_target_pairs={{484,480},{492,488},{500,496},{508,504},{4,0},{12,8},{20,16},{28,2... | collective-permute-start | bytes 1769480 | tf_op jit(solution)/shard_map/ppermute | solution.py:100
  70.7 1.6 %collective-permute-done.8.next_down = bf16[768,384]{1,0:T(8,128)(2,1)S(1)} collective-permute-done((bf16[768,384]{1,0:T(8,128)(2,1)S(1)}, bf16[768,384]{1,0:T(8,128)(2,1)S(1)}, u32[]{:S(2)}, u32[]{:S(2)}) %collective-permute-start.8) | collective-permute-done | bytes 589856 | tf_op jit(solution)/shard_map/ppermute | solution.py:100
  72.3 2.3 %interior.1 = (bf16[2,384,384]{2,1,0:T(8,128)(2,1)}, bf16[2,384,384]{2,1,0:T(8,128)(2,1)}) custom-call(s32[1]{0:T(128)} %bitcast.place, bf16[1,384,384]{2,1,0:T(8,128)(2,1)S(1)} %copy-done.3, bf16[1,384,384]{2,1,0:T(8,128)(2,1)S(1)} %copy-done.4, bf16[1,384,384]{2,1,0:T(8,128)(2,1)S(1)} %copy-done.5, bf16[768,384]{1,0:T(8,128)(2,1)S(1)} %get-tuple-element.16.own_up, ...), custom_call_target="tpu_custom_call" | custom-call | tf_op jit(solution)/shard_map/interior/pallas_call | solution.py:135
  (12 shorter events, 0.0 us)
Async XLA Ops:
  0.6 2.7 %copy-start = (bf16[1,384,384]{2,1,0:T(8,128)(2,1)S(1)}, bf16[1,384,384]{2,1,0:T(8,128)(2,1)}, u32[]{:S(2)}) copy-start(bf16[1,384,384]{2,1,0:T(8,128)(2,1)} %inv.8) | copy-start | bytes 884740
  0.6 2.7 %copy-start.1 = (bf16[1,384,384]{2,1,0:T(8,128)(2,1)S(1)}, bf16[1,384,384]{2,1,0:T(8,128)(2,1)}, u32[]{:S(2)}) copy-start(bf16[1,384,384]{2,1,0:T(8,128)(2,1)} %low.8) | copy-start | bytes 884740
  0.7 2.7 %copy-start.2 = (bf16[1,384,384]{2,1,0:T(8,128)(2,1)S(1)}, bf16[1,384,384]{2,1,0:T(8,128)(2,1)}, u32[]{:S(2)}) copy-start(bf16[1,384,384]{2,1,0:T(8,128)(2,1)} %up.8) | copy-start | bytes 884740
  1.8 1.4 %collective-permute-start.1 = (bf16[768,384]{1,0:T(8,128)(2,1)S(1)}, bf16[768,384]{1,0:T(8,128)(2,1)S(1)}, u32[]{:S(2)}, u32[]{:S(2)}) collective-permute-start(bf16[768,384]{1,0:T(8,128)(2,1)S(1)} %pad_maximum_fusion.own_up.own_down), channel_id=1, source_target_pairs={{32,0},{96,64},{160,128},{224,192},{288,256},{352,320},{416,384},{... | collective-permute-start | bytes 1769480 | tf_op jit(solution)/shard_map/ppermute | solution.py:100
  2.6 0.7 collective-permute-start
  3.4 1.4 %collective-permute-start.2 = (bf16[768,384]{1,0:T(8,128)(2,1)S(1)}, bf16[768,384]{1,0:T(8,128)(2,1)S(1)}, u32[]{:S(2)}, u32[]{:S(2)}) collective-permute-start(bf16[768,384]{1,0:T(8,128)(2,1)S(1)} %get-tuple-element.10.own_up), channel_id=1, source_target_pairs={{480,496},{0,16},{32,48},{64,80},{96,112},{128,144},{160,176},{192... | collective-permute-start | bytes 1769480 | tf_op jit(solution)/shard_map/ppermute | solution.py:100
  4.2 0.7 collective-permute-start.3
  5.0 1.4 %collective-permute-start.4 = (bf16[768,384]{1,0:T(8,128)(2,1)S(1)}, bf16[768,384]{1,0:T(8,128)(2,1)S(1)}, u32[]{:S(2)}, u32[]{:S(2)}) collective-permute-start(bf16[768,384]{1,0:T(8,128)(2,1)S(1)} %get-tuple-element.12.own_up), channel_id=1, source_target_pairs={{480,488},{496,504},{0,8},{16,24},{32,40},{48,56},{64,72},{80,88},... | collective-permute-start | bytes 1769480 | tf_op jit(solution)/shard_map/ppermute | solution.py:100
  5.7 0.7 collective-permute-start.5
  6.6 49.0 %collective-permute-start.6 = (bf16[768,384]{1,0:T(8,128)(2,1)S(1)}, bf16[768,384]{1,0:T(8,128)(2,1)S(1)}, u32[]{:S(2)}, u32[]{:S(2)}) collective-permute-start(bf16[768,384]{1,0:T(8,128)(2,1)S(1)} %get-tuple-element.14.own_up), channel_id=1, source_target_pairs={{480,484},{488,492},{496,500},{504,508},{0,4},{8,12},{16,20},{24,2... | collective-permute-start | bytes 1769480 | tf_op jit(solution)/shard_map/ppermute | solution.py:100
  7.9 64.5 %copy-start.3 = (bf16[1,384,384]{2,1,0:T(8,128)(2,1)S(1)}, bf16[1,384,384]{2,1,0:T(8,128)(2,1)}, u32[]{:S(2)}) copy-start(bf16[1,384,384]{2,1,0:T(8,128)(2,1)} %inv.9) | copy-start | bytes 884740
  7.9 64.4 %copy-start.4 = (bf16[1,384,384]{2,1,0:T(8,128)(2,1)S(1)}, bf16[1,384,384]{2,1,0:T(8,128)(2,1)}, u32[]{:S(2)}) copy-start(bf16[1,384,384]{2,1,0:T(8,128)(2,1)} %low.9) | copy-start | bytes 884740
  7.9 64.4 %copy-start.5 = (bf16[1,384,384]{2,1,0:T(8,128)(2,1)S(1)}, bf16[1,384,384]{2,1,0:T(8,128)(2,1)}, u32[]{:S(2)}) copy-start(bf16[1,384,384]{2,1,0:T(8,128)(2,1)} %up.9) | copy-start | bytes 884740
  7.9 60.2 %collective-permute-start.7 = (bf16[768,384]{1,0:T(8,128)(2,1)S(1)}, bf16[768,384]{1,0:T(8,128)(2,1)S(1)}, u32[]{:S(2)}, u32[]{:S(2)}) collective-permute-start(bf16[768,384]{1,0:T(8,128)(2,1)S(1)} %get-tuple-element.15.own_down), channel_id=1, source_target_pairs={{488,484},{496,492},{504,500},{0,508},{8,4},{16,12},{24,20},{32,28... | collective-permute-start | bytes 1769480 | tf_op jit(solution)/shard_map/ppermute | solution.py:100
  69.4 2.9 %collective-permute-start.8 = (bf16[768,384]{1,0:T(8,128)(2,1)S(1)}, bf16[768,384]{1,0:T(8,128)(2,1)S(1)}, u32[]{:S(2)}, u32[]{:S(2)}) collective-permute-start(bf16[768,384]{1,0:T(8,128)(2,1)S(1)} %get-tuple-element.17), channel_id=1, source_target_pairs={{484,480},{492,488},{500,496},{508,504},{4,0},{12,8},{20,16},{28,2... | collective-permute-start | bytes 1769480 | tf_op jit(solution)/shard_map/ppermute | solution.py:100

commit v2 on v1

v2 whole, which is shorter than its diff:
```python
import functools

import jax
import jax.numpy as jnp
from jax import lax
from jax.experimental import pallas as pl
from jax.experimental.pallas import tpu as pltpu
from jax.sharding import PartitionSpec as P


BF = jnp.bfloat16
F32 = jnp.float32
NT = (((1,), (1,)), ((), ()))


def mm(left_op, right_op):
    return jnp.dot(left_op, right_op, preferred_element_type=F32)


def mt(left_op, right_op):
    return lax.dot_general(left_op, right_op, NT, preferred_element_type=F32)


def packed_parts(t):
    return (
        ((0, 0), (0, 0), 3 * t),
        ((t, 0), (t, t), 2 * t),
        ((t, 2 * t), (2 * t, 2 * t), t),
    )


def unpack(dst, src, base=0):
    t = dst.shape[0] // 3
    for (pr, pc), (fr, fc), width in packed_parts(t):
        dst[fr : fr + t, fc : fc + width] = src[base + pr : base + pr + t, pc : pc + width]
    dst[t : 2 * t, :t] = src[base : base + t, t : 2 * t].T
    dst[2 * t :, :t] = src[base : base + t, 2 * t :].T
    dst[2 * t :, t : 2 * t] = src[base + t : base + 2 * t, t : 2 * t].T


def eliminate(t, inv, low, up, diag_low, diag_up, coup, coup_holds, out_down, out_up, out_diag):
    if coup_holds:
        down = mm(low, diag_low[...]) + mt(up, coup)
        upw = mm(low, coup) + mm(up, diag_up[...])
    else:
        down = mm(low, diag_low[...]) + mm(up, coup)
        upw = mt(low, coup) + mm(up, diag_up[...])
    down = down.astype(BF)
    upw = upw.astype(BF)
    out_down(down)
    out_up(upw)
    for (pr, pc), (fr, fc), width in packed_parts(t):
        rows = slice(fr, fr + t)
        cols = slice(fc, fc + width)
        part = inv(pr, pc, fr, fc, width).astype(F32)
        part = part + mt(down[rows], low[cols]) + mt(upw[rows], up[cols])
        out_diag(pr, pc, width, part.astype(BF))


def roles(place):
    j = place[0]
    r = lax.rem(j, 16)
    return r, lax.rem(j, 2), lax.div(r, 2)


def pack_kernel(place, inv, low, up, top, coup, up_msg, down_msg, d_msg, in_msg, sems):
    n = low.shape[1]
    t = n // 3
    r, core, chip = roles(place)

    def run(copies):
        for i, (src, dst) in enumerate(copies):
            pltpu.make_async_copy(src, dst, sems.at[i]).start()
        for i, (src, dst) in enumerate(copies):
            pltpu.make_async_copy(src, dst, sems.at[i]).wait()

    def diag_copies(src, dst):
        return [
            (src.at[0, fr : fr + t, fc : fc + width], dst.at[pr : pr + t, pc : pc + width])
            for (pr, pc), (fr, fc), width in packed_parts(t)
        ]

    @pl.when(r == 0)
    def _():
        copies = [(coup.at[0], up_msg.at[2 * t :, :])]
        for dst in (up_msg, d_msg, down_msg):
            copies += diag_copies(top, dst)
        run(copies)

    @pl.when(jnp.logical_or(core == 1, lax.rem(chip, 2) == 1))
    def _():
        copies = diag_copies(inv, in_msg)
        copies.append((low.at[0], in_msg.at[2 * t : 2 * t + n, :]))
        copies.append((up.at[0], in_msg.at[2 * t + n :, :]))
        run(copies)


def level_kernel(height, place, inv, low, up, from_low, from_up, up_in, down_in, d_in,
                 up_msg, down_msg, d_msg, diag_low, diag_up):
    n = low.shape[1]
    t = n // 3
    r, _, _ = roles(place)

    def go(coup, holds):
        unpack(diag_low, from_low)
        unpack(diag_up, from_up)

        def out_down(v):
            down_msg[2 * t :, :] = v

        def out_up(v):
            up_msg[2 * t :, :] = v

        def out_diag(pr, pc, width, v):
            for dst in (up_msg, down_msg, d_msg):
                dst[pr : pr + t, pc : pc + width] = v

        eliminate(
            t, lambda pr, pc, fr, fc, w: inv[0, fr : fr + t, fc : fc + w], low[0], up[0],
            diag_low, diag_up, coup[2 * t :, :], holds, out_down, out_up, out_diag,
        )

    if height == 4:
        @pl.when(r == 8)
        def _():
            go(from_low, True)
    else:
        @pl.when(r == 4)
        def _():
            go(from_up, False)

        @pl.when(r == 12)
        def _():
            go(from_low, True)


def fine_kernel(place, own_in, near_in, first_in, up_msg, d_msg, from_up3, y_two, y_one, y_low, n_low, n_up,
                own, other, lo, hi, mid, half):
    n = up_msg.shape[1]
    t = n // 3
    _, core, chip = roles(place)

    def go(low_src, up_src, coup, holds, second, odd):
        unpack(lo, low_src)
        unpack(hi, up_src)
        mid_packed = other if not odd else own
        mid_row = 2 * t if not odd else 0

        def parts(src):
            return (
                lambda pr, pc, fr, fc, w: src[pr : pr + t, pc : pc + w],
                src[2 * t : 2 * t + n, :],
                src[2 * t + n :, :],
            )

        def keep(v):
            half[...] = v

        def drop(v):
            pass

        def out_mid(pr, pc, width, v):
            mid_packed[mid_row + pr : mid_row + pr + t, pc : pc + width] = v

        eliminate(
            t, *parts(second), lo, hi, coup[2 * t :, :], holds,
            drop if odd else keep, keep if odd else drop, out_mid,
        )
        unpack(mid, mid_packed, mid_row)

        def out_down(v):
            own[4 * t :, :] = v

        def out_up(v):
            other[4 * t :, :] = v

        def out_diag(pr, pc, width, v):
            own[2 * t + pr : 3 * t + pr, pc : pc + width] = v
            other[pr : pr + t, pc : pc + width] = v

        eliminate(
            t, *parts(first_in), mid if odd else lo, hi if odd else mid, half[...], odd,
            out_down, out_up, out_diag,
        )
        if odd:
            other[2 * t : 4 * t, :] = up_src[: 2 * t, :]
        else:
            own[: 2 * t, :] = low_src[: 2 * t, :]

    phase = jnp.where(core == 0, lax.rem(chip, 4), 4)

    @pl.when(phase == 0)
    def _():
        go(d_msg, y_two, y_two, False, near_in, False)

    @pl.when(phase == 1)
    def _():
        go(n_low, y_one, y_one, False, own_in, True)

    @pl.when(phase == 2)
    def _():
        go(up_msg, from_up3, up_msg, True, near_in, False)

    @pl.when(phase == 3)
    def _():
        go(y_low, n_up, y_low, True, own_in, True)


def interior_kernel(place, inv, low, up, own, other, out_diag, out_below, here, above):
    n = low.shape[1]
    t = n // 3
    _, core, _ = roles(place)

    def go(src, holds):
        unpack(here, src)
        unpack(above, src, 2 * t)
        coup = src[4 * t :, :]
        out_diag[0] = here[...]
        if holds:
            p = mm(low[0], here[...]) + mt(up[0], coup)
            q = mm(low[0], coup) + mm(up[0], above[...])
        else:
            p = mm(low[0], here[...]) + mm(up[0], coup)
            q = mt(low[0], coup) + mm(up[0], above[...])
        p = p.astype(BF)
        q = q.astype(BF)
        out_below[0] = p
        out_below[1] = q.T
        out_diag[1] = (inv[0].astype(F32) + mt(p, low[0]) + mt(q, up[0])).astype(BF)

    @pl.when(core == 0)
    def _():
        go(own, False)

    @pl.when(core == 1)
    def _():
        go(other, True)


def on_device(
    separator_inverse,
    separator_lower,
    separator_upper,
    top_diagonal,
    top_coupling,
    interior_inverse,
    interior_lower,
    interior_upper,
):
    devices = lax.axis_size("tm")
    spacing = 16
    margin = spacing // 2
    n = separator_lower.shape[1]
    t = n // 3
    place = lax.rem(lax.axis_index("tm") + margin, devices).astype(jnp.int32).reshape(1)

    def moved(value, select, step):
        pairs = [
            ((p - margin) % devices, (p + step - margin) % devices)
            for p in range(devices)
            if select(p % spacing)
        ]
        return lax.ppermute(value, "tm", pairs)

    smem = pl.BlockSpec(memory_space=pltpu.SMEM)
    vmem = pl.BlockSpec(memory_space=pltpu.VMEM)
    anywhere = pl.BlockSpec(memory_space=pl.ANY)
    params = pltpu.CompilerParams(vmem_limit_bytes=16 << 20)
    block = pltpu.VMEM((n, n), BF)
    message = pltpu.VMEM((2 * t + n, n), BF)
    diagonal = pltpu.VMEM((2 * t, n), BF)
    inputs = pltpu.VMEM((2 * t + 2 * n, n), BF)
    both = pltpu.VMEM((4 * t + n, n), BF)

    def near(*values):
        return [pltpu.with_memory_space_constraint(v, pltpu.VMEM) for v in values]

    up_msg, down_msg, d_msg, in_msg = pl.pallas_call(
        pack_kernel,
        out_shape=(message, message, diagonal, inputs),
        in_specs=[smem] + [anywhere] * 5,
        out_specs=(vmem,) * 4,
        scratch_shapes=[pltpu.SemaphoreType.DMA((10,))],
        compiler_params=params,
        name="pack",
    )(
        place,
        *[
            pltpu.with_memory_space_constraint(v, pltpu.HBM)
            for v in (separator_inverse, separator_lower, separator_upper, top_diagonal, top_coupling)
        ],
    )

    def level(height, from_low, from_up, up_msg, down_msg, d_msg):
        return pl.pallas_call(
            functools.partial(level_kernel, height),
            out_shape=(message, message, diagonal),
            in_specs=[smem] + [vmem] * 8,
            out_specs=(vmem,) * 3,
            scratch_shapes=[block, block],
            input_output_aliases={6: 0, 7: 1, 8: 2},
            compiler_params=params,
        )(
            place,
            separator_inverse,
            separator_lower,
            separator_upper,
            *near(from_low, from_up, up_msg, down_msg, d_msg),
        )

    from_low = moved(up_msg, lambda r: r == 0, 8)
    from_up = moved(d_msg, lambda r: r == 0, -8)
    near_in = moved(in_msg, lambda r: r % 4 == 2, -2)
    first_in = moved(in_msg, lambda r: r % 2 == 1, -1)
    up_msg, down_msg, d_msg = level(4, from_low, from_up, up_msg, down_msg, d_msg)
    from_low = moved(up_msg, lambda r: r % 8 == 0, 4)
    from_up = moved(down_msg, lambda r: r % 8 == 0, -4)
    up_msg, down_msg, d_msg = level(3, from_low, from_up, up_msg, down_msg, d_msg)
    y_two = moved(down_msg, lambda r: r % 8 == 4, -4)
    y_one = moved(down_msg, lambda r: r % 8 == 4, -2)
    y_low = moved(up_msg, lambda r: r % 8 == 4, 2)
    n_low = moved(d_msg, lambda r: r % 8 == 0, 2)
    n_up = moved(d_msg, lambda r: r % 8 == 0, -2)
    own, other = pl.pallas_call(
        fine_kernel,
        out_shape=(both, both),
        in_specs=[smem] + [vmem] * 11,
        out_specs=(vmem,) * 2,
        scratch_shapes=[block] * 4,
        compiler_params=params,
        name="fine",
    )(place, *near(in_msg, near_in, first_in, up_msg, d_msg, from_up, y_two, y_one, y_low, n_low, n_up))
    other = moved(other, lambda r: r % 2 == 0, 1)
    pair = jax.ShapeDtypeStruct((2, n, n), BF)
    return pl.pallas_call(
        interior_kernel,
        out_shape=(pair, pair),
        in_specs=[smem] + [vmem] * 5,
        out_specs=(vmem,) * 2,
        scratch_shapes=[block] * 2,
        compiler_params=params,
        name="interior",
    )(place, interior_inverse, interior_lower, interior_upper, *near(own, other))


def solution(mesh):
    spec = P(("rep", "tm"), None, None)

    return jax.shard_map(
        on_device, mesh=mesh, in_specs=(spec,) * 8, out_specs=(spec, spec), check_vma=False
    )
```

time: 74.9 us -> 61.3 us (0.82)
  waiting for transfers between devices: 60.4 us -> 38.8 us
  starting transfers between devices: 8.23 us -> 17.2 us
  other arithmetic: 1.19 us -> 0 us
    ppermute x9 -> x12, waiting for transfers between devices: 60.4 us -> 38.8 us  [moved(): return lax.ppermute(value, 'tm', pairs)]
    ppermute x9 -> x12, starting transfers between devices: 8.23 us -> 17.2 us  [moved(): return lax.ppermute(value, 'tm', pairs)]
    concatenate x1 -> x0, other arithmetic: 1.19 us -> none  [on_device(): own_up = jnp.concatenate([top_diagonal[0], top_coupling[0]], axis=0)]
  transfers between devices with their start and end apart: 9 -> 12, of which waited for: 3 -> 1; matrix products, arithmetic and copies ran while one was open for 0% -> 0% of each run, Pallas kernels for 0% -> 0%
where the time goes in v2:
time: 61.3 us; the launch traced here: 60.9 us
  waiting for transfers between devices  38.8 us (63%)
  starting transfers between devices  17.2 us (28%)
  Pallas kernels  3.91 us (6%)
  between operations  0.93 us (2%)
    ppermute x12, waiting for transfers between devices, moved(): return lax.ppermute(value, 'tm', pairs)  38.8 us
    ppermute x12, starting transfers between devices, moved(): return lax.ppermute(value, 'tm', pairs)  17.2 us
    pallas_call x1, Pallas kernels, on_device(): pl.pallas_call(interior_kernel, out_shape=(pair, pair), in_specs=[smem] +...  2.33 us
    pallas_call x1, Pallas kernels, on_device(): pl.pallas_call(pack_kernel, out_shape=(message, message, diagonal, inputs...  1.33 us
  transfers between devices with their start and end apart: 12, of which 1 were waited for; matrix products, arithmetic and copies ran while one was open for 0% of the time, Pallas kernels for 0%

profile of v2, /device:TPU:1, one launch (start us, length us, event | category | flops | bytes accessed | tf_op | source)
XLA Modules:
  0.0 60.9 jit_solution(14106376863805819369)
XLA Ops:
  0.7 1.3 %pack.1 = (bf16[640,384]{1,0:T(8,128)(2,1)S(1)}, bf16[640,384]{1,0:T(8,128)(2,1)S(1)}, bf16[256,384]{1,0:T(8,128)(2,1)S(1)}, bf16[1024,384]{1,0:T(8,128)(2,1)S(1)}) custom-call(s32[1]{0:T(128)} %bitcast.place, bf16[1,384,384]{2,1,0:T(8,128)(2,1)} %inv.6, bf16[1,384,384]{2,1,0:T(8,128)(2,1)} %low.6, bf16[1,384,384]{2,1,0:T(8,128)(2,1)} %up.6, ...), custom_call_target="tpu_custom_call" | custom-call | tf_op jit(solution)/shard_map/pack/pallas_call | solution.py:278
  2.0 0.7 %collective-permute-start.2 = (bf16[640,384]{1,0:T(8,128)(2,1)S(1)}, bf16[640,384]{1,0:T(8,128)(2,1)S(1)}, u32[]{:S(2)}, u32[]{:S(2)}) collective-permute-start(bf16[640,384]{1,0:T(8,128)(2,1)S(1)} %get-tuple-element.15.up_in), channel_id=1, source_target_pairs={{480,0},{32,64},{96,128},{160,192},{224,256},{288,320},{352,384},{... | collective-permute-start | bytes 1474568 | tf_op jit(solution)/shard_map/ppermute | solution.py:263
  2.7 0.7 %collective-permute-start.3 = (bf16[256,384]{1,0:T(8,128)(2,1)S(1)}, bf16[256,384]{1,0:T(8,128)(2,1)S(1)}, u32[]{:S(2)}, u32[]{:S(2)}) collective-permute-start(bf16[256,384]{1,0:T(8,128)(2,1)S(1)} %get-tuple-element.16.d_in), channel_id=1, source_target_pairs={{480,448},{32,0},{96,64},{160,128},{224,192},{288,256},{352,320},{... | collective-permute-start | bytes 589832 | tf_op jit(solution)/shard_map/ppermute | solution.py:263
  3.4 8.9 %collective-permute-start.1 = (bf16[1024,384]{1,0:T(8,128)(2,1)S(1)}, bf16[1024,384]{1,0:T(8,128)(2,1)S(1)}, u32[]{:S(2)}, u32[]{:S(2)}) collective-permute-start(bf16[1024,384]{1,0:T(8,128)(2,1)S(1)} %get-tuple-element.14.own_in), channel_id=1, source_target_pairs={{484,480},{492,488},{500,496},{508,504},{4,0},{12,8},{20,16},{28,2... | collective-permute-start | bytes 2359304 | tf_op jit(solution)/shard_map/ppermute | solution.py:263
  12.3 0.0 collective-permute-done.3.from_up
  12.4 0.7 %collective-permute-start.4 = (bf16[640,384]{1,0:T(8,128)(2,1)S(1)}, bf16[640,384]{1,0:T(8,128)(2,1)S(1)}, u32[]{:S(2)}, u32[]{:S(2)}) collective-permute-start(bf16[640,384]{1,0:T(8,128)(2,1)S(1)} %get-tuple-element.18.up_in), channel_id=1, source_target_pairs={{480,496},{0,16},{32,48},{64,80},{96,112},{128,144},{160,176},{192... | collective-permute-start | bytes 1474568 | tf_op jit(solution)/shard_map/ppermute | solution.py:263
  13.1 0.7 %collective-permute-start.5 = (bf16[640,384]{1,0:T(8,128)(2,1)S(1)}, bf16[640,384]{1,0:T(8,128)(2,1)S(1)}, u32[]{:S(2)}, u32[]{:S(2)}) collective-permute-start(bf16[640,384]{1,0:T(8,128)(2,1)S(1)} %get-tuple-element.19.down_in), channel_id=1, source_target_pairs={{480,464},{0,496},{32,16},{64,48},{96,80},{128,112},{160,144},{192... | collective-permute-start | bytes 1474568 | tf_op jit(solution)/shard_map/ppermute | solution.py:263
  13.8 0.7 %collective-permute-start = (bf16[1024,384]{1,0:T(8,128)(2,1)S(1)}, bf16[1024,384]{1,0:T(8,128)(2,1)S(1)}, u32[]{:S(2)}, u32[]{:S(2)}) collective-permute-start(bf16[1024,384]{1,0:T(8,128)(2,1)S(1)} %get-tuple-element.14.own_in), channel_id=1, source_target_pairs={{488,480},{504,496},{8,0},{24,16},{40,32},{56,48},{72,64},{88,80},... | collective-permute-start | bytes 2359304 | tf_op jit(solution)/shard_map/ppermute | solution.py:263
  14.5 0.0 collective-permute-done.5.from_up.from_up3
  14.6 0.7 %collective-permute-start.8 = (bf16[640,384]{1,0:T(8,128)(2,1)S(1)}, bf16[640,384]{1,0:T(8,128)(2,1)S(1)}, u32[]{:S(2)}, u32[]{:S(2)}) collective-permute-start(bf16[640,384]{1,0:T(8,128)(2,1)S(1)} %get-tuple-element.21.up_msg), channel_id=1, source_target_pairs={{496,504},{16,24},{48,56},{80,88},{112,120},{144,152},{176,184},{2... | collective-permute-start | bytes 1474568 | tf_op jit(solution)/shard_map/ppermute | solution.py:263
  15.3 0.7 %collective-permute-start.7 = (bf16[640,384]{1,0:T(8,128)(2,1)S(1)}, bf16[640,384]{1,0:T(8,128)(2,1)S(1)}, u32[]{:S(2)}, u32[]{:S(2)}) collective-permute-start(bf16[640,384]{1,0:T(8,128)(2,1)S(1)} %get-tuple-element.23), channel_id=1, source_target_pairs={{496,488},{16,8},{48,40},{80,72},{112,104},{144,136},{176,168},{20... | collective-permute-start | bytes 1474568 | tf_op jit(solution)/shard_map/ppermute | solution.py:263
  16.0 0.7 %collective-permute-start.6 = (bf16[640,384]{1,0:T(8,128)(2,1)S(1)}, bf16[640,384]{1,0:T(8,128)(2,1)S(1)}, u32[]{:S(2)}, u32[]{:S(2)}) collective-permute-start(bf16[640,384]{1,0:T(8,128)(2,1)S(1)} %get-tuple-element.23), channel_id=1, source_target_pairs={{496,480},{16,0},{48,32},{80,64},{112,96},{144,128},{176,160},{208... | collective-permute-start | bytes 1474568 | tf_op jit(solution)/shard_map/ppermute | solution.py:263
  16.7 0.0 collective-permute-done.1.first_in
  16.7 0.0 copy-start.3
  16.7 0.0 copy-start.4
  16.7 0.0 copy-start.5
  16.7 0.8 %collective-permute-start.10 = (bf16[256,384]{1,0:T(8,128)(2,1)S(1)}, bf16[256,384]{1,0:T(8,128)(2,1)S(1)}, u32[]{:S(2)}, u32[]{:S(2)}) collective-permute-start(bf16[256,384]{1,0:T(8,128)(2,1)S(1)} %get-tuple-element.22.d_msg), channel_id=1, source_target_pairs={{480,472},{0,504},{32,24},{64,56},{96,88},{128,120},{160,152},{192... | collective-permute-start | bytes 589832 | tf_op jit(solution)/shard_map/ppermute | solution.py:263
  17.5 0.0 collective-permute-done.near_in
  17.5 0.7 %collective-permute-start.9 = (bf16[256,384]{1,0:T(8,128)(2,1)S(1)}, bf16[256,384]{1,0:T(8,128)(2,1)S(1)}, u32[]{:S(2)}, u32[]{:S(2)}) collective-permute-start(bf16[256,384]{1,0:T(8,128)(2,1)S(1)} %get-tuple-element.22.d_msg), channel_id=1, source_target_pairs={{480,488},{0,8},{32,40},{64,72},{96,104},{128,136},{160,168},{192,... | collective-permute-start | bytes 589832 | tf_op jit(solution)/shard_map/ppermute | solution.py:263
  18.2 0.0 collective-permute-done.10.n_up
  18.3 0.2 fine.1
  18.5 1.3 %collective-permute-start.11 = (bf16[896,384]{1,0:T(8,128)(2,1)S(1)}, bf16[896,384]{1,0:T(8,128)(2,1)S(1)}, u32[]{:S(2)}, u32[]{:S(2)}) collective-permute-start(bf16[896,384]{1,0:T(8,128)(2,1)S(1)} %get-tuple-element.25), channel_id=1, source_target_pairs={{480,484},{488,492},{496,500},{504,508},{0,4},{8,12},{16,20},{24,2... | collective-permute-start | bytes 2064392 | tf_op jit(solution)/shard_map/ppermute | solution.py:263
  19.8 38.8 %collective-permute-done.11.other = bf16[896,384]{1,0:T(8,128)(2,1)S(1)} collective-permute-done((bf16[896,384]{1,0:T(8,128)(2,1)S(1)}, bf16[896,384]{1,0:T(8,128)(2,1)S(1)}, u32[]{:S(2)}, u32[]{:S(2)}) %collective-permute-start.11) | collective-permute-done | bytes 688160 | tf_op jit(solution)/shard_map/ppermute | solution.py:263
  58.6 2.3 %interior.1 = (bf16[2,384,384]{2,1,0:T(8,128)(2,1)}, bf16[2,384,384]{2,1,0:T(8,128)(2,1)}) custom-call(s32[1]{0:T(128)} %bitcast.place, bf16[1,384,384]{2,1,0:T(8,128)(2,1)S(1)} %copy-done.3, bf16[1,384,384]{2,1,0:T(8,128)(2,1)S(1)} %copy-done.4, bf16[1,384,384]{2,1,0:T(8,128)(2,1)S(1)} %copy-done.5, bf16[896,384]{1,0:T(8,128)(2,1)S(1)} %get-tuple-element.24.own, ...), custom_call_target="tpu_custom_call" | custom-call | tf_op jit(solution)/shard_map/interior/pallas_call | solution.py:335
  (17 shorter events, 0.1 us)
Async XLA Ops:
  0.6 11.7 %copy-start = (bf16[1,384,384]{2,1,0:T(8,128)(2,1)S(1)}, bf16[1,384,384]{2,1,0:T(8,128)(2,1)}, u32[]{:S(2)}) copy-start(bf16[1,384,384]{2,1,0:T(8,128)(2,1)} %inv.6) | copy-start | bytes 884740
  0.6 11.7 %copy-start.1 = (bf16[1,384,384]{2,1,0:T(8,128)(2,1)S(1)}, bf16[1,384,384]{2,1,0:T(8,128)(2,1)}, u32[]{:S(2)}) copy-start(bf16[1,384,384]{2,1,0:T(8,128)(2,1)} %low.6) | copy-start | bytes 884740
  0.7 11.7 %copy-start.2 = (bf16[1,384,384]{2,1,0:T(8,128)(2,1)S(1)}, bf16[1,384,384]{2,1,0:T(8,128)(2,1)}, u32[]{:S(2)}) copy-start(bf16[1,384,384]{2,1,0:T(8,128)(2,1)} %up.6) | copy-start | bytes 884740
  2.0 10.3 %collective-permute-start.2 = (bf16[640,384]{1,0:T(8,128)(2,1)S(1)}, bf16[640,384]{1,0:T(8,128)(2,1)S(1)}, u32[]{:S(2)}, u32[]{:S(2)}) collective-permute-start(bf16[640,384]{1,0:T(8,128)(2,1)S(1)} %get-tuple-element.15.up_in), channel_id=1, source_target_pairs={{480,0},{32,64},{96,128},{160,192},{224,256},{288,320},{352,384},{... | collective-permute-start | bytes 1474568 | tf_op jit(solution)/shard_map/ppermute | solution.py:263
  2.7 9.6 %collective-permute-start.3 = (bf16[256,384]{1,0:T(8,128)(2,1)S(1)}, bf16[256,384]{1,0:T(8,128)(2,1)S(1)}, u32[]{:S(2)}, u32[]{:S(2)}) collective-permute-start(bf16[256,384]{1,0:T(8,128)(2,1)S(1)} %get-tuple-element.16.d_in), channel_id=1, source_target_pairs={{480,448},{32,0},{96,64},{160,128},{224,192},{288,256},{352,320},{... | collective-permute-start | bytes 589832 | tf_op jit(solution)/shard_map/ppermute | solution.py:263
  3.4 13.3 %collective-permute-start.1 = (bf16[1024,384]{1,0:T(8,128)(2,1)S(1)}, bf16[1024,384]{1,0:T(8,128)(2,1)S(1)}, u32[]{:S(2)}, u32[]{:S(2)}) collective-permute-start(bf16[1024,384]{1,0:T(8,128)(2,1)S(1)} %get-tuple-element.14.own_in), channel_id=1, source_target_pairs={{484,480},{492,488},{500,496},{508,504},{4,0},{12,8},{20,16},{28,2... | collective-permute-start | bytes 2359304 | tf_op jit(solution)/shard_map/ppermute | solution.py:263
  12.4 2.1 %collective-permute-start.4 = (bf16[640,384]{1,0:T(8,128)(2,1)S(1)}, bf16[640,384]{1,0:T(8,128)(2,1)S(1)}, u32[]{:S(2)}, u32[]{:S(2)}) collective-permute-start(bf16[640,384]{1,0:T(8,128)(2,1)S(1)} %get-tuple-element.18.up_in), channel_id=1, source_target_pairs={{480,496},{0,16},{32,48},{64,80},{96,112},{128,144},{160,176},{192... | collective-permute-start | bytes 1474568 | tf_op jit(solution)/shard_map/ppermute | solution.py:263
  13.1 1.4 %collective-permute-start.5 = (bf16[640,384]{1,0:T(8,128)(2,1)S(1)}, bf16[640,384]{1,0:T(8,128)(2,1)S(1)}, u32[]{:S(2)}, u32[]{:S(2)}) collective-permute-start(bf16[640,384]{1,0:T(8,128)(2,1)S(1)} %get-tuple-element.19.down_in), channel_id=1, source_target_pairs={{480,464},{0,496},{32,16},{64,48},{96,80},{128,112},{160,144},{192... | collective-permute-start | bytes 1474568 | tf_op jit(solution)/shard_map/ppermute | solution.py:263
  13.8 3.7 %collective-permute-start = (bf16[1024,384]{1,0:T(8,128)(2,1)S(1)}, bf16[1024,384]{1,0:T(8,128)(2,1)S(1)}, u32[]{:S(2)}, u32[]{:S(2)}) collective-permute-start(bf16[1024,384]{1,0:T(8,128)(2,1)S(1)} %get-tuple-element.14.own_in), channel_id=1, source_target_pairs={{488,480},{504,496},{8,0},{24,16},{40,32},{56,48},{72,64},{88,80},... | collective-permute-start | bytes 2359304 | tf_op jit(solution)/shard_map/ppermute | solution.py:263
  14.6 3.7 %collective-permute-start.8 = (bf16[640,384]{1,0:T(8,128)(2,1)S(1)}, bf16[640,384]{1,0:T(8,128)(2,1)S(1)}, u32[]{:S(2)}, u32[]{:S(2)}) collective-permute-start(bf16[640,384]{1,0:T(8,128)(2,1)S(1)} %get-tuple-element.21.up_msg), channel_id=1, source_target_pairs={{496,504},{16,24},{48,56},{80,88},{112,120},{144,152},{176,184},{2... | collective-permute-start | bytes 1474568 | tf_op jit(solution)/shard_map/ppermute | solution.py:263
  15.3 3.0 %collective-permute-start.7 = (bf16[640,384]{1,0:T(8,128)(2,1)S(1)}, bf16[640,384]{1,0:T(8,128)(2,1)S(1)}, u32[]{:S(2)}, u32[]{:S(2)}) collective-permute-start(bf16[640,384]{1,0:T(8,128)(2,1)S(1)} %get-tuple-element.23), channel_id=1, source_target_pairs={{496,488},{16,8},{48,40},{80,72},{112,104},{144,136},{176,168},{20... | collective-permute-start | bytes 1474568 | tf_op jit(solution)/shard_map/ppermute | solution.py:263
  16.0 2.3 %collective-permute-start.6 = (bf16[640,384]{1,0:T(8,128)(2,1)S(1)}, bf16[640,384]{1,0:T(8,128)(2,1)S(1)}, u32[]{:S(2)}, u32[]{:S(2)}) collective-permute-start(bf16[640,384]{1,0:T(8,128)(2,1)S(1)} %get-tuple-element.23), channel_id=1, source_target_pairs={{496,480},{16,0},{48,32},{80,64},{112,96},{144,128},{176,160},{208... | collective-permute-start | bytes 1474568 | tf_op jit(solution)/shard_map/ppermute | solution.py:263
  16.7 41.9 %copy-start.3 = (bf16[1,384,384]{2,1,0:T(8,128)(2,1)S(1)}, bf16[1,384,384]{2,1,0:T(8,128)(2,1)}, u32[]{:S(2)}) copy-start(bf16[1,384,384]{2,1,0:T(8,128)(2,1)} %inv.7) | copy-start | bytes 884740
  16.7 41.9 %copy-start.4 = (bf16[1,384,384]{2,1,0:T(8,128)(2,1)S(1)}, bf16[1,384,384]{2,1,0:T(8,128)(2,1)}, u32[]{:S(2)}) copy-start(bf16[1,384,384]{2,1,0:T(8,128)(2,1)} %low.7) | copy-start | bytes 884740
  16.7 41.9 %copy-start.5 = (bf16[1,384,384]{2,1,0:T(8,128)(2,1)S(1)}, bf16[1,384,384]{2,1,0:T(8,128)(2,1)}, u32[]{:S(2)}) copy-start(bf16[1,384,384]{2,1,0:T(8,128)(2,1)} %up.7) | copy-start | bytes 884740
  16.7 1.5 %collective-permute-start.10 = (bf16[256,384]{1,0:T(8,128)(2,1)S(1)}, bf16[256,384]{1,0:T(8,128)(2,1)S(1)}, u32[]{:S(2)}, u32[]{:S(2)}) collective-permute-start(bf16[256,384]{1,0:T(8,128)(2,1)S(1)} %get-tuple-element.22.d_msg), channel_id=1, source_target_pairs={{480,472},{0,504},{32,24},{64,56},{96,88},{128,120},{160,152},{192... | collective-permute-start | bytes 589832 | tf_op jit(solution)/shard_map/ppermute | solution.py:263
  17.5 0.7 %collective-permute-start.9 = (bf16[256,384]{1,0:T(8,128)(2,1)S(1)}, bf16[256,384]{1,0:T(8,128)(2,1)S(1)}, u32[]{:S(2)}, u32[]{:S(2)}) collective-permute-start(bf16[256,384]{1,0:T(8,128)(2,1)S(1)} %get-tuple-element.22.d_msg), channel_id=1, source_target_pairs={{480,488},{0,8},{32,40},{64,72},{96,104},{128,136},{160,168},{192,... | collective-permute-start | bytes 589832 | tf_op jit(solution)/shard_map/ppermute | solution.py:263
  18.5 40.1 %collective-permute-start.11 = (bf16[896,384]{1,0:T(8,128)(2,1)S(1)}, bf16[896,384]{1,0:T(8,128)(2,1)S(1)}, u32[]{:S(2)}, u32[]{:S(2)}) collective-permute-start(bf16[896,384]{1,0:T(8,128)(2,1)S(1)} %get-tuple-element.25), channel_id=1, source_target_pairs={{480,484},{488,492},{496,500},{504,508},{0,4},{8,12},{16,20},{24,2... | collective-permute-start | bytes 2064392 | tf_op jit(solution)/shard_map/ppermute | solution.py:263

commit v3 on v2

--- a/solution.py
+++ b/solution.py
@@ -1,5 +1,3 @@
-import functools
-
 import jax
 import jax.numpy as jnp
 from jax import lax
@@ -63,7 +61,7 @@
     return r, lax.rem(j, 2), lax.div(r, 2)
 
 
-def pack_kernel(place, inv, low, up, top, coup, up_msg, down_msg, d_msg, in_msg, sems):
+def pack_kernel(place, inv, low, up, top, coup, up_msg, d_msg, in_msg, sems):
     n = low.shape[1]
     t = n // 3
     r, core, chip = roles(place)
@@ -83,11 +81,11 @@
     @pl.when(r == 0)
     def _():
         copies = [(coup.at[0], up_msg.at[2 * t :, :])]
-        for dst in (up_msg, d_msg, down_msg):
+        for dst in (up_msg, d_msg):
             copies += diag_copies(top, dst)
         run(copies)
 
-    @pl.when(jnp.logical_or(core == 1, lax.rem(chip, 2) == 1))
+    @pl.when(jnp.logical_or(jnp.logical_or(core == 1, lax.rem(chip, 2) == 1), r == 8))
     def _():
         copies = diag_copies(inv, in_msg)
         copies.append((low.at[0], in_msg.at[2 * t : 2 * t + n, :]))
@@ -95,15 +93,42 @@
         run(copies)
 
 
-def level_kernel(height, place, inv, low, up, from_low, from_up, up_in, down_in, d_in,
-                 up_msg, down_msg, d_msg, diag_low, diag_up):
+def source_parts(t, n, src):
+    return (
+        lambda pr, pc, fr, fc, w: src[pr : pr + t, pc : pc + w],
+        src[2 * t : 2 * t + n, :],
+        src[2 * t + n :, :],
+    )
+
+
+def block_parts(t, inv, low, up):
+    return (lambda pr, pc, fr, fc, w: inv[0, fr : fr + t, fc : fc + w], low[0], up[0])
+
+
+def coarse_kernel(place, inv, low, up, early_r, late_r, early_l, late_l, early_in, late_in,
+                  up_msg, down_msg, far, lo, hi, mid, half):
     n = low.shape[1]
     t = n // 3
-    r, _, _ = roles(place)
-
-    def go(coup, holds):
-        unpack(diag_low, from_low)
-        unpack(diag_up, from_up)
+
+    def go(low_src, up_src, upper_in, upper_half):
+        unpack(lo, low_src)
+        unpack(hi, up_src)
+        mid_packed = far if not upper_half else down_msg
+
+        def keep(v):
+            half[...] = v
+
+        def drop(v):
+            pass
+
+        def out_mid(pr, pc, width, v):
+            mid_packed[pr : pr + t, pc : pc + width] = v
+
+        eliminate(
+            t, *source_parts(t, n, upper_in), lo, hi, low_src[2 * t :, :], True,
+            drop if upper_half else keep, keep if upper_half else drop, out_mid,
+        )
+        unpack(mid, mid_packed)
 
         def out_down(v):
             down_msg[2 * t :, :] = v
@@ -112,33 +137,61 @@
             up_msg[2 * t :, :] = v
 
         def out_diag(pr, pc, width, v):
-            for dst in (up_msg, down_msg, d_msg):
-                dst[pr : pr + t, pc : pc + width] = v
+            up_msg[pr : pr + t, pc : pc + width] = v
+            down_msg[pr : pr + t, pc : pc + width] = v
 
         eliminate(
-            t, lambda pr, pc, fr, fc, w: inv[0, fr : fr + t, fc : fc + w], low[0], up[0],
-            diag_low, diag_up, coup[2 * t :, :], holds, out_down, out_up, out_diag,
+            t, *block_parts(t, inv, low, up), mid if upper_half else lo, hi if upper_half else mid,
+            half[...], upper_half, out_down, out_up, out_diag,
         )
-
-    if height == 4:
-        @pl.when(r == 8)
-        def _():
-            go(from_low, True)
-    else:
-        @pl.when(r == 4)
-        def _():
-            go(from_up, False)
-
-        @pl.when(r == 12)
-        def _():
-            go(from_low, True)
-
-
-def fine_kernel(place, own_in, near_in, first_in, up_msg, d_msg, from_up3, y_two, y_one, y_low, n_low, n_up,
+        if upper_half:
+            far[...] = up_src[...]
+
+    row = lax.rem(place[0], 32)
+
+    @pl.when(row == 20)
+    def _():
+        go(early_r, early_l, early_in, False)
+
+    @pl.when(row == 4)
+    def _():
+        go(late_r, late_l, late_in, False)
+
+    @pl.when(row == 12)
+    def _():
+        go(early_r, early_l, early_in, True)
+
+    @pl.when(row == 28)
+    def _():
+        go(late_r, late_l, late_in, True)
+
+
+def middle_kernel(place, inv, low, up, four_r, four_l, d_in, d_msg, lo, hi):
+    n = low.shape[1]
+    t = n // 3
+    r, _, _ = roles(place)
+
+    @pl.when(r == 8)
+    def _():
+        unpack(lo, four_r)
+        unpack(hi, four_l)
+
+        def drop(v):
+            pass
+
+        def out_diag(pr, pc, width, v):
+            d_msg[pr : pr + t, pc : pc + width] = v
+
+        eliminate(
+            t, *block_parts(t, inv, low, up), lo, hi, four_r[2 * t :, :], True, drop, drop, out_diag
+        )
+
+
+def fine_kernel(place, own_in, near_a, near_b, first_in, up_msg, d_msg, far, y_two, y_one, y_low, n_low, n_up,
                 own, other, lo, hi, mid, half):
     n = up_msg.shape[1]
     t = n // 3
-    _, core, chip = roles(place)
+    r, core, chip = roles(place)
 
     def go(low_src, up_src, coup, holds, second, odd):
         unpack(lo, low_src)
@@ -146,13 +199,6 @@
         mid_packed = other if not odd else own
         mid_row = 2 * t if not odd else 0
 
-        def parts(src):
-            return (
-                lambda pr, pc, fr, fc, w: src[pr : pr + t, pc : pc + w],
-                src[2 * t : 2 * t + n, :],
-                src[2 * t + n :, :],
-            )
-
         def keep(v):
             half[...] = v
 
@@ -163,7 +209,7 @@
             mid_packed[mid_row + pr : mid_row + pr + t, pc : pc + width] = v
 
         eliminate(
-            t, *parts(second), lo, hi, coup[2 * t :, :], holds,
+            t, *source_parts(t, n, second), lo, hi, coup[2 * t :, :], holds,
             drop if odd else keep, keep if odd else drop, out_mid,
         )
         unpack(mid, mid_packed, mid_row)
@@ -179,7 +225,7 @@
             other[pr : pr + t, pc : pc + width] = v
 
         eliminate(
-            t, *parts(first_in), mid if odd else lo, hi if odd else mid, half[...], odd,
+            t, *source_parts(t, n, first_in), mid if odd else lo, hi if odd else mid, half[...], odd,
             out_down, out_up, out_diag,
         )
         if odd:
@@ -191,15 +237,19 @@
 
     @pl.when(phase == 0)
     def _():
-        go(d_msg, y_two, y_two, False, near_in, False)
+        go(d_msg, y_two, y_two, False, near_a, False)
 
     @pl.when(phase == 1)
     def _():
         go(n_low, y_one, y_one, False, own_in, True)
 
-    @pl.when(phase == 2)
-    def _():
-        go(up_msg, from_up3, up_msg, True, near_in, False)
+    @pl.when(jnp.logical_and(phase == 2, r == 4))
+    def _():
+        go(up_msg, far, up_msg, True, near_b, False)
+
+    @pl.when(jnp.logical_and(phase == 2, r == 12))
+    def _():
+        go(up_msg, far, up_msg, True, near_a, False)
 
     @pl.when(phase == 3)
     def _():
@@ -254,11 +304,12 @@
     t = n // 3
     place = lax.rem(lax.axis_index("tm") + margin, devices).astype(jnp.int32).reshape(1)
 
-    def moved(value, select, step):
+    def moved(value, *moves):
         pairs = [
             ((p - margin) % devices, (p + step - margin) % devices)
             for p in range(devices)
-            if select(p % spacing)
+            for mod, at, step in moves
+            if p % mod == at
         ]
         return lax.ppermute(value, "tm", pairs)
 
@@ -275,12 +326,12 @@
     def near(*values):
         return [pltpu.with_memory_space_constraint(v, pltpu.VMEM) for v in values]
 
-    up_msg, down_msg, d_msg, in_msg = pl.pallas_call(
+    up_msg, d_msg, in_msg = pl.pallas_call(
         pack_kernel,
-        out_shape=(message, message, diagonal, inputs),
+        out_shape=(message, diagonal, inputs),
         in_specs=[smem] + [anywhere] * 5,
-        out_specs=(vmem,) * 4,
-        scratch_shapes=[pltpu.SemaphoreType.DMA((10,))],
+        out_specs=(vmem,) * 3,
+        scratch_shapes=[pltpu.SemaphoreType.DMA((7,))],
         compiler_params=params,
         name="pack",
     )(
@@ -290,47 +341,52 @@
             for v in (separator_inverse, separator_lower, separator_upper, top_diagonal, top_coupling)
         ],
     )
-
-    def level(height, from_low, from_up, up_msg, down_msg, d_msg):
-        return pl.pallas_call(
-            functools.partial(level_kernel, height),
-            out_shape=(message, message, diagonal),
-            in_specs=[smem] + [vmem] * 8,
-            out_specs=(vmem,) * 3,
-            scratch_shapes=[block, block],
-            input_output_aliases={6: 0, 7: 1, 8: 2},
-            compiler_params=params,
-        )(
-            place,
-            separator_inverse,
-            separator_lower,
-            separator_upper,
-            *near(from_low, from_up, up_msg, down_msg, d_msg),
-        )
-
-    from_low = moved(up_msg, lambda r: r == 0, 8)
-    from_up = moved(d_msg, lambda r: r == 0, -8)
-    near_in = moved(in_msg, lambda r: r % 4 == 2, -2)
-    first_in = moved(in_msg, lambda r: r % 2 == 1, -1)
-    up_msg, down_msg, d_msg = level(4, from_low, from_up, up_msg, down_msg, d_msg)
-    from_low = moved(up_msg, lambda r: r % 8 == 0, 4)
-    from_up = moved(down_msg, lambda r: r % 8 == 0, -4)
-    up_msg, down_msg, d_msg = level(3, from_low, from_up, up_msg, down_msg, d_msg)
-    y_two = moved(down_msg, lambda r: r % 8 == 4, -4)
-    y_one = moved(down_msg, lambda r: r % 8 == 4, -2)
-    y_low = moved(up_msg, lambda r: r % 8 == 4, 2)
-    n_low = moved(d_msg, lambda r: r % 8 == 0, 2)
-    n_up = moved(d_msg, lambda r: r % 8 == 0, -2)
+    late_in = moved(in_msg, (32, 24, 4), (32, 8, -4))
+    early_r = moved(up_msg, (32, 0, 12), (32, 16, 4))
+    late_r = moved(up_msg, (32, 16, 12), (32, 0, 4))
+    late_l = moved(d_msg, (32, 16, -12), (32, 0, -4))
+    early_in = moved(in_msg, (32, 24, -4), (32, 8, 4))
+    early_l = moved(d_msg, (32, 0, -12), (32, 16, -4))
+    near_a = moved(in_msg, (16, 2, -2), (16, 10, -2), (16, 14, -2))
+    near_b = moved(in_msg, (16, 6, -2))
+    first_in = moved(in_msg, (2, 1, -1))
+    four_r = moved(up_msg, (16, 0, 8))
+    four_l = moved(d_msg, (16, 0, -8))
+    separators = (separator_inverse, separator_lower, separator_upper)
+    up_three, down_msg, far = pl.pallas_call(
+        coarse_kernel,
+        out_shape=(message, message, diagonal),
+        in_specs=[smem] + [vmem] * 9,
+        out_specs=(vmem,) * 3,
+        scratch_shapes=[block] * 4,
+        compiler_params=params,
+        name="coarse",
+    )(place, *separators, *near(early_r, late_r, early_l, late_l, early_in, late_in))
+    y_two = moved(down_msg, (8, 4, -4))
+    y_one = moved(down_msg, (8, 4, -2))
+    y_low = moved(up_three, (8, 4, 2))
+    d_msg = pl.pallas_call(
+        middle_kernel,
+        out_shape=diagonal,
+        in_specs=[smem] + [vmem] * 6,
+        out_specs=vmem,
+        scratch_shapes=[block] * 2,
+        input_output_aliases={6: 0},
+        compiler_params=params,
+        name="middle",
+    )(place, *separators, *near(four_r, four_l, d_msg))
+    n_low = moved(d_msg, (8, 0, 2))
+    n_up = moved(d_msg, (8, 0, -2))
     own, other = pl.pallas_call(
         fine_kernel,
         out_shape=(both, both),
-        in_specs=[smem] + [vmem] * 11,
+        in_specs=[smem] + [vmem] * 12,
         out_specs=(vmem,) * 2,
         scratch_shapes=[block] * 4,
         compiler_params=params,
         name="fine",
-    )(place, *near(in_msg, near_in, first_in, up_msg, d_msg, from_up, y_two, y_one, y_low, n_low, n_up))
-    other = moved(other, lambda r: r % 2 == 0, 1)
+    )(place, *near(in_msg, near_a, near_b, first_in, up_three, d_msg, far, y_two, y_one, y_low, n_low, n_up))
+    other = moved(other, (2, 0, 1))
     pair = jax.ShapeDtypeStruct((2, n, n), BF)
     return pl.pallas_call(
         interior_kernel,

time: 61.3 us -> 87.7 us (1.43)
  starting transfers between devices: 17.2 us -> 33.5 us
  waiting for transfers between devices: 38.8 us -> 48.9 us
    ppermute x12 -> x17, starting transfers between devices: 17.2 us -> 33.5 us  [moved(): return lax.ppermute(value, 'tm', pairs)]
    ppermute x12 -> x17, waiting for transfers between devices: 38.8 us -> 48.9 us  [moved(): return lax.ppermute(value, 'tm', pairs)]
  transfers between devices with their start and end apart: 12 -> 17, of which waited for: 1 -> 1; matrix products, arithmetic and copies ran while one was open for 0% -> 0% of each run, Pallas kernels for 0% -> 0%
where the time goes in v3:
time: 87.7 us; the launch traced here: 87.3 us
  waiting for transfers between devices  48.9 us (56%)
  starting transfers between devices  33.5 us (38%)
  Pallas kernels  3.9 us (4%)
  between operations  1.01 us (1%)
    ppermute x17, waiting for transfers between devices, moved(): return lax.ppermute(value, 'tm', pairs)  48.9 us
    ppermute x17, starting transfers between devices, moved(): return lax.ppermute(value, 'tm', pairs)  33.5 us
    pallas_call x1, Pallas kernels, on_device(): pl.pallas_call(interior_kernel, out_shape=(pair, pair), in_specs=[smem] +...  2.33 us
  transfers between devices with their start and end apart: 17, of which 1 were waited for; matrix products, arithmetic and copies ran while one was open for 0% of the time, Pallas kernels for 0%

profile of v3, /device:TPU:1, one launch (start us, length us, event | category | flops | bytes accessed | tf_op | source)
XLA Modules:
  0.0 87.3 jit_solution(5648190925407058622)
XLA Ops:
  0.7 1.3 %pack.1 = (bf16[640,384]{1,0:T(8,128)(2,1)S(1)}, bf16[256,384]{1,0:T(8,128)(2,1)S(1)}, bf16[1024,384]{1,0:T(8,128)(2,1)S(1)}) custom-call(s32[1]{0:T(128)} %bitcast.place, bf16[1,384,384]{2,1,0:T(8,128)(2,1)} %inv.6, bf16[1,384,384]{2,1,0:T(8,128)(2,1)} %low.6, bf16[1,384,384]{2,1,0:T(8,128)(2,1)} %up.6, bf16[1,384,384]{2,1,0:T(8,128)(2,1)} %top.1, ...), custom_call_target="tpu_custom_call" | custom-call | tf_op jit(solution)/shard_map/pack/pallas_call | solution.py:329
  2.0 0.7 collective-permute-start.9
  2.7 0.7 collective-permute-start.10
  3.4 0.7 collective-permute-start.6
  4.0 0.7 collective-permute-start.8
  4.8 0.7 collective-permute-start.5
  5.5 0.7 collective-permute-start.7
  6.2 0.7 collective-permute-start.4
  6.9 0.7 collective-permute-start.3
  7.6 21.8 %collective-permute-start.2 = (bf16[1024,384]{1,0:T(8,128)(2,1)S(1)}, bf16[1024,384]{1,0:T(8,128)(2,1)S(1)}, u32[]{:S(2)}, u32[]{:S(2)}) collective-permute-start(bf16[1024,384]{1,0:T(8,128)(2,1)S(1)} %get-tuple-element.10.own_in), channel_id=1, source_target_pairs={{484,480},{492,488},{500,496},{508,504},{4,0},{12,8},{20,16},{28,2... | collective-permute-start | bytes 2359304 | tf_op jit(solution)/shard_map/ppermute | solution.py:314
  29.5 0.7 collective-permute-start.1
  30.2 0.7 collective-permute-start
  31.0 0.7 collective-permute-start.15
  31.7 0.7 collective-permute-start.14
  32.4 0.7 collective-permute-start.13
  33.1 0.7 collective-permute-start.12
  33.8 0.7 collective-permute-start.11
  34.6 0.0 copy-start.3
  34.6 0.0 copy-start.4
  34.6 0.0 copy-start.5
  34.6 0.2 fine.1
  34.8 1.3 %collective-permute-start.16 = (bf16[896,384]{1,0:T(8,128)(2,1)S(1)}, bf16[896,384]{1,0:T(8,128)(2,1)S(1)}, u32[]{:S(2)}, u32[]{:S(2)}) collective-permute-start(bf16[896,384]{1,0:T(8,128)(2,1)S(1)} %get-tuple-element.17), channel_id=1, source_target_pairs={{480,484},{488,492},{496,500},{504,508},{0,4},{8,12},{16,20},{24,2... | collective-permute-start | bytes 2064392 | tf_op jit(solution)/shard_map/ppermute | solution.py:314
  36.1 48.8 %collective-permute-done.16.other = bf16[896,384]{1,0:T(8,128)(2,1)S(1)} collective-permute-done((bf16[896,384]{1,0:T(8,128)(2,1)S(1)}, bf16[896,384]{1,0:T(8,128)(2,1)S(1)}, u32[]{:S(2)}, u32[]{:S(2)}) %collective-permute-start.16) | collective-permute-done | bytes 688160 | tf_op jit(solution)/shard_map/ppermute | solution.py:314
  85.0 2.3 %interior.1 = (bf16[2,384,384]{2,1,0:T(8,128)(2,1)}, bf16[2,384,384]{2,1,0:T(8,128)(2,1)}) custom-call(s32[1]{0:T(128)} %bitcast.place, bf16[1,384,384]{2,1,0:T(8,128)(2,1)S(1)} %copy-done.3, bf16[1,384,384]{2,1,0:T(8,128)(2,1)S(1)} %copy-done.4, bf16[1,384,384]{2,1,0:T(8,128)(2,1)S(1)} %copy-done.5, bf16[896,384]{1,0:T(8,128)(2,1)S(1)} %get-tuple-element.16.own, ...), custom_call_target="tpu_custom_call" | custom-call | tf_op jit(solution)/shard_map/interior/pallas_call | solution.py:391
  (27 shorter events, 0.1 us)
Async XLA Ops:
  0.6 30.3 %copy-start = (bf16[1,384,384]{2,1,0:T(8,128)(2,1)S(1)}, bf16[1,384,384]{2,1,0:T(8,128)(2,1)}, u32[]{:S(2)}) copy-start(bf16[1,384,384]{2,1,0:T(8,128)(2,1)} %inv.6) | copy-start | bytes 884740
  0.6 30.3 %copy-start.1 = (bf16[1,384,384]{2,1,0:T(8,128)(2,1)S(1)}, bf16[1,384,384]{2,1,0:T(8,128)(2,1)}, u32[]{:S(2)}) copy-start(bf16[1,384,384]{2,1,0:T(8,128)(2,1)} %low.6) | copy-start | bytes 884740
  0.7 30.3 %copy-start.2 = (bf16[1,384,384]{2,1,0:T(8,128)(2,1)S(1)}, bf16[1,384,384]{2,1,0:T(8,128)(2,1)}, u32[]{:S(2)}) copy-start(bf16[1,384,384]{2,1,0:T(8,128)(2,1)} %up.6) | copy-start | bytes 884740
  2.0 5.6 %collective-permute-start.9 = (bf16[640,384]{1,0:T(8,128)(2,1)S(1)}, bf16[640,384]{1,0:T(8,128)(2,1)S(1)}, u32[]{:S(2)}, u32[]{:S(2)}) collective-permute-start(bf16[640,384]{1,0:T(8,128)(2,1)S(1)} %get-tuple-element.11), channel_id=1, source_target_pairs={{480,0},{32,64},{96,128},{160,192},{224,256},{288,320},{352,384},{... | collective-permute-start | bytes 1474568 | tf_op jit(solution)/shard_map/ppermute | solution.py:314
  2.7 2.8 %collective-permute-start.10 = (bf16[256,384]{1,0:T(8,128)(2,1)S(1)}, bf16[256,384]{1,0:T(8,128)(2,1)S(1)}, u32[]{:S(2)}, u32[]{:S(2)}) collective-permute-start(bf16[256,384]{1,0:T(8,128)(2,1)S(1)} %get-tuple-element.12.d_in), channel_id=1, source_target_pairs={{480,448},{32,0},{96,64},{160,128},{224,192},{288,256},{352,320},{... | collective-permute-start | bytes 589832 | tf_op jit(solution)/shard_map/ppermute | solution.py:314
  3.4 2.8 %collective-permute-start.6 = (bf16[256,384]{1,0:T(8,128)(2,1)S(1)}, bf16[256,384]{1,0:T(8,128)(2,1)S(1)}, u32[]{:S(2)}, u32[]{:S(2)}) collective-permute-start(bf16[256,384]{1,0:T(8,128)(2,1)S(1)} %get-tuple-element.12.d_in), channel_id=1, source_target_pairs={{480,464},{32,496},{96,80},{160,112},{224,208},{288,240},{352,336}... | collective-permute-start | bytes 589832 | tf_op jit(solution)/shard_map/ppermute | solution.py:314
  4.0 26.9 %collective-permute-start.8 = (bf16[1024,384]{1,0:T(8,128)(2,1)S(1)}, bf16[1024,384]{1,0:T(8,128)(2,1)S(1)}, u32[]{:S(2)}, u32[]{:S(2)}) collective-permute-start(bf16[1024,384]{1,0:T(8,128)(2,1)S(1)} %get-tuple-element.10.own_in), channel_id=1, source_target_pairs={{0,496},{64,80},{128,112},{192,208},{256,240},{320,336},{384,368},... | collective-permute-start | bytes 2359304 | tf_op jit(solution)/shard_map/ppermute | solution.py:314
  4.8 2.1 %collective-permute-start.5 = (bf16[256,384]{1,0:T(8,128)(2,1)S(1)}, bf16[256,384]{1,0:T(8,128)(2,1)S(1)}, u32[]{:S(2)}, u32[]{:S(2)}) collective-permute-start(bf16[256,384]{1,0:T(8,128)(2,1)S(1)} %get-tuple-element.12.d_in), channel_id=1, source_target_pairs={{480,432},{32,16},{96,48},{160,144},{224,176},{288,272},{352,304},... | collective-permute-start | bytes 589832 | tf_op jit(solution)/shard_map/ppermute | solution.py:314
  5.5 26.2 %collective-permute-start.7 = (bf16[1024,384]{1,0:T(8,128)(2,1)S(1)}, bf16[1024,384]{1,0:T(8,128)(2,1)S(1)}, u32[]{:S(2)}, u32[]{:S(2)}) collective-permute-start(bf16[1024,384]{1,0:T(8,128)(2,1)S(1)} %get-tuple-element.10.own_in), channel_id=1, source_target_pairs={{0,16},{64,48},{128,144},{192,176},{256,272},{320,304},{384,400},{... | collective-permute-start | bytes 2359304 | tf_op jit(solution)/shard_map/ppermute | solution.py:314
  6.2 23.3 %collective-permute-start.4 = (bf16[640,384]{1,0:T(8,128)(2,1)S(1)}, bf16[640,384]{1,0:T(8,128)(2,1)S(1)}, u32[]{:S(2)}, u32[]{:S(2)}) collective-permute-start(bf16[640,384]{1,0:T(8,128)(2,1)S(1)} %get-tuple-element.11), channel_id=1, source_target_pairs={{480,496},{32,80},{96,112},{160,208},{224,240},{288,336},{352,368}... | collective-permute-start | bytes 1474568 | tf_op jit(solution)/shard_map/ppermute | solution.py:314
  6.9 23.3 %collective-permute-start.3 = (bf16[640,384]{1,0:T(8,128)(2,1)S(1)}, bf16[640,384]{1,0:T(8,128)(2,1)S(1)}, u32[]{:S(2)}, u32[]{:S(2)}) collective-permute-start(bf16[640,384]{1,0:T(8,128)(2,1)S(1)} %get-tuple-element.11), channel_id=1, source_target_pairs={{480,16},{32,48},{96,144},{160,176},{224,272},{288,304},{352,400},... | collective-permute-start | bytes 1474568 | tf_op jit(solution)/shard_map/ppermute | solution.py:314
  7.6 26.2 %collective-permute-start.2 = (bf16[1024,384]{1,0:T(8,128)(2,1)S(1)}, bf16[1024,384]{1,0:T(8,128)(2,1)S(1)}, u32[]{:S(2)}, u32[]{:S(2)}) collective-permute-start(bf16[1024,384]{1,0:T(8,128)(2,1)S(1)} %get-tuple-element.10.own_in), channel_id=1, source_target_pairs={{484,480},{492,488},{500,496},{508,504},{4,0},{12,8},{20,16},{28,2... | collective-permute-start | bytes 2359304 | tf_op jit(solution)/shard_map/ppermute | solution.py:314
  29.5 5.1 %collective-permute-start.1 = (bf16[1024,384]{1,0:T(8,128)(2,1)S(1)}, bf16[1024,384]{1,0:T(8,128)(2,1)S(1)}, u32[]{:S(2)}, u32[]{:S(2)}) collective-permute-start(bf16[1024,384]{1,0:T(8,128)(2,1)S(1)} %get-tuple-element.10.own_in), channel_id=1, source_target_pairs={{504,496},{56,48},{120,112},{184,176},{248,240},{312,304},{376,368... | collective-permute-start | bytes 2359304 | tf_op jit(solution)/shard_map/ppermute | solution.py:314
  30.2 4.3 %collective-permute-start = (bf16[1024,384]{1,0:T(8,128)(2,1)S(1)}, bf16[1024,384]{1,0:T(8,128)(2,1)S(1)}, u32[]{:S(2)}, u32[]{:S(2)}) collective-permute-start(bf16[1024,384]{1,0:T(8,128)(2,1)S(1)} %get-tuple-element.10.own_in), channel_id=1, source_target_pairs={{488,480},{8,0},{24,16},{40,32},{72,64},{88,80},{104,96},{136,128}... | collective-permute-start | bytes 2359304 | tf_op jit(solution)/shard_map/ppermute | solution.py:314
  31.0 1.4 %collective-permute-start.15 = (bf16[256,384]{1,0:T(8,128)(2,1)S(1)}, bf16[256,384]{1,0:T(8,128)(2,1)S(1)}, u32[]{:S(2)}, u32[]{:S(2)}) collective-permute-start(bf16[256,384]{1,0:T(8,128)(2,1)S(1)} %middle.1.d_msg), channel_id=1, source_target_pairs={{480,472},{0,504},{32,24},{64,56},{96,88},{128,120},{160,152},{192... | collective-permute-start | bytes 589832 | tf_op jit(solution)/shard_map/ppermute | solution.py:314
  31.7 1.4 %collective-permute-start.14 = (bf16[256,384]{1,0:T(8,128)(2,1)S(1)}, bf16[256,384]{1,0:T(8,128)(2,1)S(1)}, u32[]{:S(2)}, u32[]{:S(2)}) collective-permute-start(bf16[256,384]{1,0:T(8,128)(2,1)S(1)} %middle.1.d_msg), channel_id=1, source_target_pairs={{480,488},{0,8},{32,40},{64,72},{96,104},{128,136},{160,168},{192,... | collective-permute-start | bytes 589832 | tf_op jit(solution)/shard_map/ppermute | solution.py:314
  32.4 2.1 %collective-permute-start.13 = (bf16[640,384]{1,0:T(8,128)(2,1)S(1)}, bf16[640,384]{1,0:T(8,128)(2,1)S(1)}, u32[]{:S(2)}, u32[]{:S(2)}) collective-permute-start(bf16[640,384]{1,0:T(8,128)(2,1)S(1)} %get-tuple-element.13.up_msg), channel_id=1, source_target_pairs={{496,504},{16,24},{48,56},{80,88},{112,120},{144,152},{176,184},{2... | collective-permute-start | bytes 1474568 | tf_op jit(solution)/shard_map/ppermute | solution.py:314
  33.1 1.4 %collective-permute-start.12 = (bf16[640,384]{1,0:T(8,128)(2,1)S(1)}, bf16[640,384]{1,0:T(8,128)(2,1)S(1)}, u32[]{:S(2)}, u32[]{:S(2)}) collective-permute-start(bf16[640,384]{1,0:T(8,128)(2,1)S(1)} %get-tuple-element.15), channel_id=1, source_target_pairs={{496,488},{16,8},{48,40},{80,72},{112,104},{144,136},{176,168},{20... | collective-permute-start | bytes 1474568 | tf_op jit(solution)/shard_map/ppermute | solution.py:314
  33.8 0.7 collective-permute-start.11
  34.6 50.4 %copy-start.3 = (bf16[1,384,384]{2,1,0:T(8,128)(2,1)S(1)}, bf16[1,384,384]{2,1,0:T(8,128)(2,1)}, u32[]{:S(2)}) copy-start(bf16[1,384,384]{2,1,0:T(8,128)(2,1)} %inv.7) | copy-start | bytes 884740
  34.6 50.4 %copy-start.4 = (bf16[1,384,384]{2,1,0:T(8,128)(2,1)S(1)}, bf16[1,384,384]{2,1,0:T(8,128)(2,1)}, u32[]{:S(2)}) copy-start(bf16[1,384,384]{2,1,0:T(8,128)(2,1)} %low.7) | copy-start | bytes 884740
  34.6 50.4 %copy-start.5 = (bf16[1,384,384]{2,1,0:T(8,128)(2,1)S(1)}, bf16[1,384,384]{2,1,0:T(8,128)(2,1)}, u32[]{:S(2)}) copy-start(bf16[1,384,384]{2,1,0:T(8,128)(2,1)} %up.7) | copy-start | bytes 884740
  34.8 50.1 %collective-permute-start.16 = (bf16[896,384]{1,0:T(8,128)(2,1)S(1)}, bf16[896,384]{1,0:T(8,128)(2,1)S(1)}, u32[]{:S(2)}, u32[]{:S(2)}) collective-permute-start(bf16[896,384]{1,0:T(8,128)(2,1)S(1)} %get-tuple-element.17), channel_id=1, source_target_pairs={{480,484},{488,492},{496,500},{504,508},{0,4},{8,12},{16,20},{24,2... | collective-permute-start | bytes 2064392 | tf_op jit(solution)/shard_map/ppermute | solution.py:314

commit v4 on v3

--- a/solution.py
+++ b/solution.py
@@ -187,12 +187,7 @@
         )
 
 
-def fine_kernel(place, own_in, near_a, near_b, first_in, up_msg, d_msg, far, y_two, y_one, y_low, n_low, n_up,
-                own, other, lo, hi, mid, half):
-    n = up_msg.shape[1]
-    t = n // 3
-    r, core, chip = roles(place)
-
+def fine_steps(t, n, first_in, own, other, lo, hi, mid, half):
     def go(low_src, up_src, coup, holds, second, odd):
         unpack(lo, low_src)
         unpack(hi, up_src)
@@ -233,39 +228,59 @@
         else:
             own[: 2 * t, :] = low_src[: 2 * t, :]
 
-    phase = jnp.where(core == 0, lax.rem(chip, 4), 4)
-
-    @pl.when(phase == 0)
+    return go
+
+
+def even_kernel(place, near_a, near_b, first_in, up_msg, d_msg, far, y_two, own, other, lo, hi, mid, half):
+    n = up_msg.shape[1]
+    t = n // 3
+    r, _, _ = roles(place)
+    go = fine_steps(t, n, first_in, own, other, lo, hi, mid, half)
+
+    @pl.when(jnp.logical_or(r == 0, r == 8))
     def _():
         go(d_msg, y_two, y_two, False, near_a, False)
 
-    @pl.when(phase == 1)
+    @pl.when(r == 4)
+    def _():
+        go(up_msg, far, up_msg, True, near_b, False)
+
+    @pl.when(r == 12)
+    def _():
+        go(up_msg, far, up_msg, True, near_a, False)
+
+
+def odd_kernel(place, own_in, first_in, y_one, y_low, n_low, n_up, own_0, other_0, own, other, lo, hi, mid, half):
+    n = own_in.shape[1]
+    t = n // 3
+    r, _, _ = roles(place)
+    go = fine_steps(t, n, first_in, own, other, lo, hi, mid, half)
+
+    @pl.when(jnp.logical_or(r == 2, r == 10))
     def _():
         go(n_low, y_one, y_one, False, own_in, True)
 
-    @pl.when(jnp.logical_and(phase == 2, r == 4))
-    def _():
-        go(up_msg, far, up_msg, True, near_b, False)
-
-    @pl.when(jnp.logical_and(phase == 2, r == 12))
-    def _():
-        go(up_msg, far, up_msg, True, near_a, False)
-
-    @pl.when(phase == 3)
+    @pl.when(jnp.logical_or(r == 6, r == 14))
     def _():
         go(y_low, n_up, y_low, True, own_in, True)
 
 
-def interior_kernel(place, inv, low, up, own, other, out_diag, out_below, here, above):
+def interior_kernel(place, inv, low, up, own, other, out_diag, out_below, here, above, p_buf, q_buf, d_buf, sems):
     n = low.shape[1]
     t = n // 3
     _, core, _ = roles(place)
+    writes = [
+        pltpu.make_async_copy(here, out_diag.at[0], sems.at[0]),
+        pltpu.make_async_copy(p_buf, out_below.at[0], sems.at[1]),
+        pltpu.make_async_copy(q_buf, out_below.at[1], sems.at[2]),
+        pltpu.make_async_copy(d_buf, out_diag.at[1], sems.at[3]),
+    ]
 
     def go(src, holds):
         unpack(here, src)
+        writes[0].start()
         unpack(above, src, 2 * t)
         coup = src[4 * t :, :]
-        out_diag[0] = here[...]
         if holds:
             p = mm(low[0], here[...]) + mt(up[0], coup)
             q = mm(low[0], coup) + mm(up[0], above[...])
@@ -274,9 +289,12 @@
             q = mt(low[0], coup) + mm(up[0], above[...])
         p = p.astype(BF)
         q = q.astype(BF)
-        out_below[0] = p
-        out_below[1] = q.T
-        out_diag[1] = (inv[0].astype(F32) + mt(p, low[0]) + mt(q, up[0])).astype(BF)
+        p_buf[...] = p
+        writes[1].start()
+        q_buf[...] = q.T
+        writes[2].start()
+        d_buf[...] = (inv[0].astype(F32) + mt(p, low[0]) + mt(q, up[0])).astype(BF)
+        writes[3].start()
 
     @pl.when(core == 0)
     def _():
@@ -285,6 +303,9 @@
     @pl.when(core == 1)
     def _():
         go(other, True)
+
+    for write in writes:
+        write.wait()
 
 
 def on_device(
@@ -378,22 +399,32 @@
     n_low = moved(d_msg, (8, 0, 2))
     n_up = moved(d_msg, (8, 0, -2))
     own, other = pl.pallas_call(
-        fine_kernel,
+        even_kernel,
         out_shape=(both, both),
-        in_specs=[smem] + [vmem] * 12,
+        in_specs=[smem] + [vmem] * 7,
         out_specs=(vmem,) * 2,
         scratch_shapes=[block] * 4,
         compiler_params=params,
-        name="fine",
-    )(place, *near(in_msg, near_a, near_b, first_in, up_three, d_msg, far, y_two, y_one, y_low, n_low, n_up))
+        name="even",
+    )(place, *near(near_a, near_b, first_in, up_three, d_msg, far, y_two))
+    own, other = pl.pallas_call(
+        odd_kernel,
+        out_shape=(both, both),
+        in_specs=[smem] + [vmem] * 8,
+        out_specs=(vmem,) * 2,
+        scratch_shapes=[block] * 4,
+        input_output_aliases={7: 0, 8: 1},
+        compiler_params=params,
+        name="odd",
+    )(place, *near(in_msg, first_in, y_one, y_low, n_low, n_up, own, other))
     other = moved(other, (2, 0, 1))
     pair = jax.ShapeDtypeStruct((2, n, n), BF)
     return pl.pallas_call(
         interior_kernel,
         out_shape=(pair, pair),
         in_specs=[smem] + [vmem] * 5,
-        out_specs=(vmem,) * 2,
-        scratch_shapes=[block] * 2,
+        out_specs=(anywhere,) * 2,
+        scratch_shapes=[block] * 5 + [pltpu.SemaphoreType.DMA((4,))],
         compiler_params=params,
         name="interior",
     )(place, interior_inverse, interior_lower, interior_upper, *near(own, other))

time: 87.7 us -> 64 us (0.73)
  the two profiles are of different devices: /device:TPU:1 before, /device:TPU:33 now
where the time goes in v4:
time: 64 us; the launch traced here: 63.6 us
  waiting for transfers between devices  44.3 us (69%)
  starting transfers between devices  14.4 us (22%)
  Pallas kernels  3.68 us (6%)
  between operations  1.17 us (2%)
    ppermute x17, waiting for transfers between devices, moved(): return lax.ppermute(value, 'tm', pairs)  44.3 us
    ppermute x17, starting transfers between devices, moved(): return lax.ppermute(value, 'tm', pairs)  14.4 us
    pallas_call x1, Pallas kernels, on_device(): pl.pallas_call(interior_kernel, out_shape=(pair, pair), in_specs=[smem] +...  2.11 us
    pallas_call x1, Pallas kernels, on_device(): pl.pallas_call(pack_kernel, out_shape=(message, diagonal, inputs), in_spe...  1.3 us
  transfers between devices with their start and end apart: 17, of which 1 were waited for; matrix products, arithmetic and copies ran while one was open for 0% of the time, Pallas kernels for 0%

profile of v4, /device:TPU:33, one launch (start us, length us, event | category | flops | bytes accessed | tf_op | source)
XLA Modules:
  0.0 63.6 jit_solution(12956655933930362096)
XLA Ops:
  0.7 1.3 %pack.1 = (bf16[640,384]{1,0:T(8,128)(2,1)S(1)}, bf16[256,384]{1,0:T(8,128)(2,1)S(1)}, bf16[1024,384]{1,0:T(8,128)(2,1)S(1)}) custom-call(s32[1]{0:T(128)} %bitcast.place, bf16[1,384,384]{2,1,0:T(8,128)(2,1)} %inv.6, bf16[1,384,384]{2,1,0:T(8,128)(2,1)} %low.6, bf16[1,384,384]{2,1,0:T(8,128)(2,1)} %up.6, bf16[1,384,384]{2,1,0:T(8,128)(2,1)} %top.1, ...), custom_call_target="tpu_custom_call" | custom-call | tf_op jit(solution)/shard_map/pack/pallas_call | solution.py:350
  2.0 0.7 %collective-permute-start.5 = (bf16[1024,384]{1,0:T(8,128)(2,1)S(1)}, bf16[1024,384]{1,0:T(8,128)(2,1)S(1)}, u32[]{:S(2)}, u32[]{:S(2)}) collective-permute-start(bf16[1024,384]{1,0:T(8,128)(2,1)S(1)} %get-tuple-element.12.own_in), channel_id=1, source_target_pairs={{0,16},{64,48},{128,144},{192,176},{256,272},{320,304},{384,400},{... | collective-permute-start | bytes 2359304 | tf_op jit(solution)/shard_map/ppermute | solution.py:335
  2.7 0.7 %collective-permute-start.3 = (bf16[256,384]{1,0:T(8,128)(2,1)S(1)}, bf16[256,384]{1,0:T(8,128)(2,1)S(1)}, u32[]{:S(2)}, u32[]{:S(2)}) collective-permute-start(bf16[256,384]{1,0:T(8,128)(2,1)S(1)} %get-tuple-element.14.d_in), channel_id=1, source_target_pairs={{480,432},{32,16},{96,48},{160,144},{224,176},{288,272},{352,304},... | collective-permute-start | bytes 589832 | tf_op jit(solution)/shard_map/ppermute | solution.py:335
  3.4 0.7 %collective-permute-start.6 = (bf16[1024,384]{1,0:T(8,128)(2,1)S(1)}, bf16[1024,384]{1,0:T(8,128)(2,1)S(1)}, u32[]{:S(2)}, u32[]{:S(2)}) collective-permute-start(bf16[1024,384]{1,0:T(8,128)(2,1)S(1)} %get-tuple-element.12.own_in), channel_id=1, source_target_pairs={{0,496},{64,80},{128,112},{192,208},{256,240},{320,336},{384,368},... | collective-permute-start | bytes 2359304 | tf_op jit(solution)/shard_map/ppermute | solution.py:335
  4.1 0.7 %collective-permute-start.1 = (bf16[640,384]{1,0:T(8,128)(2,1)S(1)}, bf16[640,384]{1,0:T(8,128)(2,1)S(1)}, u32[]{:S(2)}, u32[]{:S(2)}) collective-permute-start(bf16[640,384]{1,0:T(8,128)(2,1)S(1)} %get-tuple-element.13), channel_id=1, source_target_pairs={{480,16},{32,48},{96,144},{160,176},{224,272},{288,304},{352,400},... | collective-permute-start | bytes 1474568 | tf_op jit(solution)/shard_map/ppermute | solution.py:335
  4.8 0.7 %collective-permute-start.2 = (bf16[640,384]{1,0:T(8,128)(2,1)S(1)}, bf16[640,384]{1,0:T(8,128)(2,1)S(1)}, u32[]{:S(2)}, u32[]{:S(2)}) collective-permute-start(bf16[640,384]{1,0:T(8,128)(2,1)S(1)} %get-tuple-element.13), channel_id=1, source_target_pairs={{480,496},{32,80},{96,112},{160,208},{224,240},{288,336},{352,368}... | collective-permute-start | bytes 1474568 | tf_op jit(solution)/shard_map/ppermute | solution.py:335
  5.5 0.7 %collective-permute-start.4 = (bf16[256,384]{1,0:T(8,128)(2,1)S(1)}, bf16[256,384]{1,0:T(8,128)(2,1)S(1)}, u32[]{:S(2)}, u32[]{:S(2)}) collective-permute-start(bf16[256,384]{1,0:T(8,128)(2,1)S(1)} %get-tuple-element.14.d_in), channel_id=1, source_target_pairs={{480,464},{32,496},{96,80},{160,112},{224,208},{288,240},{352,336}... | collective-permute-start | bytes 589832 | tf_op jit(solution)/shard_map/ppermute | solution.py:335
  6.2 2.6 %collective-permute-start = (bf16[1024,384]{1,0:T(8,128)(2,1)S(1)}, bf16[1024,384]{1,0:T(8,128)(2,1)S(1)}, u32[]{:S(2)}, u32[]{:S(2)}) collective-permute-start(bf16[1024,384]{1,0:T(8,128)(2,1)S(1)} %get-tuple-element.12.own_in), channel_id=1, source_target_pairs={{484,480},{492,488},{500,496},{508,504},{4,0},{12,8},{20,16},{28,2... | collective-permute-start | bytes 2359304 | tf_op jit(solution)/shard_map/ppermute | solution.py:335
  8.8 0.7 %collective-permute-start.9 = (bf16[640,384]{1,0:T(8,128)(2,1)S(1)}, bf16[640,384]{1,0:T(8,128)(2,1)S(1)}, u32[]{:S(2)}, u32[]{:S(2)}) collective-permute-start(bf16[640,384]{1,0:T(8,128)(2,1)S(1)} %get-tuple-element.13), channel_id=1, source_target_pairs={{480,0},{32,64},{96,128},{160,192},{224,256},{288,320},{352,384},{... | collective-permute-start | bytes 1474568 | tf_op jit(solution)/shard_map/ppermute | solution.py:335
  9.6 0.7 %collective-permute-start.13 = (bf16[1024,384]{1,0:T(8,128)(2,1)S(1)}, bf16[1024,384]{1,0:T(8,128)(2,1)S(1)}, u32[]{:S(2)}, u32[]{:S(2)}) collective-permute-start(bf16[1024,384]{1,0:T(8,128)(2,1)S(1)} %get-tuple-element.12.own_in), channel_id=1, source_target_pairs={{488,480},{8,0},{24,16},{40,32},{72,64},{88,80},{104,96},{136,128}... | collective-permute-start | bytes 2359304 | tf_op jit(solution)/shard_map/ppermute | solution.py:335
  10.3 0.7 %collective-permute-start.14 = (bf16[1024,384]{1,0:T(8,128)(2,1)S(1)}, bf16[1024,384]{1,0:T(8,128)(2,1)S(1)}, u32[]{:S(2)}, u32[]{:S(2)}) collective-permute-start(bf16[1024,384]{1,0:T(8,128)(2,1)S(1)} %get-tuple-element.12.own_in), channel_id=1, source_target_pairs={{504,496},{56,48},{120,112},{184,176},{248,240},{312,304},{376,368... | collective-permute-start | bytes 2359304 | tf_op jit(solution)/shard_map/ppermute | solution.py:335
  11.0 0.7 %collective-permute-start.10 = (bf16[256,384]{1,0:T(8,128)(2,1)S(1)}, bf16[256,384]{1,0:T(8,128)(2,1)S(1)}, u32[]{:S(2)}, u32[]{:S(2)}) collective-permute-start(bf16[256,384]{1,0:T(8,128)(2,1)S(1)} %get-tuple-element.14.d_in), channel_id=1, source_target_pairs={{480,448},{32,0},{96,64},{160,128},{224,192},{288,256},{352,320},{... | collective-permute-start | bytes 589832 | tf_op jit(solution)/shard_map/ppermute | solution.py:335
  11.8 0.7 %collective-permute-start.15 = (bf16[640,384]{1,0:T(8,128)(2,1)S(1)}, bf16[640,384]{1,0:T(8,128)(2,1)S(1)}, u32[]{:S(2)}, u32[]{:S(2)}) collective-permute-start(bf16[640,384]{1,0:T(8,128)(2,1)S(1)} %get-tuple-element.15), channel_id=1, source_target_pairs={{496,480},{16,0},{48,32},{80,64},{112,96},{144,128},{176,160},{208... | collective-permute-start | bytes 1474568 | tf_op jit(solution)/shard_map/ppermute | solution.py:335
  12.5 0.7 %collective-permute-start.7 = (bf16[640,384]{1,0:T(8,128)(2,1)S(1)}, bf16[640,384]{1,0:T(8,128)(2,1)S(1)}, u32[]{:S(2)}, u32[]{:S(2)}) collective-permute-start(bf16[640,384]{1,0:T(8,128)(2,1)S(1)} %get-tuple-element.15), channel_id=1, source_target_pairs={{496,488},{16,8},{48,40},{80,72},{112,104},{144,136},{176,168},{20... | collective-permute-start | bytes 1474568 | tf_op jit(solution)/shard_map/ppermute | solution.py:335
  13.2 0.7 %collective-permute-start.8 = (bf16[640,384]{1,0:T(8,128)(2,1)S(1)}, bf16[640,384]{1,0:T(8,128)(2,1)S(1)}, u32[]{:S(2)}, u32[]{:S(2)}) collective-permute-start(bf16[640,384]{1,0:T(8,128)(2,1)S(1)} %get-tuple-element.16.up_msg), channel_id=1, source_target_pairs={{496,504},{16,24},{48,56},{80,88},{112,120},{144,152},{176,184},{2... | collective-permute-start | bytes 1474568 | tf_op jit(solution)/shard_map/ppermute | solution.py:335
  13.9 0.7 %collective-permute-start.11 = (bf16[256,384]{1,0:T(8,128)(2,1)S(1)}, bf16[256,384]{1,0:T(8,128)(2,1)S(1)}, u32[]{:S(2)}, u32[]{:S(2)}) collective-permute-start(bf16[256,384]{1,0:T(8,128)(2,1)S(1)} %middle.1.d_msg), channel_id=1, source_target_pairs={{480,488},{0,8},{32,40},{64,72},{96,104},{128,136},{160,168},{192,... | collective-permute-start | bytes 589832 | tf_op jit(solution)/shard_map/ppermute | solution.py:335
  14.6 0.7 %collective-permute-start.12 = (bf16[256,384]{1,0:T(8,128)(2,1)S(1)}, bf16[256,384]{1,0:T(8,128)(2,1)S(1)}, u32[]{:S(2)}, u32[]{:S(2)}) collective-permute-start(bf16[256,384]{1,0:T(8,128)(2,1)S(1)} %middle.1.d_msg), channel_id=1, source_target_pairs={{480,472},{0,504},{32,24},{64,56},{96,88},{128,120},{160,152},{192... | collective-permute-start | bytes 589832 | tf_op jit(solution)/shard_map/ppermute | solution.py:335
  15.3 0.2 even.1
  15.6 0.0 copy-start.3
  15.6 0.0 copy-start.4
  15.6 0.0 copy-start.5
  15.6 1.4 %collective-permute-start.16 = (bf16[896,384]{1,0:T(8,128)(2,1)S(1)}, bf16[896,384]{1,0:T(8,128)(2,1)S(1)}, u32[]{:S(2)}, u32[]{:S(2)}) collective-permute-start(bf16[896,384]{1,0:T(8,128)(2,1)S(1)} %get-tuple-element.21), channel_id=1, source_target_pairs={{480,484},{488,492},{496,500},{504,508},{0,4},{8,12},{16,20},{24,2... | collective-permute-start | bytes 2064392 | tf_op jit(solution)/shard_map/ppermute | solution.py:335
  17.1 44.3 %collective-permute-done.16.other = bf16[896,384]{1,0:T(8,128)(2,1)S(1)} collective-permute-done((bf16[896,384]{1,0:T(8,128)(2,1)S(1)}, bf16[896,384]{1,0:T(8,128)(2,1)S(1)}, u32[]{:S(2)}, u32[]{:S(2)}) %collective-permute-start.16) | collective-permute-done | bytes 688160 | tf_op jit(solution)/shard_map/ppermute | solution.py:335
  61.4 2.1 %interior.1 = (bf16[2,384,384]{2,1,0:T(8,128)(2,1)}, bf16[2,384,384]{2,1,0:T(8,128)(2,1)}) custom-call(s32[1]{0:T(128)} %bitcast.place, bf16[1,384,384]{2,1,0:T(8,128)(2,1)S(1)} %copy-done.3, bf16[1,384,384]{2,1,0:T(8,128)(2,1)S(1)} %copy-done.4, bf16[1,384,384]{2,1,0:T(8,128)(2,1)S(1)} %copy-done.5, bf16[896,384]{1,0:T(8,128)(2,1)S(1)} %get-tuple-element.20.own, ...), custom_call_target="tpu_custom_call" | custom-call | tf_op jit(solution)/shard_map/interior/pallas_call | solution.py:422
  (28 shorter events, 0.1 us)
Async XLA Ops:
  0.6 11.1 %copy-start = (bf16[1,384,384]{2,1,0:T(8,128)(2,1)S(1)}, bf16[1,384,384]{2,1,0:T(8,128)(2,1)}, u32[]{:S(2)}) copy-start(bf16[1,384,384]{2,1,0:T(8,128)(2,1)} %inv.6) | copy-start | bytes 884740
  0.6 11.1 %copy-start.1 = (bf16[1,384,384]{2,1,0:T(8,128)(2,1)S(1)}, bf16[1,384,384]{2,1,0:T(8,128)(2,1)}, u32[]{:S(2)}) copy-start(bf16[1,384,384]{2,1,0:T(8,128)(2,1)} %low.6) | copy-start | bytes 884740
  0.7 11.1 %copy-start.2 = (bf16[1,384,384]{2,1,0:T(8,128)(2,1)S(1)}, bf16[1,384,384]{2,1,0:T(8,128)(2,1)}, u32[]{:S(2)}) copy-start(bf16[1,384,384]{2,1,0:T(8,128)(2,1)} %up.6) | copy-start | bytes 884740
  2.0 8.3 %collective-permute-start.5 = (bf16[1024,384]{1,0:T(8,128)(2,1)S(1)}, bf16[1024,384]{1,0:T(8,128)(2,1)S(1)}, u32[]{:S(2)}, u32[]{:S(2)}) collective-permute-start(bf16[1024,384]{1,0:T(8,128)(2,1)S(1)} %get-tuple-element.12.own_in), channel_id=1, source_target_pairs={{0,16},{64,48},{128,144},{192,176},{256,272},{320,304},{384,400},{... | collective-permute-start | bytes 2359304 | tf_op jit(solution)/shard_map/ppermute | solution.py:335
  2.7 2.8 %collective-permute-start.3 = (bf16[256,384]{1,0:T(8,128)(2,1)S(1)}, bf16[256,384]{1,0:T(8,128)(2,1)S(1)}, u32[]{:S(2)}, u32[]{:S(2)}) collective-permute-start(bf16[256,384]{1,0:T(8,128)(2,1)S(1)} %get-tuple-element.14.d_in), channel_id=1, source_target_pairs={{480,432},{32,16},{96,48},{160,144},{224,176},{288,272},{352,304},... | collective-permute-start | bytes 589832 | tf_op jit(solution)/shard_map/ppermute | solution.py:335
  3.4 7.6 %collective-permute-start.6 = (bf16[1024,384]{1,0:T(8,128)(2,1)S(1)}, bf16[1024,384]{1,0:T(8,128)(2,1)S(1)}, u32[]{:S(2)}, u32[]{:S(2)}) collective-permute-start(bf16[1024,384]{1,0:T(8,128)(2,1)S(1)} %get-tuple-element.12.own_in), channel_id=1, source_target_pairs={{0,496},{64,80},{128,112},{192,208},{256,240},{320,336},{384,368},... | collective-permute-start | bytes 2359304 | tf_op jit(solution)/shard_map/ppermute | solution.py:335
  4.1 4.7 %collective-permute-start.1 = (bf16[640,384]{1,0:T(8,128)(2,1)S(1)}, bf16[640,384]{1,0:T(8,128)(2,1)S(1)}, u32[]{:S(2)}, u32[]{:S(2)}) collective-permute-start(bf16[640,384]{1,0:T(8,128)(2,1)S(1)} %get-tuple-element.13), channel_id=1, source_target_pairs={{480,16},{32,48},{96,144},{160,176},{224,272},{288,304},{352,400},... | collective-permute-start | bytes 1474568 | tf_op jit(solution)/shard_map/ppermute | solution.py:335
  4.8 4.8 %collective-permute-start.2 = (bf16[640,384]{1,0:T(8,128)(2,1)S(1)}, bf16[640,384]{1,0:T(8,128)(2,1)S(1)}, u32[]{:S(2)}, u32[]{:S(2)}) collective-permute-start(bf16[640,384]{1,0:T(8,128)(2,1)S(1)} %get-tuple-element.13), channel_id=1, source_target_pairs={{480,496},{32,80},{96,112},{160,208},{224,240},{288,336},{352,368}... | collective-permute-start | bytes 1474568 | tf_op jit(solution)/shard_map/ppermute | solution.py:335
  5.5 0.7 %collective-permute-start.4 = (bf16[256,384]{1,0:T(8,128)(2,1)S(1)}, bf16[256,384]{1,0:T(8,128)(2,1)S(1)}, u32[]{:S(2)}, u32[]{:S(2)}) collective-permute-start(bf16[256,384]{1,0:T(8,128)(2,1)S(1)} %get-tuple-element.14.d_in), channel_id=1, source_target_pairs={{480,464},{32,496},{96,80},{160,112},{224,208},{288,240},{352,336}... | collective-permute-start | bytes 589832 | tf_op jit(solution)/shard_map/ppermute | solution.py:335
  6.2 7.0 %collective-permute-start = (bf16[1024,384]{1,0:T(8,128)(2,1)S(1)}, bf16[1024,384]{1,0:T(8,128)(2,1)S(1)}, u32[]{:S(2)}, u32[]{:S(2)}) collective-permute-start(bf16[1024,384]{1,0:T(8,128)(2,1)S(1)} %get-tuple-element.12.own_in), channel_id=1, source_target_pairs={{484,480},{492,488},{500,496},{508,504},{4,0},{12,8},{20,16},{28,2... | collective-permute-start | bytes 2359304 | tf_op jit(solution)/shard_map/ppermute | solution.py:335
  8.8 3.6 %collective-permute-start.9 = (bf16[640,384]{1,0:T(8,128)(2,1)S(1)}, bf16[640,384]{1,0:T(8,128)(2,1)S(1)}, u32[]{:S(2)}, u32[]{:S(2)}) collective-permute-start(bf16[640,384]{1,0:T(8,128)(2,1)S(1)} %get-tuple-element.13), channel_id=1, source_target_pairs={{480,0},{32,64},{96,128},{160,192},{224,256},{288,320},{352,384},{... | collective-permute-start | bytes 1474568 | tf_op jit(solution)/shard_map/ppermute | solution.py:335
  9.6 4.4 %collective-permute-start.13 = (bf16[1024,384]{1,0:T(8,128)(2,1)S(1)}, bf16[1024,384]{1,0:T(8,128)(2,1)S(1)}, u32[]{:S(2)}, u32[]{:S(2)}) collective-permute-start(bf16[1024,384]{1,0:T(8,128)(2,1)S(1)} %get-tuple-element.12.own_in), channel_id=1, source_target_pairs={{488,480},{8,0},{24,16},{40,32},{72,64},{88,80},{104,96},{136,128}... | collective-permute-start | bytes 2359304 | tf_op jit(solution)/shard_map/ppermute | solution.py:335
  10.3 4.3 %collective-permute-start.14 = (bf16[1024,384]{1,0:T(8,128)(2,1)S(1)}, bf16[1024,384]{1,0:T(8,128)(2,1)S(1)}, u32[]{:S(2)}, u32[]{:S(2)}) collective-permute-start(bf16[1024,384]{1,0:T(8,128)(2,1)S(1)} %get-tuple-element.12.own_in), channel_id=1, source_target_pairs={{504,496},{56,48},{120,112},{184,176},{248,240},{312,304},{376,368... | collective-permute-start | bytes 2359304 | tf_op jit(solution)/shard_map/ppermute | solution.py:335
  11.0 0.8 %collective-permute-start.10 = (bf16[256,384]{1,0:T(8,128)(2,1)S(1)}, bf16[256,384]{1,0:T(8,128)(2,1)S(1)}, u32[]{:S(2)}, u32[]{:S(2)}) collective-permute-start(bf16[256,384]{1,0:T(8,128)(2,1)S(1)} %get-tuple-element.14.d_in), channel_id=1, source_target_pairs={{480,448},{32,0},{96,64},{160,128},{224,192},{288,256},{352,320},{... | collective-permute-start | bytes 589832 | tf_op jit(solution)/shard_map/ppermute | solution.py:335
  11.8 3.5 %collective-permute-start.15 = (bf16[640,384]{1,0:T(8,128)(2,1)S(1)}, bf16[640,384]{1,0:T(8,128)(2,1)S(1)}, u32[]{:S(2)}, u32[]{:S(2)}) collective-permute-start(bf16[640,384]{1,0:T(8,128)(2,1)S(1)} %get-tuple-element.15), channel_id=1, source_target_pairs={{496,480},{16,0},{48,32},{80,64},{112,96},{144,128},{176,160},{208... | collective-permute-start | bytes 1474568 | tf_op jit(solution)/shard_map/ppermute | solution.py:335
  12.5 3.1 %collective-permute-start.7 = (bf16[640,384]{1,0:T(8,128)(2,1)S(1)}, bf16[640,384]{1,0:T(8,128)(2,1)S(1)}, u32[]{:S(2)}, u32[]{:S(2)}) collective-permute-start(bf16[640,384]{1,0:T(8,128)(2,1)S(1)} %get-tuple-element.15), channel_id=1, source_target_pairs={{496,488},{16,8},{48,40},{80,72},{112,104},{144,136},{176,168},{20... | collective-permute-start | bytes 1474568 | tf_op jit(solution)/shard_map/ppermute | solution.py:335
  13.2 2.4 %collective-permute-start.8 = (bf16[640,384]{1,0:T(8,128)(2,1)S(1)}, bf16[640,384]{1,0:T(8,128)(2,1)S(1)}, u32[]{:S(2)}, u32[]{:S(2)}) collective-permute-start(bf16[640,384]{1,0:T(8,128)(2,1)S(1)} %get-tuple-element.16.up_msg), channel_id=1, source_target_pairs={{496,504},{16,24},{48,56},{80,88},{112,120},{144,152},{176,184},{2... | collective-permute-start | bytes 1474568 | tf_op jit(solution)/shard_map/ppermute | solution.py:335
  13.9 1.6 %collective-permute-start.11 = (bf16[256,384]{1,0:T(8,128)(2,1)S(1)}, bf16[256,384]{1,0:T(8,128)(2,1)S(1)}, u32[]{:S(2)}, u32[]{:S(2)}) collective-permute-start(bf16[256,384]{1,0:T(8,128)(2,1)S(1)} %middle.1.d_msg), channel_id=1, source_target_pairs={{480,488},{0,8},{32,40},{64,72},{96,104},{128,136},{160,168},{192,... | collective-permute-start | bytes 589832 | tf_op jit(solution)/shard_map/ppermute | solution.py:335
  14.6 0.9 %collective-permute-start.12 = (bf16[256,384]{1,0:T(8,128)(2,1)S(1)}, bf16[256,384]{1,0:T(8,128)(2,1)S(1)}, u32[]{:S(2)}, u32[]{:S(2)}) collective-permute-start(bf16[256,384]{1,0:T(8,128)(2,1)S(1)} %middle.1.d_msg), channel_id=1, source_target_pairs={{480,472},{0,504},{32,24},{64,56},{96,88},{128,120},{160,152},{192... | collective-permute-start | bytes 589832 | tf_op jit(solution)/shard_map/ppermute | solution.py:335
  15.6 45.8 %copy-start.3 = (bf16[1,384,384]{2,1,0:T(8,128)(2,1)S(1)}, bf16[1,384,384]{2,1,0:T(8,128)(2,1)}, u32[]{:S(2)}) copy-start(bf16[1,384,384]{2,1,0:T(8,128)(2,1)} %inv.7) | copy-start | bytes 884740
  15.6 45.8 %copy-start.4 = (bf16[1,384,384]{2,1,0:T(8,128)(2,1)S(1)}, bf16[1,384,384]{2,1,0:T(8,128)(2,1)}, u32[]{:S(2)}) copy-start(bf16[1,384,384]{2,1,0:T(8,128)(2,1)} %low.7) | copy-start | bytes 884740
  15.6 45.8 %copy-start.5 = (bf16[1,384,384]{2,1,0:T(8,128)(2,1)S(1)}, bf16[1,384,384]{2,1,0:T(8,128)(2,1)}, u32[]{:S(2)}) copy-start(bf16[1,384,384]{2,1,0:T(8,128)(2,1)} %up.7) | copy-start | bytes 884740
  15.6 45.7 %collective-permute-start.16 = (bf16[896,384]{1,0:T(8,128)(2,1)S(1)}, bf16[896,384]{1,0:T(8,128)(2,1)S(1)}, u32[]{:S(2)}, u32[]{:S(2)}) collective-permute-start(bf16[896,384]{1,0:T(8,128)(2,1)S(1)} %get-tuple-element.21), channel_id=1, source_target_pairs={{480,484},{488,492},{496,500},{504,508},{0,4},{8,12},{16,20},{24,2... | collective-permute-start | bytes 2064392 | tf_op jit(solution)/shard_map/ppermute | solution.py:335

commit v5 on v4

--- a/solution.py
+++ b/solution.py
@@ -85,7 +85,7 @@
             copies += diag_copies(top, dst)
         run(copies)
 
-    @pl.when(jnp.logical_or(jnp.logical_or(core == 1, lax.rem(chip, 2) == 1), r == 8))
+    @pl.when(jnp.logical_or(jnp.logical_or(core == 1, lax.rem(chip, 2) == 1), jnp.logical_or(r == 8, r == 12)))
     def _():
         copies = diag_copies(inv, in_msg)
         copies.append((low.at[0], in_msg.at[2 * t : 2 * t + n, :]))
@@ -105,15 +105,120 @@
     return (lambda pr, pc, fr, fc, w: inv[0, fr : fr + t, fc : fc + w], low[0], up[0])
 
 
+def message_writers(t, n, *messages):
+    def out_coup(v):
+        messages[0][2 * t : 2 * t + n, :] = v
+
+    def out_diag(pr, pc, width, v):
+        for dst in messages:
+            dst[pr : pr + t, pc : pc + width] = v
+
+    return out_coup, out_diag
+
+
+def drop(*_):
+    pass
+
+
+def outer_level(t, n, low_src, up_src, outer, mid_dst, mid_row, ends, keep_up):
+    lo, hi, mid, half = ends
+    unpack(lo, low_src)
+    unpack(hi, up_src)
+
+    def keep(v):
+        half[...] = v
+
+    def out_mid(pr, pc, width, v):
+        mid_dst[mid_row + pr : mid_row + pr + t, pc : pc + width] = v
+
+    eliminate(
+        t, *outer, lo, hi, low_src[2 * t : 2 * t + n, :], True,
+        drop if keep_up else keep, keep if keep_up else drop, out_mid,
+    )
+    unpack(mid, mid_dst, mid_row)
+
+
+def lower_steps(t, n, low_src, up_src, outer, own, mid_dst, mid_row, down_msg, up_msg, ends):
+    lo, _, mid, half = ends
+    outer_level(t, n, low_src, up_src, outer, mid_dst, mid_row, ends, False)
+    out_down, _ = message_writers(t, n, down_msg)
+    out_up, _ = message_writers(t, n, up_msg)
+    _, out_diag = message_writers(t, n, up_msg, down_msg)
+    eliminate(t, *own, lo, mid, half[...], False, out_down, out_up, out_diag)
+
+
+def upper_steps(t, n, low_src, up_src, outer, own, mid_dst, mid_row, down_msg, up_msg, ends):
+    _, hi, mid, half = ends
+    outer_level(t, n, low_src, up_src, outer, mid_dst, mid_row, ends, True)
+    out_down, _ = message_writers(t, n, down_msg)
+    if up_msg is None:
+        out_up = drop
+        _, out_diag = message_writers(t, n, down_msg)
+    else:
+        out_up, _ = message_writers(t, n, up_msg)
+        _, out_diag = message_writers(t, n, up_msg, down_msg)
+    eliminate(t, *own, mid, hi, half[...], True, out_down, out_up, out_diag)
+
+
 def coarse_kernel(place, inv, low, up, early_r, late_r, early_l, late_l, early_in, late_in,
-                  up_msg, down_msg, far, lo, hi, mid, half):
+                  up_msg, down_msg, wide, lo, hi, mid, half):
     n = low.shape[1]
     t = n // 3
 
     def go(low_src, up_src, upper_in, upper_half):
-        unpack(lo, low_src)
-        unpack(hi, up_src)
-        mid_packed = far if not upper_half else down_msg
+        own = block_parts(t, inv, low, up)
+        outer = source_parts(t, n, upper_in)
+        ends = (lo, hi, mid, half)
+        if upper_half:
+            upper_steps(t, n, low_src, up_src, outer, own, wide, 2 * t + n, wide, up_msg, ends)
+            up_msg[2 * t + n :, :] = up_src[: 2 * t, :]
+        else:
+            lower_steps(t, n, low_src, up_src, outer, own, up_msg, 2 * t + n, down_msg, up_msg, ends)
+
+    row = lax.rem(place[0], 32)
+
+    @pl.when(row == 20)
+    def _():
+        go(early_r, early_l, early_in, False)
+
+    @pl.when(row == 4)
+    def _():
+        go(late_r, late_l, late_in, False)
+
+    @pl.when(row == 12)
+    def _():
+        go(early_r, early_l, early_in, True)
+
+    @pl.when(row == 28)
+    def _():
+        go(late_r, late_l, late_in, True)
+
+
+def middle_kernel(place, inv, low, up, four_r, four_l, upper_e, upper_l, d_in, d_msg, above, lo, hi, mid, half):
+    n = low.shape[1]
+    t = n // 3
+
+    def go(upper_in):
+        upper_steps(
+            t, n, four_r, four_l, block_parts(t, inv, low, up), source_parts(t, n, upper_in),
+            d_msg, 0, above, None, (lo, hi, mid, half),
+        )
+
+    @pl.when(lax.rem(place[0], 32) == 8)
+    def _():
+        go(upper_e)
+
+    @pl.when(lax.rem(place[0], 32) == 24)
+    def _():
+        go(upper_l)
+
+
+def fine_steps(t, n, first_in, own, other, lo, hi, mid, half):
+    def go(low_src, up_src, coup, holds, second, odd, low_row=0, up_row=0):
+        unpack(lo, low_src, low_row)
+        unpack(hi, up_src, up_row)
+        mid_packed = other if not odd else own
+        mid_row = 2 * t if not odd else 0
 
         def keep(v):
             half[...] = v
@@ -122,89 +227,10 @@
             pass
 
         def out_mid(pr, pc, width, v):
-            mid_packed[pr : pr + t, pc : pc + width] = v
+            mid_packed[mid_row + pr : mid_row + pr + t, pc : pc + width] = v
 
         eliminate(
-            t, *source_parts(t, n, upper_in), lo, hi, low_src[2 * t :, :], True,
-            drop if upper_half else keep, keep if upper_half else drop, out_mid,
-        )
-        unpack(mid, mid_packed)
-
-        def out_down(v):
-            down_msg[2 * t :, :] = v
-
-        def out_up(v):
-            up_msg[2 * t :, :] = v
-
-        def out_diag(pr, pc, width, v):
-            up_msg[pr : pr + t, pc : pc + width] = v
-            down_msg[pr : pr + t, pc : pc + width] = v
-
-        eliminate(
-            t, *block_parts(t, inv, low, up), mid if upper_half else lo, hi if upper_half else mid,
-            half[...], upper_half, out_down, out_up, out_diag,
-        )
-        if upper_half:
-            far[...] = up_src[...]
-
-    row = lax.rem(place[0], 32)
-
-    @pl.when(row == 20)
-    def _():
-        go(early_r, early_l, early_in, False)
-
-    @pl.when(row == 4)
-    def _():
-        go(late_r, late_l, late_in, False)
-
-    @pl.when(row == 12)
-    def _():
-        go(early_r, early_l, early_in, True)
-
-    @pl.when(row == 28)
-    def _():
-        go(late_r, late_l, late_in, True)
-
-
-def middle_kernel(place, inv, low, up, four_r, four_l, d_in, d_msg, lo, hi):
-    n = low.shape[1]
-    t = n // 3
-    r, _, _ = roles(place)
-
-    @pl.when(r == 8)
-    def _():
-        unpack(lo, four_r)
-        unpack(hi, four_l)
-
-        def drop(v):
-            pass
-
-        def out_diag(pr, pc, width, v):
-            d_msg[pr : pr + t, pc : pc + width] = v
-
-        eliminate(
-            t, *block_parts(t, inv, low, up), lo, hi, four_r[2 * t :, :], True, drop, drop, out_diag
-        )
-
-
-def fine_steps(t, n, first_in, own, other, lo, hi, mid, half):
-    def go(low_src, up_src, coup, holds, second, odd):
-        unpack(lo, low_src)
-        unpack(hi, up_src)
-        mid_packed = other if not odd else own
-        mid_row = 2 * t if not odd else 0
-
-        def keep(v):
-            half[...] = v
-
-        def drop(v):
-            pass
-
-        def out_mid(pr, pc, width, v):
-            mid_packed[mid_row + pr : mid_row + pr + t, pc : pc + width] = v
-
-        eliminate(
-            t, *source_parts(t, n, second), lo, hi, coup[2 * t :, :], holds,
+            t, *source_parts(t, n, second), lo, hi, coup[2 * t : 2 * t + n, :], holds,
             drop if odd else keep, keep if odd else drop, out_mid,
         )
         unpack(mid, mid_packed, mid_row)
@@ -224,45 +250,49 @@
             out_down, out_up, out_diag,
         )
         if odd:
-            other[2 * t : 4 * t, :] = up_src[: 2 * t, :]
+            other[2 * t : 4 * t, :] = up_src[up_row : up_row + 2 * t, :]
         else:
             own[: 2 * t, :] = low_src[: 2 * t, :]
 
     return go
 
 
-def even_kernel(place, near_a, near_b, first_in, up_msg, d_msg, far, y_two, own, other, lo, hi, mid, half):
+def even_kernel(place, near_a, near_b, first_in, up_msg, d_msg, y_two, above, own, other, lo, hi, mid, half):
     n = up_msg.shape[1]
     t = n // 3
     r, _, _ = roles(place)
     go = fine_steps(t, n, first_in, own, other, lo, hi, mid, half)
 
-    @pl.when(jnp.logical_or(r == 0, r == 8))
+    @pl.when(r == 0)
     def _():
         go(d_msg, y_two, y_two, False, near_a, False)
 
-    @pl.when(r == 4)
-    def _():
-        go(up_msg, far, up_msg, True, near_b, False)
-
-    @pl.when(r == 12)
-    def _():
-        go(up_msg, far, up_msg, True, near_a, False)
-
-
-def odd_kernel(place, own_in, first_in, y_one, y_low, n_low, n_up, own_0, other_0, own, other, lo, hi, mid, half):
+    @pl.when(r == 8)
+    def _():
+        go(d_msg, above, above, False, near_a, False)
+
+    @pl.when(jnp.logical_or(r == 4, r == 12))
+    def _():
+        go(up_msg, up_msg, up_msg, True, near_b, False, 0, 2 * t + n)
+
+
+def odd_kernel(place, own_in, first_in, y_one, y_up, y_low, n_low, own_0, other_0, own, other, lo, hi, mid, half):
     n = own_in.shape[1]
     t = n // 3
     r, _, _ = roles(place)
     go = fine_steps(t, n, first_in, own, other, lo, hi, mid, half)
 
-    @pl.when(jnp.logical_or(r == 2, r == 10))
+    @pl.when(r == 2)
     def _():
         go(n_low, y_one, y_one, False, own_in, True)
 
+    @pl.when(r == 10)
+    def _():
+        go(y_up, y_up, y_up, False, own_in, True, 2 * t + n, 0)
+
     @pl.when(jnp.logical_or(r == 6, r == 14))
     def _():
-        go(y_low, n_up, y_low, True, own_in, True)
+        go(y_low, y_low, y_low, True, own_in, True, 0, 2 * t + n)
 
 
 def interior_kernel(place, inv, low, up, own, other, out_diag, out_below, here, above, p_buf, q_buf, d_buf, sems):
@@ -368,36 +398,38 @@
     late_l = moved(d_msg, (32, 16, -12), (32, 0, -4))
     early_in = moved(in_msg, (32, 24, -4), (32, 8, 4))
     early_l = moved(d_msg, (32, 0, -12), (32, 16, -4))
-    near_a = moved(in_msg, (16, 2, -2), (16, 10, -2), (16, 14, -2))
-    near_b = moved(in_msg, (16, 6, -2))
+    near_a = moved(in_msg, (8, 2, -2))
+    near_b = moved(in_msg, (8, 6, -2))
     first_in = moved(in_msg, (2, 1, -1))
     four_r = moved(up_msg, (16, 0, 8))
     four_l = moved(d_msg, (16, 0, -8))
+    n_low = moved(d_msg, (16, 0, 2))
     separators = (separator_inverse, separator_lower, separator_upper)
-    up_three, down_msg, far = pl.pallas_call(
+    upper_e = moved(in_msg, (32, 12, -4))
+    upper_l = moved(in_msg, (32, 28, -4))
+    up_three, down_msg, wide = pl.pallas_call(
         coarse_kernel,
-        out_shape=(message, message, diagonal),
+        out_shape=(both, message, both),
         in_specs=[smem] + [vmem] * 9,
         out_specs=(vmem,) * 3,
         scratch_shapes=[block] * 4,
         compiler_params=params,
         name="coarse",
     )(place, *separators, *near(early_r, late_r, early_l, late_l, early_in, late_in))
-    y_two = moved(down_msg, (8, 4, -4))
-    y_one = moved(down_msg, (8, 4, -2))
+    y_two = moved(down_msg, (16, 4, -4))
+    y_up = moved(wide, (16, 12, -2))
+    y_one = moved(down_msg, (16, 4, -2))
     y_low = moved(up_three, (8, 4, 2))
-    d_msg = pl.pallas_call(
+    d_msg, above = pl.pallas_call(
         middle_kernel,
-        out_shape=diagonal,
-        in_specs=[smem] + [vmem] * 6,
-        out_specs=vmem,
-        scratch_shapes=[block] * 2,
-        input_output_aliases={6: 0},
+        out_shape=(diagonal, message),
+        in_specs=[smem] + [vmem] * 8,
+        out_specs=(vmem,) * 2,
+        scratch_shapes=[block] * 4,
+        input_output_aliases={8: 0},
         compiler_params=params,
         name="middle",
-    )(place, *separators, *near(four_r, four_l, d_msg))
-    n_low = moved(d_msg, (8, 0, 2))
-    n_up = moved(d_msg, (8, 0, -2))
+    )(place, *separators, *near(four_r, four_l, upper_e, upper_l, d_msg))
     own, other = pl.pallas_call(
         even_kernel,
         out_shape=(both, both),
@@ -406,7 +438,7 @@
         scratch_shapes=[block] * 4,
         compiler_params=params,
         name="even",
-    )(place, *near(near_a, near_b, first_in, up_three, d_msg, far, y_two))
+    )(place, *near(near_a, near_b, first_in, up_three, d_msg, y_two, above))
     own, other = pl.pallas_call(
         odd_kernel,
         out_shape=(both, both),
@@ -416,7 +448,7 @@
         input_output_aliases={7: 0, 8: 1},
         compiler_params=params,
         name="odd",
-    )(place, *near(in_msg, first_in, y_one, y_low, n_low, n_up, own, other))
+    )(place, *near(in_msg, first_in, y_one, y_up, y_low, n_low, own, other))
     other = moved(other, (2, 0, 1))
     pair = jax.ShapeDtypeStruct((2, n, n), BF)
     return pl.pallas_call(

time: 64 us -> 72.6 us (1.13)
  the two profiles are of different devices: /device:TPU:33 before, /device:TPU:1 now
where the time goes in v5:
time: 72.6 us; the launch traced here: 72.2 us
  starting transfers between devices  45.1 us (62%)
  waiting for transfers between devices  22 us (30%)
  Pallas kernels  3.91 us (5%)
  between operations  1.22 us (2%)
    ppermute x19, starting transfers between devices, moved(): return lax.ppermute(value, 'tm', pairs)  45.1 us
    ppermute x19, waiting for transfers between devices, moved(): return lax.ppermute(value, 'tm', pairs)  22 us
    pallas_call x1, Pallas kernels, on_device(): pl.pallas_call(interior_kernel, out_shape=(pair, pair), in_specs=[smem] +...  2.1 us
  transfers between devices with their start and end apart: 19, of which 1 were waited for; matrix products, arithmetic and copies ran while one was open for 0% of the time, Pallas kernels for 0%

profile of v5, /device:TPU:1, one launch (start us, length us, event | category | flops | bytes accessed | tf_op | source)
XLA Modules:
  0.0 72.2 jit_solution(14675690856681433062)
XLA Ops:
  0.7 1.3 %pack.1 = (bf16[640,384]{1,0:T(8,128)(2,1)S(1)}, bf16[256,384]{1,0:T(8,128)(2,1)S(1)}, bf16[1024,384]{1,0:T(8,128)(2,1)S(1)}) custom-call(s32[1]{0:T(128)} %bitcast.place, bf16[1,384,384]{2,1,0:T(8,128)(2,1)} %inv.6, bf16[1,384,384]{2,1,0:T(8,128)(2,1)} %low.6, bf16[1,384,384]{2,1,0:T(8,128)(2,1)} %up.6, bf16[1,384,384]{2,1,0:T(8,128)(2,1)} %top.1, ...), custom_call_target="tpu_custom_call" | custom-call | tf_op jit(solution)/shard_map/pack/pallas_call | solution.py:380
  2.0 0.7 collective-permute-start.10
  2.7 0.7 collective-permute-start.5
  3.4 0.7 collective-permute-start.14
  4.1 0.7 collective-permute-start.3
  4.7 0.7 collective-permute-start.13
  5.5 0.7 collective-permute-start.1
  6.2 0.7 collective-permute-start.4
  6.9 0.7 collective-permute-start.2
  7.6 0.7 collective-permute-start.6
  8.3 0.7 collective-permute-start.15
  9.0 0.7 collective-permute-start.16
  9.8 32.0 %collective-permute-start = (bf16[1024,384]{1,0:T(8,128)(2,1)S(1)}, bf16[1024,384]{1,0:T(8,128)(2,1)S(1)}, u32[]{:S(2)}, u32[]{:S(2)}) collective-permute-start(bf16[1024,384]{1,0:T(8,128)(2,1)S(1)} %get-tuple-element.14.own_in), channel_id=1, source_target_pairs={{484,480},{492,488},{500,496},{508,504},{4,0},{12,8},{20,16},{28,2... | collective-permute-start | bytes 2359304 | tf_op jit(solution)/shard_map/ppermute | solution.py:365
  41.7 0.7 collective-permute-start.11
  42.5 0.7 collective-permute-start.12
  43.3 0.7 collective-permute-start.8
  44.0 0.7 collective-permute-start.9
  44.7 0.7 collective-permute-start.17
  45.4 0.7 collective-permute-start.7
  46.1 0.2 middle.1
  46.4 0.2 odd.1
  46.7 1.3 %collective-permute-start.18 = (bf16[896,384]{1,0:T(8,128)(2,1)S(1)}, bf16[896,384]{1,0:T(8,128)(2,1)S(1)}, u32[]{:S(2)}, u32[]{:S(2)}) collective-permute-start(bf16[896,384]{1,0:T(8,128)(2,1)S(1)} %get-tuple-element.25), channel_id=1, source_target_pairs={{480,484},{488,492},{496,500},{504,508},{0,4},{8,12},{16,20},{24,2... | collective-permute-start | bytes 2064392 | tf_op jit(solution)/shard_map/ppermute | solution.py:365
  48.0 21.9 %collective-permute-done.18.other = bf16[896,384]{1,0:T(8,128)(2,1)S(1)} collective-permute-done((bf16[896,384]{1,0:T(8,128)(2,1)S(1)}, bf16[896,384]{1,0:T(8,128)(2,1)S(1)}, u32[]{:S(2)}, u32[]{:S(2)}) %collective-permute-start.18) | collective-permute-done | bytes 688160 | tf_op jit(solution)/shard_map/ppermute | solution.py:365
  69.9 2.1 %interior.1 = (bf16[2,384,384]{2,1,0:T(8,128)(2,1)}, bf16[2,384,384]{2,1,0:T(8,128)(2,1)}) custom-call(s32[1]{0:T(128)} %bitcast.place, bf16[1,384,384]{2,1,0:T(8,128)(2,1)S(1)} %copy-done.3, bf16[1,384,384]{2,1,0:T(8,128)(2,1)S(1)} %copy-done.4, bf16[1,384,384]{2,1,0:T(8,128)(2,1)S(1)} %copy-done.5, bf16[896,384]{1,0:T(8,128)(2,1)S(1)} %get-tuple-element.24.own, ...), custom_call_target="tpu_custom_call" | custom-call | tf_op jit(solution)/shard_map/interior/pallas_call | solution.py:454
  (32 shorter events, 0.1 us)
Async XLA Ops:
  0.6 42.5 %copy-start = (bf16[1,384,384]{2,1,0:T(8,128)(2,1)S(1)}, bf16[1,384,384]{2,1,0:T(8,128)(2,1)}, u32[]{:S(2)}) copy-start(bf16[1,384,384]{2,1,0:T(8,128)(2,1)} %inv.6) | copy-start | bytes 884740
  0.6 42.5 %copy-start.1 = (bf16[1,384,384]{2,1,0:T(8,128)(2,1)S(1)}, bf16[1,384,384]{2,1,0:T(8,128)(2,1)}, u32[]{:S(2)}) copy-start(bf16[1,384,384]{2,1,0:T(8,128)(2,1)} %low.6) | copy-start | bytes 884740
  0.7 42.5 %copy-start.2 = (bf16[1,384,384]{2,1,0:T(8,128)(2,1)S(1)}, bf16[1,384,384]{2,1,0:T(8,128)(2,1)}, u32[]{:S(2)}) copy-start(bf16[1,384,384]{2,1,0:T(8,128)(2,1)} %up.6) | copy-start | bytes 884740
  2.0 3.5 %collective-permute-start.10 = (bf16[256,384]{1,0:T(8,128)(2,1)S(1)}, bf16[256,384]{1,0:T(8,128)(2,1)S(1)}, u32[]{:S(2)}, u32[]{:S(2)}) collective-permute-start(bf16[256,384]{1,0:T(8,128)(2,1)S(1)} %get-tuple-element.16.d_in), channel_id=1, source_target_pairs={{480,488},{32,40},{96,104},{160,168},{224,232},{288,296},{352,360}... | collective-permute-start | bytes 589832 | tf_op jit(solution)/shard_map/ppermute | solution.py:365
  2.7 39.1 %collective-permute-start.5 = (bf16[1024,384]{1,0:T(8,128)(2,1)S(1)}, bf16[1024,384]{1,0:T(8,128)(2,1)S(1)}, u32[]{:S(2)}, u32[]{:S(2)}) collective-permute-start(bf16[1024,384]{1,0:T(8,128)(2,1)S(1)} %get-tuple-element.14.own_in), channel_id=1, source_target_pairs={{0,16},{64,48},{128,144},{192,176},{256,272},{320,304},{384,400},{... | collective-permute-start | bytes 2359304 | tf_op jit(solution)/shard_map/ppermute | solution.py:365
  3.4 2.8 %collective-permute-start.14 = (bf16[256,384]{1,0:T(8,128)(2,1)S(1)}, bf16[256,384]{1,0:T(8,128)(2,1)S(1)}, u32[]{:S(2)}, u32[]{:S(2)}) collective-permute-start(bf16[256,384]{1,0:T(8,128)(2,1)S(1)} %get-tuple-element.16.d_in), channel_id=1, source_target_pairs={{480,448},{32,0},{96,64},{160,128},{224,192},{288,256},{352,320},{... | collective-permute-start | bytes 589832 | tf_op jit(solution)/shard_map/ppermute | solution.py:365
  4.1 2.8 %collective-permute-start.3 = (bf16[256,384]{1,0:T(8,128)(2,1)S(1)}, bf16[256,384]{1,0:T(8,128)(2,1)S(1)}, u32[]{:S(2)}, u32[]{:S(2)}) collective-permute-start(bf16[256,384]{1,0:T(8,128)(2,1)S(1)} %get-tuple-element.16.d_in), channel_id=1, source_target_pairs={{480,432},{32,16},{96,48},{160,144},{224,176},{288,272},{352,304},... | collective-permute-start | bytes 589832 | tf_op jit(solution)/shard_map/ppermute | solution.py:365
  4.7 3.5 %collective-permute-start.13 = (bf16[640,384]{1,0:T(8,128)(2,1)S(1)}, bf16[640,384]{1,0:T(8,128)(2,1)S(1)}, u32[]{:S(2)}, u32[]{:S(2)}) collective-permute-start(bf16[640,384]{1,0:T(8,128)(2,1)S(1)} %get-tuple-element.15), channel_id=1, source_target_pairs={{480,0},{32,64},{96,128},{160,192},{224,256},{288,320},{352,384},{... | collective-permute-start | bytes 1474568 | tf_op jit(solution)/shard_map/ppermute | solution.py:365
  5.5 3.6 %collective-permute-start.1 = (bf16[640,384]{1,0:T(8,128)(2,1)S(1)}, bf16[640,384]{1,0:T(8,128)(2,1)S(1)}, u32[]{:S(2)}, u32[]{:S(2)}) collective-permute-start(bf16[640,384]{1,0:T(8,128)(2,1)S(1)} %get-tuple-element.15), channel_id=1, source_target_pairs={{480,16},{32,48},{96,144},{160,176},{224,272},{288,304},{352,400},... | collective-permute-start | bytes 1474568 | tf_op jit(solution)/shard_map/ppermute | solution.py:365
  6.2 1.4 %collective-permute-start.4 = (bf16[256,384]{1,0:T(8,128)(2,1)S(1)}, bf16[256,384]{1,0:T(8,128)(2,1)S(1)}, u32[]{:S(2)}, u32[]{:S(2)}) collective-permute-start(bf16[256,384]{1,0:T(8,128)(2,1)S(1)} %get-tuple-element.16.d_in), channel_id=1, source_target_pairs={{480,464},{32,496},{96,80},{160,112},{224,208},{288,240},{352,336}... | collective-permute-start | bytes 589832 | tf_op jit(solution)/shard_map/ppermute | solution.py:365
  6.9 2.9 %collective-permute-start.2 = (bf16[640,384]{1,0:T(8,128)(2,1)S(1)}, bf16[640,384]{1,0:T(8,128)(2,1)S(1)}, u32[]{:S(2)}, u32[]{:S(2)}) collective-permute-start(bf16[640,384]{1,0:T(8,128)(2,1)S(1)} %get-tuple-element.15), channel_id=1, source_target_pairs={{480,496},{32,80},{96,112},{160,208},{224,240},{288,336},{352,368}... | collective-permute-start | bytes 1474568 | tf_op jit(solution)/shard_map/ppermute | solution.py:365
  7.6 34.9 %collective-permute-start.6 = (bf16[1024,384]{1,0:T(8,128)(2,1)S(1)}, bf16[1024,384]{1,0:T(8,128)(2,1)S(1)}, u32[]{:S(2)}, u32[]{:S(2)}) collective-permute-start(bf16[1024,384]{1,0:T(8,128)(2,1)S(1)} %get-tuple-element.14.own_in), channel_id=1, source_target_pairs={{0,496},{64,80},{128,112},{192,208},{256,240},{320,336},{384,368},... | collective-permute-start | bytes 2359304 | tf_op jit(solution)/shard_map/ppermute | solution.py:365
  8.3 35.0 %collective-permute-start.15 = (bf16[1024,384]{1,0:T(8,128)(2,1)S(1)}, bf16[1024,384]{1,0:T(8,128)(2,1)S(1)}, u32[]{:S(2)}, u32[]{:S(2)}) collective-permute-start(bf16[1024,384]{1,0:T(8,128)(2,1)S(1)} %get-tuple-element.14.own_in), channel_id=1, source_target_pairs={{16,0},{144,128},{272,256},{400,384},{17,1},{145,129},{273,257},{4... | collective-permute-start | bytes 2359304 | tf_op jit(solution)/shard_map/ppermute | solution.py:365
  9.0 34.9 %collective-permute-start.16 = (bf16[1024,384]{1,0:T(8,128)(2,1)S(1)}, bf16[1024,384]{1,0:T(8,128)(2,1)S(1)}, u32[]{:S(2)}, u32[]{:S(2)}) collective-permute-start(bf16[1024,384]{1,0:T(8,128)(2,1)S(1)} %get-tuple-element.14.own_in), channel_id=1, source_target_pairs={{80,64},{208,192},{336,320},{464,448},{81,65},{209,193},{337,321},... | collective-permute-start | bytes 2359304 | tf_op jit(solution)/shard_map/ppermute | solution.py:365
  9.8 34.9 %collective-permute-start = (bf16[1024,384]{1,0:T(8,128)(2,1)S(1)}, bf16[1024,384]{1,0:T(8,128)(2,1)S(1)}, u32[]{:S(2)}, u32[]{:S(2)}) collective-permute-start(bf16[1024,384]{1,0:T(8,128)(2,1)S(1)} %get-tuple-element.14.own_in), channel_id=1, source_target_pairs={{484,480},{492,488},{500,496},{508,504},{4,0},{12,8},{20,16},{28,2... | collective-permute-start | bytes 2359304 | tf_op jit(solution)/shard_map/ppermute | solution.py:365
  41.7 3.7 %collective-permute-start.11 = (bf16[1024,384]{1,0:T(8,128)(2,1)S(1)}, bf16[1024,384]{1,0:T(8,128)(2,1)S(1)}, u32[]{:S(2)}, u32[]{:S(2)}) collective-permute-start(bf16[1024,384]{1,0:T(8,128)(2,1)S(1)} %get-tuple-element.14.own_in), channel_id=1, source_target_pairs={{488,480},{8,0},{40,32},{72,64},{104,96},{136,128},{168,160},{200,... | collective-permute-start | bytes 2359304 | tf_op jit(solution)/shard_map/ppermute | solution.py:365
  42.5 3.9 %collective-permute-start.12 = (bf16[1024,384]{1,0:T(8,128)(2,1)S(1)}, bf16[1024,384]{1,0:T(8,128)(2,1)S(1)}, u32[]{:S(2)}, u32[]{:S(2)}) collective-permute-start(bf16[1024,384]{1,0:T(8,128)(2,1)S(1)} %get-tuple-element.14.own_in), channel_id=1, source_target_pairs={{504,496},{24,16},{56,48},{88,80},{120,112},{152,144},{184,176},{2... | collective-permute-start | bytes 2359304 | tf_op jit(solution)/shard_map/ppermute | solution.py:365
  43.3 3.1 %collective-permute-start.8 = (bf16[896,384]{1,0:T(8,128)(2,1)S(1)}, bf16[896,384]{1,0:T(8,128)(2,1)S(1)}, u32[]{:S(2)}, u32[]{:S(2)}) collective-permute-start(bf16[896,384]{1,0:T(8,128)(2,1)S(1)} %get-tuple-element.18), channel_id=1, source_target_pairs={{16,8},{80,72},{144,136},{208,200},{272,264},{336,328},{400,392},{... | collective-permute-start | bytes 2064392 | tf_op jit(solution)/shard_map/ppermute | solution.py:365
  44.0 2.4 %collective-permute-start.9 = (bf16[896,384]{1,0:T(8,128)(2,1)S(1)}, bf16[896,384]{1,0:T(8,128)(2,1)S(1)}, u32[]{:S(2)}, u32[]{:S(2)}) collective-permute-start(bf16[896,384]{1,0:T(8,128)(2,1)S(1)} %get-tuple-element.19.up_msg), channel_id=1, source_target_pairs={{496,504},{16,24},{48,56},{80,88},{112,120},{144,152},{176,184},{2... | collective-permute-start | bytes 2064392 | tf_op jit(solution)/shard_map/ppermute | solution.py:365
  44.7 1.6 %collective-permute-start.17 = (bf16[640,384]{1,0:T(8,128)(2,1)S(1)}, bf16[640,384]{1,0:T(8,128)(2,1)S(1)}, u32[]{:S(2)}, u32[]{:S(2)}) collective-permute-start(bf16[640,384]{1,0:T(8,128)(2,1)S(1)} %get-tuple-element.17), channel_id=1, source_target_pairs={{496,480},{48,32},{112,96},{176,160},{240,224},{304,288},{368,352}... | collective-permute-start | bytes 1474568 | tf_op jit(solution)/shard_map/ppermute | solution.py:365
  45.4 1.0 %collective-permute-start.7 = (bf16[640,384]{1,0:T(8,128)(2,1)S(1)}, bf16[640,384]{1,0:T(8,128)(2,1)S(1)}, u32[]{:S(2)}, u32[]{:S(2)}) collective-permute-start(bf16[640,384]{1,0:T(8,128)(2,1)S(1)} %get-tuple-element.17), channel_id=1, source_target_pairs={{496,488},{48,40},{112,104},{176,168},{240,232},{304,296},{368,360... | collective-permute-start | bytes 1474568 | tf_op jit(solution)/shard_map/ppermute | solution.py:365
  46.4 23.5 %copy-start.3 = (bf16[1,384,384]{2,1,0:T(8,128)(2,1)S(1)}, bf16[1,384,384]{2,1,0:T(8,128)(2,1)}, u32[]{:S(2)}) copy-start(bf16[1,384,384]{2,1,0:T(8,128)(2,1)} %inv.7) | copy-start | bytes 884740
  46.4 23.5 %copy-start.4 = (bf16[1,384,384]{2,1,0:T(8,128)(2,1)S(1)}, bf16[1,384,384]{2,1,0:T(8,128)(2,1)}, u32[]{:S(2)}) copy-start(bf16[1,384,384]{2,1,0:T(8,128)(2,1)} %low.7) | copy-start | bytes 884740
  46.7 23.2 %collective-permute-start.18 = (bf16[896,384]{1,0:T(8,128)(2,1)S(1)}, bf16[896,384]{1,0:T(8,128)(2,1)S(1)}, u32[]{:S(2)}, u32[]{:S(2)}) collective-permute-start(bf16[896,384]{1,0:T(8,128)(2,1)S(1)} %get-tuple-element.25), channel_id=1, source_target_pairs={{480,484},{488,492},{496,500},{504,508},{0,4},{8,12},{16,20},{24,2... | collective-permute-start | bytes 2064392 | tf_op jit(solution)/shard_map/ppermute | solution.py:365
  (1 other events, 23.5 us)

commit v6 on v5

v6 whole, which is shorter than its diff:
```python
import jax
import jax.numpy as jnp
from jax import lax
from jax.experimental import pallas as pl
from jax.experimental.pallas import tpu as pltpu
from jax.sharding import PartitionSpec as P


BF = jnp.bfloat16
F32 = jnp.float32
NT = (((1,), (1,)), ((), ()))


def mm(left_op, right_op):
    return jnp.dot(left_op, right_op, preferred_element_type=F32)


def mt(left_op, right_op):
    return lax.dot_general(left_op, right_op, NT, preferred_element_type=F32)


def packed_parts(t):
    return (
        ((0, 0), (0, 0), 3 * t),
        ((t, 0), (t, t), 2 * t),
        ((t, 2 * t), (2 * t, 2 * t), t),
    )


def unpack(w, src, base=0, at=0):
    t = src.shape[1] // 3
    for (pr, pc), (fr, fc), width in packed_parts(t):
        part = src[base + pr : base + pr + t, pc : pc + width]
        w[at + fr : at + fr + t, at + fc : at + fc + width] = part
    w[at + t : at + 2 * t, at : at + t] = src[base : base + t, t : 2 * t].T
    w[at + 2 * t : at + 3 * t, at : at + t] = src[base : base + t, 2 * t :].T
    w[at + 2 * t : at + 3 * t, at + t : at + 2 * t] = src[base + t : base + 2 * t, t : 2 * t].T


def couple(w, coup, holds):
    n = coup.shape[1]
    if holds:
        w[:n, n:] = coup
        w[n:, :n] = coup.T
    else:
        w[n:, :n] = coup
        w[:n, n:] = coup.T


def eliminate(t, inv, low, up, w, out_down, out_up, out_diag):
    n = 3 * t
    pair = jnp.concatenate([low, up], axis=1)
    both = mm(pair, w[...]).astype(BF)
    out_down(both[:, :n])
    out_up(both[:, n:])
    for (pr, pc), (fr, fc), width in packed_parts(t):
        part = inv(pr, pc, fr, fc, width).astype(F32)
        part = part + mt(both[fr : fr + t], pair[fc : fc + width])
        out_diag(pr, pc, width, part.astype(BF))


def roles(place):
    j = place[0]
    r = lax.rem(j, 16)
    return r, lax.rem(j, 2), lax.div(r, 2)


def pack_kernel(place, inv, low, up, top, coup, up_msg, d_msg, in_msg, sems):
    n = low.shape[1]
    t = n // 3
    r, core, chip = roles(place)

    def run(copies):
        for i, (src, dst) in enumerate(copies):
            pltpu.make_async_copy(src, dst, sems.at[i]).start()
        for i, (src, dst) in enumerate(copies):
            pltpu.make_async_copy(src, dst, sems.at[i]).wait()

    def diag_copies(src, dst):
        return [
            (src.at[0, fr : fr + t, fc : fc + width], dst.at[pr : pr + t, pc : pc + width])
            for (pr, pc), (fr, fc), width in packed_parts(t)
        ]

    @pl.when(r == 0)
    def _():
        copies = [(coup.at[0], up_msg.at[2 * t :, :])]
        for dst in (up_msg, d_msg):
            copies += diag_copies(top, dst)
        run(copies)

    @pl.when(jnp.logical_or(jnp.logical_or(core == 1, lax.rem(chip, 2) == 1), jnp.logical_or(r == 8, lax.rem(place[0], 32) == 12)))
    def _():
        copies = diag_copies(inv, in_msg)
        copies.append((low.at[0], in_msg.at[2 * t : 2 * t + n, :]))
        copies.append((up.at[0], in_msg.at[2 * t + n :, :]))
        run(copies)


def source_parts(t, n, src):
    return (
        lambda pr, pc, fr, fc, w: src[pr : pr + t, pc : pc + w],
        src[2 * t : 2 * t + n, :],
        src[2 * t + n :, :],
    )


def block_parts(t, inv, low, up):
    return (lambda pr, pc, fr, fc, w: inv[0, fr : fr + t, fc : fc + w], low[0], up[0])


def message_writers(t, n, *messages):
    def out_coup(v):
        messages[0][2 * t : 2 * t + n, :] = v

    def out_diag(pr, pc, width, v):
        for dst in messages:
            dst[pr : pr + t, pc : pc + width] = v

    return out_coup, out_diag


def drop(*_):
    pass


def outer_level(t, n, low_src, up_src, outer, mid_dst, mid_row, w, upper):
    unpack(w, low_src)
    unpack(w, up_src, 0, n)
    couple(w, low_src[2 * t : 2 * t + n, :], True)

    def keep(v):
        couple(w, v, upper)

    def out_mid(pr, pc, width, v):
        mid_dst[mid_row + pr : mid_row + pr + t, pc : pc + width] = v

    eliminate(t, *outer, w, drop if upper else keep, keep if upper else drop, out_mid)
    unpack(w, mid_dst, mid_row, 0 if upper else n)


def lower_steps(t, n, low_src, up_src, outer, own, mid_dst, mid_row, down_msg, up_msg, w):
    outer_level(t, n, low_src, up_src, outer, mid_dst, mid_row, w, False)
    out_down, _ = message_writers(t, n, down_msg)
    out_up, _ = message_writers(t, n, up_msg)
    _, out_diag = message_writers(t, n, up_msg, down_msg)
    eliminate(t, *own, w, out_down, out_up, out_diag)


def upper_steps(t, n, low_src, up_src, outer, own, mid_dst, mid_row, down_msg, up_msg, w):
    outer_level(t, n, low_src, up_src, outer, mid_dst, mid_row, w, True)
    out_down, _ = message_writers(t, n, down_msg)
    if up_msg is None:
        out_up = drop
        _, out_diag = message_writers(t, n, down_msg)
    else:
        out_up, _ = message_writers(t, n, up_msg)
        _, out_diag = message_writers(t, n, up_msg, down_msg)
    eliminate(t, *own, w, out_down, out_up, out_diag)


def coarse_kernel(place, inv, low, up, early_r, late_r, early_l, late_l, early_in, late_in,
                  near_msg, far_msg, w):
    n = low.shape[1]
    t = n // 3

    def go(low_src, up_src, upper_in, upper_half):
        own = block_parts(t, inv, low, up)
        outer = source_parts(t, n, upper_in)
        if upper_half:
            upper_steps(t, n, low_src, up_src, outer, own, far_msg, 2 * t + n, far_msg, near_msg, w)
        else:
            lower_steps(t, n, low_src, up_src, outer, own, far_msg, 2 * t + n, near_msg, far_msg, w)

    row = lax.rem(place[0], 32)

    @pl.when(row == 20)
    def _():
        go(early_r, early_l, early_in, False)

    @pl.when(row == 4)
    def _():
        go(late_r, late_l, late_in, False)

    @pl.when(row == 12)
    def _():
        go(early_r, early_l, early_in, True)

    @pl.when(row == 28)
    def _():
        go(late_r, late_l, late_in, True)


def middle_kernel(place, inv, low, up, four_r, four_l, upper_e, upper_l, d_in, d_msg, above, w):
    n = low.shape[1]
    t = n // 3

    def go(upper_in):
        upper_steps(
            t, n, four_r, four_l, block_parts(t, inv, low, up), source_parts(t, n, upper_in),
            d_msg, 0, above, None, w,
        )

    @pl.when(lax.rem(place[0], 32) == 8)
    def _():
        go(upper_e)

    @pl.when(lax.rem(place[0], 32) == 24)
    def _():
        go(upper_l)


def inputs_kernel(place, inv, low, up, late_msg, sems):
    n = low.shape[1]
    t = n // 3

    @pl.when(lax.rem(place[0], 32) == 28)
    def _():
        copies = [
            (inv.at[0, fr : fr + t, fc : fc + width], late_msg.at[pr : pr + t, pc : pc + width])
            for (pr, pc), (fr, fc), width in packed_parts(t)
        ]
        copies.append((low.at[0], late_msg.at[2 * t : 2 * t + n, :]))
        copies.append((up.at[0], late_msg.at[2 * t + n :, :]))
        for i, (src, dst) in enumerate(copies):
            pltpu.make_async_copy(src, dst, sems.at[i]).start()
        for i, (src, dst) in enumerate(copies):
            pltpu.make_async_copy(src, dst, sems.at[i]).wait()


def fine_steps(t, n, first_in, own, other, w):
    def go(low_src, up_src, coup, holds, second, odd, low_row=0, up_row=0):
        unpack(w, low_src, low_row)
        unpack(w, up_src, up_row, n)
        couple(w, coup[2 * t : 2 * t + n, :], holds)
        mid_packed = other if not odd else own
        mid_row = 2 * t if not odd else 0

        def keep(v):
            couple(w, v, odd)

        def out_mid(pr, pc, width, v):
            mid_packed[mid_row + pr : mid_row + pr + t, pc : pc + width] = v

        outer = source_parts(t, n, second)
        eliminate(t, *outer, w, drop if odd else keep, keep if odd else drop, out_mid)
        unpack(w, mid_packed, mid_row, 0 if odd else n)

        def out_down(v):
            own[4 * t :, :] = v

        def out_up(v):
            other[4 * t :, :] = v

        def out_diag(pr, pc, width, v):
            own[2 * t + pr : 3 * t + pr, pc : pc + width] = v
            other[pr : pr + t, pc : pc + width] = v

        eliminate(t, *source_parts(t, n, first_in), w, out_down, out_up, out_diag)
        if odd:
            other[2 * t : 4 * t, :] = up_src[up_row : up_row + 2 * t, :]
        else:
            own[: 2 * t, :] = low_src[: 2 * t, :]

    return go


def even_kernel(place, near_a, near_u, near_b, first_in, near_msg, far_msg, early_l, late_l, d_msg, y_two, above,
                own, other, w):
    n = near_msg.shape[1]
    t = n // 3
    r, _, _ = roles(place)
    row = lax.rem(place[0], 32)
    go = fine_steps(t, n, first_in, own, other, w)

    @pl.when(r == 0)
    def _():
        go(d_msg, y_two, y_two, False, near_a, False)

    @pl.when(r == 8)
    def _():
        go(d_msg, above, above, False, near_a, False)

    @pl.when(r == 4)
    def _():
        go(far_msg, far_msg, far_msg, True, near_b, False, 0, 2 * t + n)

    @pl.when(row == 12)
    def _():
        go(near_msg, early_l, near_msg, True, near_u, False)

    @pl.when(row == 28)
    def _():
        go(near_msg, late_l, near_msg, True, near_u, False)


def odd_kernel(place, own_in, first_in, y_mid, y_end, n_low, n_up, own_0, other_0, own, other, w):
    n = own_in.shape[1]
    t = n // 3
    r, _, _ = roles(place)
    go = fine_steps(t, n, first_in, own, other, w)

    @pl.when(r == 2)
    def _():
        go(n_low, y_end, y_end, False, own_in, True)

    @pl.when(r == 10)
    def _():
        go(y_mid, y_mid, y_mid, False, own_in, True, 2 * t + n, 0)

    @pl.when(r == 6)
    def _():
        go(y_mid, y_mid, y_mid, True, own_in, True, 0, 2 * t + n)

    @pl.when(r == 14)
    def _():
        go(y_end, n_up, y_end, True, own_in, True)


def interior_kernel(place, inv, low, up, own, other, out_diag, out_below, w, p_buf, q_buf, d_buf, sems):
    n = low.shape[1]
    t = n // 3
    _, core, _ = roles(place)
    writes = [
        pltpu.make_async_copy(w.at[:n, :n], out_diag.at[0], sems.at[0]),
        pltpu.make_async_copy(p_buf, out_below.at[0], sems.at[1]),
        pltpu.make_async_copy(q_buf, out_below.at[1], sems.at[2]),
        pltpu.make_async_copy(d_buf, out_diag.at[1], sems.at[3]),
    ]

    def go(src, holds):
        unpack(w, src)
        writes[0].start()
        unpack(w, src, 2 * t, n)
        couple(w, src[4 * t :, :], holds)
        pair = jnp.concatenate([low[0], up[0]], axis=1)
        both = mm(pair, w[...]).astype(BF)
        p_buf[...] = both[:, :n]
        writes[1].start()
        q_buf[...] = both[:, n:].T
        writes[2].start()
        d_buf[...] = (inv[0].astype(F32) + mt(both, pair)).astype(BF)
        writes[3].start()

    @pl.when(core == 0)
    def _():
        go(own, False)

    @pl.when(core == 1)
    def _():
        go(other, True)

    for write in writes:
        write.wait()


def on_device(
    separator_inverse,
    separator_lower,
    separator_upper,
    top_diagonal,
    top_coupling,
    interior_inverse,
    interior_lower,
    interior_upper,
):
    devices = lax.axis_size("tm")
    spacing = 16
    margin = spacing // 2
    n = separator_lower.shape[1]
    t = n // 3
    place = lax.rem(lax.axis_index("tm") + margin, devices).astype(jnp.int32).reshape(1)

    def moved(value, *moves):
        pairs = [
            ((p - margin) % devices, (p + step - margin) % devices)
            for p in range(devices)
            for mod, at, step in moves
            if p % mod == at
        ]
        return lax.ppermute(value, "tm", pairs)

    smem = pl.BlockSpec(memory_space=pltpu.SMEM)
    vmem = pl.BlockSpec(memory_space=pltpu.VMEM)
    anywhere = pl.BlockSpec(memory_space=pl.ANY)
    params = pltpu.CompilerParams(vmem_limit_bytes=16 << 20)
    block = pltpu.VMEM((n, n), BF)
    square = pltpu.VMEM((2 * n, 2 * n), BF)
    message = pltpu.VMEM((2 * t + n, n), BF)
    diagonal = pltpu.VMEM((2 * t, n), BF)
    inputs = pltpu.VMEM((2 * t + 2 * n, n), BF)
    both = pltpu.VMEM((4 * t + n, n), BF)

    def near(*values):
        return [pltpu.with_memory_space_constraint(v, pltpu.VMEM) for v in values]

    up_msg, d_msg, in_msg = pl.pallas_call(
        pack_kernel,
        out_shape=(message, diagonal, inputs),
        in_specs=[smem] + [anywhere] * 5,
        out_specs=(vmem,) * 3,
        scratch_shapes=[pltpu.SemaphoreType.DMA((7,))],
        compiler_params=params,
        name="pack",
    )(
        place,
        *[
            pltpu.with_memory_space_constraint(v, pltpu.HBM)
            for v in (separator_inverse, separator_lower, separator_upper, top_diagonal, top_coupling)
        ],
    )
    late_in = moved(in_msg, (32, 24, 4), (32, 8, -4))
    early_r = moved(up_msg, (32, 0, 12), (32, 16, 4))
    late_r = moved(up_msg, (32, 16, 12), (32, 0, 4))
    late_l = moved(d_msg, (32, 16, -12), (32, 0, -4))
    early_in = moved(in_msg, (32, 24, -4), (32, 8, 4))
    early_l = moved(d_msg, (32, 0, -12), (32, 16, -4))
    near_a = moved(in_msg, (8, 2, -2))
    near_u = moved(in_msg, (16, 14, -2))
    near_b = moved(in_msg, (16, 6, -2))
    first_in = moved(in_msg, (2, 1, -1))
    four_r = moved(up_msg, (16, 0, 8))
    four_l = moved(d_msg, (16, 0, -8))
    n_low = moved(d_msg, (16, 0, 2))
    separators = (separator_inverse, separator_lower, separator_upper)
    upper_e = moved(in_msg, (32, 12, -4))
    n_up = moved(d_msg, (16, 0, -2))
    late_msg = pl.pallas_call(
        inputs_kernel,
        out_shape=inputs,
        in_specs=[smem] + [anywhere] * 3,
        out_specs=vmem,
        scratch_shapes=[pltpu.SemaphoreType.DMA((5,))],
        compiler_params=params,
        name="inputs",
    )(place, *[pltpu.with_memory_space_constraint(v, pltpu.HBM) for v in separators])
    upper_l = moved(late_msg, (32, 28, -4))
    near_msg, far_msg = pl.pallas_call(
        coarse_kernel,
        out_shape=(message, both),
        in_specs=[smem] + [vmem] * 9,
        out_specs=(vmem,) * 2,
        scratch_shapes=[square],
        compiler_params=params,
        name="coarse",
    )(place, *separators, *near(early_r, late_r, early_l, late_l, early_in, late_in))
    y_two = moved(near_msg, (16, 4, -4))
    y_mid = moved(far_msg, (16, 4, 2), (16, 12, -2))
    y_end = moved(near_msg, (16, 4, -2), (16, 12, 2))
    d_msg, above = pl.pallas_call(
        middle_kernel,
        out_shape=(diagonal, message),
        in_specs=[smem] + [vmem] * 8,
        out_specs=(vmem,) * 2,
        scratch_shapes=[square],
        input_output_aliases={8: 0},
        compiler_params=params,
        name="middle",
    )(place, *separators, *near(four_r, four_l, upper_e, upper_l, d_msg))
    own, other = pl.pallas_call(
        even_kernel,
        out_shape=(both, both),
        in_specs=[smem] + [vmem] * 11,
        out_specs=(vmem,) * 2,
        scratch_shapes=[square],
        compiler_params=params,
        name="even",
    )(place, *near(near_a, near_u, near_b, first_in, near_msg, far_msg, early_l, late_l, d_msg, y_two, above))
    own, other = pl.pallas_call(
        odd_kernel,
        out_shape=(both, both),
        in_specs=[smem] + [vmem] * 8,
        out_specs=(vmem,) * 2,
        scratch_shapes=[square],
        input_output_aliases={7: 0, 8: 1},
        compiler_params=params,
        name="odd",
    )(place, *near(in_msg, first_in, y_mid, y_end, n_low, n_up, own, other))
    other = moved(other, (2, 0, 1))
    pair = jax.ShapeDtypeStruct((2, n, n), BF)
    return pl.pallas_call(
        interior_kernel,
        out_shape=(pair, pair),
        in_specs=[smem] + [vmem] * 5,
        out_specs=(anywhere,) * 2,
        scratch_shapes=[square] + [block] * 3 + [pltpu.SemaphoreType.DMA((4,))],
        compiler_params=params,
        name="interior",
    )(place, interior_inverse, interior_lower, interior_upper, *near(own, other))


def solution(mesh):
    spec = P(("rep", "tm"), None, None)

    return jax.shard_map(
        on_device, mesh=mesh, in_specs=(spec,) * 8, out_specs=(spec, spec), check_vma=False
    )
```

time: 72.6 us -> 72.1 us (level)
  the two profiles are of different devices: /device:TPU:1 before, /device:TPU:183 now
where the time goes in v6:
time: 72.1 us; the launch traced here: 71.7 us
  starting transfers between devices  38.3 us (53%)
  waiting for transfers between devices  28.4 us (39%)
  Pallas kernels  3.67 us (5%)
  between operations  1.25 us (2%)
    ppermute x20, starting transfers between devices, moved(): return lax.ppermute(value, 'tm', pairs)  38.3 us
    ppermute x20, waiting for transfers between devices, moved(): return lax.ppermute(value, 'tm', pairs)  28.4 us
    pallas_call x1, Pallas kernels, on_device(): pl.pallas_call(interior_kernel, out_shape=(pair, pair), in_specs=[smem] +...  1.84 us
  transfers between devices with their start and end apart: 20, of which 1 were waited for; matrix products, arithmetic and copies ran while one was open for 0% of the time, Pallas kernels for 0%

profile of v6, /device:TPU:183, one launch (start us, length us, event | category | flops | bytes accessed | tf_op | source)
XLA Modules:
  0.0 71.7 jit_solution(4270724862451960119)
XLA Ops:
  0.6 1.3 %pack.1 = (bf16[640,384]{1,0:T(8,128)(2,1)S(1)}, bf16[256,384]{1,0:T(8,128)(2,1)S(1)}, bf16[1024,384]{1,0:T(8,128)(2,1)S(1)}) custom-call(s32[1]{0:T(128)} %bitcast.place, bf16[1,384,384]{2,1,0:T(8,128)(2,1)} %inv.8, bf16[1,384,384]{2,1,0:T(8,128)(2,1)} %low.8, bf16[1,384,384]{2,1,0:T(8,128)(2,1)} %up.8, bf16[1,384,384]{2,1,0:T(8,128)(2,1)} %top.1, ...), custom_call_target="tpu_custom_call" | custom-call | tf_op jit(solution)/shard_map/pack/pallas_call | solution.py:397
  1.9 0.7 collective-permute-start.3
  2.6 0.7 collective-permute-start.4
  3.3 0.7 collective-permute-start.14
  4.0 0.8 %collective-permute-start.16 = (bf16[1024,384]{1,0:T(8,128)(2,1)S(1)}, bf16[1024,384]{1,0:T(8,128)(2,1)S(1)}, u32[]{:S(2)}, u32[]{:S(2)}) collective-permute-start(bf16[1024,384]{1,0:T(8,128)(2,1)S(1)} %get-tuple-element.13.own_in), channel_id=1, source_target_pairs={{16,0},{144,128},{272,256},{400,384},{17,1},{145,129},{273,257},{4... | collective-permute-start | bytes 2359304 | tf_op jit(solution)/shard_map/ppermute | solution.py:381
  4.8 0.7 collective-permute-start.10
  5.5 0.7 collective-permute-start.15
  6.2 0.7 collective-permute-start.1
  6.9 0.7 collective-permute-start.9
  7.6 0.7 collective-permute-start.2
  8.3 0.7 collective-permute-start.5
  9.1 0.7 collective-permute-start.6
  9.9 0.7 collective-permute-start.17
  10.6 24.4 %collective-permute-start = (bf16[1024,384]{1,0:T(8,128)(2,1)S(1)}, bf16[1024,384]{1,0:T(8,128)(2,1)S(1)}, u32[]{:S(2)}, u32[]{:S(2)}) collective-permute-start(bf16[1024,384]{1,0:T(8,128)(2,1)S(1)} %get-tuple-element.13.own_in), channel_id=1, source_target_pairs={{484,480},{492,488},{500,496},{508,504},{4,0},{12,8},{20,16},{28,2... | collective-permute-start | bytes 2359304 | tf_op jit(solution)/shard_map/ppermute | solution.py:381
  35.0 0.7 collective-permute-start.11
  35.7 0.7 collective-permute-start.12
  36.4 0.7 collective-permute-start.13
  37.2 0.7 collective-permute-start.7
  38.0 0.7 collective-permute-start.18
  38.7 0.7 collective-permute-start.8
  39.7 0.2 odd.1
  40.0 1.3 %collective-permute-start.19 = (bf16[896,384]{1,0:T(8,128)(2,1)S(1)}, bf16[896,384]{1,0:T(8,128)(2,1)S(1)}, u32[]{:S(2)}, u32[]{:S(2)}) collective-permute-start(bf16[896,384]{1,0:T(8,128)(2,1)S(1)} %get-tuple-element.23), channel_id=1, source_target_pairs={{480,484},{488,492},{496,500},{504,508},{0,4},{8,12},{16,20},{24,2... | collective-permute-start | bytes 2064392 | tf_op jit(solution)/shard_map/ppermute | solution.py:381
  41.3 28.4 %collective-permute-done.19.other = bf16[896,384]{1,0:T(8,128)(2,1)S(1)} collective-permute-done((bf16[896,384]{1,0:T(8,128)(2,1)S(1)}, bf16[896,384]{1,0:T(8,128)(2,1)S(1)}, u32[]{:S(2)}, u32[]{:S(2)}) %collective-permute-start.19) | collective-permute-done | bytes 688160 | tf_op jit(solution)/shard_map/ppermute | solution.py:381
  69.7 1.8 %interior.1 = (bf16[2,384,384]{2,1,0:T(8,128)(2,1)}, bf16[2,384,384]{2,1,0:T(8,128)(2,1)}) custom-call(s32[1]{0:T(128)} %bitcast.place, bf16[1,384,384]{2,1,0:T(8,128)(2,1)S(1)} %copy-done.3, bf16[1,384,384]{2,1,0:T(8,128)(2,1)S(1)} %copy-done.4, bf16[1,384,384]{2,1,0:T(8,128)(2,1)S(1)} %copy-done.5, bf16[896,384]{1,0:T(8,128)(2,1)S(1)} %get-tuple-element.22.own, ...), custom_call_target="tpu_custom_call" | custom-call | tf_op jit(solution)/shard_map/interior/pallas_call | solution.py:481
  (35 shorter events, 0.4 us)
Async XLA Ops:
  1.9 3.6 %collective-permute-start.3 = (bf16[256,384]{1,0:T(8,128)(2,1)S(1)}, bf16[256,384]{1,0:T(8,128)(2,1)S(1)}, u32[]{:S(2)}, u32[]{:S(2)}) collective-permute-start(bf16[256,384]{1,0:T(8,128)(2,1)S(1)} %get-tuple-element.15.d_in), channel_id=1, source_target_pairs={{480,432},{32,16},{96,48},{160,144},{224,176},{288,272},{352,304},... | collective-permute-start | bytes 589832 | tf_op jit(solution)/shard_map/ppermute | solution.py:381
  2.6 3.6 %collective-permute-start.4 = (bf16[256,384]{1,0:T(8,128)(2,1)S(1)}, bf16[256,384]{1,0:T(8,128)(2,1)S(1)}, u32[]{:S(2)}, u32[]{:S(2)}) collective-permute-start(bf16[256,384]{1,0:T(8,128)(2,1)S(1)} %get-tuple-element.15.d_in), channel_id=1, source_target_pairs={{480,464},{32,496},{96,80},{160,112},{224,208},{288,240},{352,336}... | collective-permute-start | bytes 589832 | tf_op jit(solution)/shard_map/ppermute | solution.py:381
  3.3 5.8 %collective-permute-start.14 = (bf16[640,384]{1,0:T(8,128)(2,1)S(1)}, bf16[640,384]{1,0:T(8,128)(2,1)S(1)}, u32[]{:S(2)}, u32[]{:S(2)}) collective-permute-start(bf16[640,384]{1,0:T(8,128)(2,1)S(1)} %get-tuple-element.14), channel_id=1, source_target_pairs={{480,0},{32,64},{96,128},{160,192},{224,256},{288,320},{352,384},{... | collective-permute-start | bytes 1474568 | tf_op jit(solution)/shard_map/ppermute | solution.py:381
  4.0 33.2 %copy-start = (bf16[1,384,384]{2,1,0:T(8,128)(2,1)S(1)}, bf16[1,384,384]{2,1,0:T(8,128)(2,1)}, u32[]{:S(2)}) copy-start(bf16[1,384,384]{2,1,0:T(8,128)(2,1)} %inv.8) | copy-start | bytes 884740
  4.0 33.2 %copy-start.1 = (bf16[1,384,384]{2,1,0:T(8,128)(2,1)S(1)}, bf16[1,384,384]{2,1,0:T(8,128)(2,1)}, u32[]{:S(2)}) copy-start(bf16[1,384,384]{2,1,0:T(8,128)(2,1)} %low.8) | copy-start | bytes 884740
  4.0 33.2 %copy-start.2 = (bf16[1,384,384]{2,1,0:T(8,128)(2,1)S(1)}, bf16[1,384,384]{2,1,0:T(8,128)(2,1)}, u32[]{:S(2)}) copy-start(bf16[1,384,384]{2,1,0:T(8,128)(2,1)} %up.8) | copy-start | bytes 884740
  4.0 31.0 %collective-permute-start.16 = (bf16[1024,384]{1,0:T(8,128)(2,1)S(1)}, bf16[1024,384]{1,0:T(8,128)(2,1)S(1)}, u32[]{:S(2)}, u32[]{:S(2)}) collective-permute-start(bf16[1024,384]{1,0:T(8,128)(2,1)S(1)} %get-tuple-element.13.own_in), channel_id=1, source_target_pairs={{16,0},{144,128},{272,256},{400,384},{17,1},{145,129},{273,257},{4... | collective-permute-start | bytes 2359304 | tf_op jit(solution)/shard_map/ppermute | solution.py:381
  4.8 2.1 %collective-permute-start.10 = (bf16[256,384]{1,0:T(8,128)(2,1)S(1)}, bf16[256,384]{1,0:T(8,128)(2,1)S(1)}, u32[]{:S(2)}, u32[]{:S(2)}) collective-permute-start(bf16[256,384]{1,0:T(8,128)(2,1)S(1)} %get-tuple-element.15.d_in), channel_id=1, source_target_pairs={{480,472},{32,24},{96,88},{160,152},{224,216},{288,280},{352,344},... | collective-permute-start | bytes 589832 | tf_op jit(solution)/shard_map/ppermute | solution.py:381
  5.5 2.1 %collective-permute-start.15 = (bf16[256,384]{1,0:T(8,128)(2,1)S(1)}, bf16[256,384]{1,0:T(8,128)(2,1)S(1)}, u32[]{:S(2)}, u32[]{:S(2)}) collective-permute-start(bf16[256,384]{1,0:T(8,128)(2,1)S(1)} %get-tuple-element.15.d_in), channel_id=1, source_target_pairs={{480,448},{32,0},{96,64},{160,128},{224,192},{288,256},{352,320},{... | collective-permute-start | bytes 589832 | tf_op jit(solution)/shard_map/ppermute | solution.py:381
  6.2 3.6 %collective-permute-start.1 = (bf16[640,384]{1,0:T(8,128)(2,1)S(1)}, bf16[640,384]{1,0:T(8,128)(2,1)S(1)}, u32[]{:S(2)}, u32[]{:S(2)}) collective-permute-start(bf16[640,384]{1,0:T(8,128)(2,1)S(1)} %get-tuple-element.14), channel_id=1, source_target_pairs={{480,16},{32,48},{96,144},{160,176},{224,272},{288,304},{352,400},... | collective-permute-start | bytes 1474568 | tf_op jit(solution)/shard_map/ppermute | solution.py:381
  6.9 1.4 %collective-permute-start.9 = (bf16[256,384]{1,0:T(8,128)(2,1)S(1)}, bf16[256,384]{1,0:T(8,128)(2,1)S(1)}, u32[]{:S(2)}, u32[]{:S(2)}) collective-permute-start(bf16[256,384]{1,0:T(8,128)(2,1)S(1)} %get-tuple-element.15.d_in), channel_id=1, source_target_pairs={{480,488},{32,40},{96,104},{160,168},{224,232},{288,296},{352,360}... | collective-permute-start | bytes 589832 | tf_op jit(solution)/shard_map/ppermute | solution.py:381
  7.6 3.0 %collective-permute-start.2 = (bf16[640,384]{1,0:T(8,128)(2,1)S(1)}, bf16[640,384]{1,0:T(8,128)(2,1)S(1)}, u32[]{:S(2)}, u32[]{:S(2)}) collective-permute-start(bf16[640,384]{1,0:T(8,128)(2,1)S(1)} %get-tuple-element.14), channel_id=1, source_target_pairs={{480,496},{32,80},{96,112},{160,208},{224,240},{288,336},{352,368}... | collective-permute-start | bytes 1474568 | tf_op jit(solution)/shard_map/ppermute | solution.py:381
  8.3 27.4 %collective-permute-start.5 = (bf16[1024,384]{1,0:T(8,128)(2,1)S(1)}, bf16[1024,384]{1,0:T(8,128)(2,1)S(1)}, u32[]{:S(2)}, u32[]{:S(2)}) collective-permute-start(bf16[1024,384]{1,0:T(8,128)(2,1)S(1)} %get-tuple-element.13.own_in), channel_id=1, source_target_pairs={{0,16},{64,48},{128,144},{192,176},{256,272},{320,304},{384,400},{... | collective-permute-start | bytes 2359304 | tf_op jit(solution)/shard_map/ppermute | solution.py:381
  9.1 27.4 %collective-permute-start.6 = (bf16[1024,384]{1,0:T(8,128)(2,1)S(1)}, bf16[1024,384]{1,0:T(8,128)(2,1)S(1)}, u32[]{:S(2)}, u32[]{:S(2)}) collective-permute-start(bf16[1024,384]{1,0:T(8,128)(2,1)S(1)} %get-tuple-element.13.own_in), channel_id=1, source_target_pairs={{0,496},{64,80},{128,112},{192,208},{256,240},{320,336},{384,368},... | collective-permute-start | bytes 2359304 | tf_op jit(solution)/shard_map/ppermute | solution.py:381
  9.9 27.4 %collective-permute-start.17 = (bf16[1024,384]{1,0:T(8,128)(2,1)S(1)}, bf16[1024,384]{1,0:T(8,128)(2,1)S(1)}, u32[]{:S(2)}, u32[]{:S(2)}) collective-permute-start(bf16[1024,384]{1,0:T(8,128)(2,1)S(1)} %inputs.1), channel_id=1, source_target_pairs={{80,64},{208,192},{336,320},{464,448},{81,65},{209,193},{337,321},... | collective-permute-start | bytes 2359304 | tf_op jit(solution)/shard_map/ppermute | solution.py:381
  10.6 27.4 %collective-permute-start = (bf16[1024,384]{1,0:T(8,128)(2,1)S(1)}, bf16[1024,384]{1,0:T(8,128)(2,1)S(1)}, u32[]{:S(2)}, u32[]{:S(2)}) collective-permute-start(bf16[1024,384]{1,0:T(8,128)(2,1)S(1)} %get-tuple-element.13.own_in), channel_id=1, source_target_pairs={{484,480},{492,488},{500,496},{508,504},{4,0},{12,8},{20,16},{28,2... | collective-permute-start | bytes 2359304 | tf_op jit(solution)/shard_map/ppermute | solution.py:381
  35.0 3.7 %collective-permute-start.11 = (bf16[1024,384]{1,0:T(8,128)(2,1)S(1)}, bf16[1024,384]{1,0:T(8,128)(2,1)S(1)}, u32[]{:S(2)}, u32[]{:S(2)}) collective-permute-start(bf16[1024,384]{1,0:T(8,128)(2,1)S(1)} %get-tuple-element.13.own_in), channel_id=1, source_target_pairs={{488,480},{8,0},{40,32},{72,64},{104,96},{136,128},{168,160},{200,... | collective-permute-start | bytes 2359304 | tf_op jit(solution)/shard_map/ppermute | solution.py:381
  35.7 3.9 %collective-permute-start.12 = (bf16[1024,384]{1,0:T(8,128)(2,1)S(1)}, bf16[1024,384]{1,0:T(8,128)(2,1)S(1)}, u32[]{:S(2)}, u32[]{:S(2)}) collective-permute-start(bf16[1024,384]{1,0:T(8,128)(2,1)S(1)} %get-tuple-element.13.own_in), channel_id=1, source_target_pairs={{24,16},{88,80},{152,144},{216,208},{280,272},{344,336},{408,400},... | collective-permute-start | bytes 2359304 | tf_op jit(solution)/shard_map/ppermute | solution.py:381
  36.4 3.2 %collective-permute-start.13 = (bf16[1024,384]{1,0:T(8,128)(2,1)S(1)}, bf16[1024,384]{1,0:T(8,128)(2,1)S(1)}, u32[]{:S(2)}, u32[]{:S(2)}) collective-permute-start(bf16[1024,384]{1,0:T(8,128)(2,1)S(1)} %get-tuple-element.13.own_in), channel_id=1, source_target_pairs={{504,496},{56,48},{120,112},{184,176},{248,240},{312,304},{376,368... | collective-permute-start | bytes 2359304 | tf_op jit(solution)/shard_map/ppermute | solution.py:381
  37.2 2.4 %collective-permute-start.7 = (bf16[896,384]{1,0:T(8,128)(2,1)S(1)}, bf16[896,384]{1,0:T(8,128)(2,1)S(1)}, u32[]{:S(2)}, u32[]{:S(2)}) collective-permute-start(bf16[896,384]{1,0:T(8,128)(2,1)S(1)} %get-tuple-element.16.far_msg), channel_id=1, source_target_pairs={{496,504},{16,8},{48,56},{80,72},{112,120},{144,136},{176,184},{20... | collective-permute-start | bytes 2064392 | tf_op jit(solution)/shard_map/ppermute | solution.py:381
  38.0 1.6 %collective-permute-start.18 = (bf16[640,384]{1,0:T(8,128)(2,1)S(1)}, bf16[640,384]{1,0:T(8,128)(2,1)S(1)}, u32[]{:S(2)}, u32[]{:S(2)}) collective-permute-start(bf16[640,384]{1,0:T(8,128)(2,1)S(1)} %get-tuple-element.17.near_msg), channel_id=1, source_target_pairs={{496,480},{48,32},{112,96},{176,160},{240,224},{304,288},{368,352}... | collective-permute-start | bytes 1474568 | tf_op jit(solution)/shard_map/ppermute | solution.py:381
  38.7 1.0 %collective-permute-start.8 = (bf16[640,384]{1,0:T(8,128)(2,1)S(1)}, bf16[640,384]{1,0:T(8,128)(2,1)S(1)}, u32[]{:S(2)}, u32[]{:S(2)}) collective-permute-start(bf16[640,384]{1,0:T(8,128)(2,1)S(1)} %get-tuple-element.17.near_msg), channel_id=1, source_target_pairs={{496,488},{16,24},{48,40},{80,88},{112,104},{144,152},{176,168},{2... | collective-permute-start | bytes 1474568 | tf_op jit(solution)/shard_map/ppermute | solution.py:381
  39.7 30.0 %copy-start.3 = (bf16[1,384,384]{2,1,0:T(8,128)(2,1)S(1)}, bf16[1,384,384]{2,1,0:T(8,128)(2,1)}, u32[]{:S(2)}) copy-start(bf16[1,384,384]{2,1,0:T(8,128)(2,1)} %inv.9) | copy-start | bytes 884740
  40.0 29.7 %collective-permute-start.19 = (bf16[896,384]{1,0:T(8,128)(2,1)S(1)}, bf16[896,384]{1,0:T(8,128)(2,1)S(1)}, u32[]{:S(2)}, u32[]{:S(2)}) collective-permute-start(bf16[896,384]{1,0:T(8,128)(2,1)S(1)} %get-tuple-element.23), channel_id=1, source_target_pairs={{480,484},{488,492},{496,500},{504,508},{0,4},{8,12},{16,20},{24,2... | collective-permute-start | bytes 2064392 | tf_op jit(solution)/shard_map/ppermute | solution.py:381
  (2 other events, 59.9 us)

commit v7 on v6

--- a/solution.py
+++ b/solution.py
@@ -325,7 +325,8 @@
         pltpu.make_async_copy(w.at[:n, :n], out_diag.at[0], sems.at[0]),
         pltpu.make_async_copy(p_buf, out_below.at[0], sems.at[1]),
         pltpu.make_async_copy(q_buf, out_below.at[1], sems.at[2]),
-        pltpu.make_async_copy(d_buf, out_diag.at[1], sems.at[3]),
+        pltpu.make_async_copy(d_buf.at[:, : 2 * t], out_diag.at[1, :, : 2 * t], sems.at[3]),
+        pltpu.make_async_copy(d_buf.at[:, 2 * t :], out_diag.at[1, :, 2 * t :], sems.at[4]),
     ]
 
     def go(src, holds):
@@ -339,8 +340,10 @@
         writes[1].start()
         q_buf[...] = both[:, n:].T
         writes[2].start()
-        d_buf[...] = (inv[0].astype(F32) + mt(both, pair)).astype(BF)
+        d_buf[:, : 2 * t] = (inv[0, :, : 2 * t].astype(F32) + mt(both, pair[: 2 * t])).astype(BF)
         writes[3].start()
+        d_buf[:, 2 * t :] = (inv[0, :, 2 * t :].astype(F32) + mt(both, pair[2 * t :])).astype(BF)
+        writes[4].start()
 
     @pl.when(core == 0)
     def _():
@@ -483,7 +486,7 @@
         out_shape=(pair, pair),
         in_specs=[smem] + [vmem] * 5,
         out_specs=(anywhere,) * 2,
-        scratch_shapes=[square] + [block] * 3 + [pltpu.SemaphoreType.DMA((4,))],
+        scratch_shapes=[square] + [block] * 3 + [pltpu.SemaphoreType.DMA((5,))],
         compiler_params=params,
         name="interior",
     )(place, interior_inverse, interior_lower, interior_upper, *near(own, other))

time: 72.1 us -> 72 us (level)
  the two profiles are of different devices: /device:TPU:183 before, /device:TPU:169 now
where the time goes in v7:
time: 72 us; the launch traced here: 71.6 us
  starting transfers between devices  38.3 us (53%)
  waiting for transfers between devices  28.4 us (39%)
  Pallas kernels  3.58 us (5%)
  between operations  1.25 us (2%)
    ppermute x20, starting transfers between devices, moved(): return lax.ppermute(value, 'tm', pairs)  38.3 us
    ppermute x20, waiting for transfers between devices, moved(): return lax.ppermute(value, 'tm', pairs)  28.4 us
    pallas_call x1, Pallas kernels, on_device(): pl.pallas_call(interior_kernel, out_shape=(pair, pair), in_specs=[smem] +...  1.75 us
  transfers between devices with their start and end apart: 20, of which 1 were waited for; matrix products, arithmetic and copies ran while one was open for 0% of the time, Pallas kernels for 0%

profile of v7, /device:TPU:169, one launch (start us, length us, event | category | flops | bytes accessed | tf_op | source)
XLA Modules:
  0.0 71.6 jit_solution(10877810652053763793)
XLA Ops:
  0.6 1.3 %pack.1 = (bf16[640,384]{1,0:T(8,128)(2,1)S(1)}, bf16[256,384]{1,0:T(8,128)(2,1)S(1)}, bf16[1024,384]{1,0:T(8,128)(2,1)S(1)}) custom-call(s32[1]{0:T(128)} %bitcast.place, bf16[1,384,384]{2,1,0:T(8,128)(2,1)} %inv.8, bf16[1,384,384]{2,1,0:T(8,128)(2,1)} %low.8, bf16[1,384,384]{2,1,0:T(8,128)(2,1)} %up.8, bf16[1,384,384]{2,1,0:T(8,128)(2,1)} %top.1, ...), custom_call_target="tpu_custom_call" | custom-call | tf_op jit(solution)/shard_map/pack/pallas_call | solution.py:400
  1.9 0.7 collective-permute-start.3
  2.6 0.7 collective-permute-start.4
  3.3 0.7 collective-permute-start.14
  4.0 0.8 %collective-permute-start.16 = (bf16[1024,384]{1,0:T(8,128)(2,1)S(1)}, bf16[1024,384]{1,0:T(8,128)(2,1)S(1)}, u32[]{:S(2)}, u32[]{:S(2)}) collective-permute-start(bf16[1024,384]{1,0:T(8,128)(2,1)S(1)} %get-tuple-element.13.own_in), channel_id=1, source_target_pairs={{16,0},{144,128},{272,256},{400,384},{17,1},{145,129},{273,257},{4... | collective-permute-start | bytes 2359304 | tf_op jit(solution)/shard_map/ppermute | solution.py:384
  4.8 0.7 collective-permute-start.10
  5.5 0.7 collective-permute-start.15
  6.2 0.7 collective-permute-start.1
  6.9 0.7 collective-permute-start.9
  7.6 0.7 collective-permute-start.2
  8.3 0.7 collective-permute-start.5
  9.1 0.7 collective-permute-start.6
  9.9 0.7 collective-permute-start.17
  10.6 24.4 %collective-permute-start = (bf16[1024,384]{1,0:T(8,128)(2,1)S(1)}, bf16[1024,384]{1,0:T(8,128)(2,1)S(1)}, u32[]{:S(2)}, u32[]{:S(2)}) collective-permute-start(bf16[1024,384]{1,0:T(8,128)(2,1)S(1)} %get-tuple-element.13.own_in), channel_id=1, source_target_pairs={{484,480},{492,488},{500,496},{508,504},{4,0},{12,8},{20,16},{28,2... | collective-permute-start | bytes 2359304 | tf_op jit(solution)/shard_map/ppermute | solution.py:384
  35.0 0.7 collective-permute-start.11
  35.7 0.7 collective-permute-start.12
  36.4 0.7 collective-permute-start.13
  37.2 0.7 collective-permute-start.7
  38.0 0.7 collective-permute-start.18
  38.7 0.7 collective-permute-start.8
  39.7 0.2 odd.1
  40.0 1.3 %collective-permute-start.19 = (bf16[896,384]{1,0:T(8,128)(2,1)S(1)}, bf16[896,384]{1,0:T(8,128)(2,1)S(1)}, u32[]{:S(2)}, u32[]{:S(2)}) collective-permute-start(bf16[896,384]{1,0:T(8,128)(2,1)S(1)} %get-tuple-element.23), channel_id=1, source_target_pairs={{480,484},{488,492},{496,500},{504,508},{0,4},{8,12},{16,20},{24,2... | collective-permute-start | bytes 2064392 | tf_op jit(solution)/shard_map/ppermute | solution.py:384
  41.3 28.4 %collective-permute-done.19.other = bf16[896,384]{1,0:T(8,128)(2,1)S(1)} collective-permute-done((bf16[896,384]{1,0:T(8,128)(2,1)S(1)}, bf16[896,384]{1,0:T(8,128)(2,1)S(1)}, u32[]{:S(2)}, u32[]{:S(2)}) %collective-permute-start.19) | collective-permute-done | bytes 688160 | tf_op jit(solution)/shard_map/ppermute | solution.py:384
  69.7 1.8 %interior.1 = (bf16[2,384,384]{2,1,0:T(8,128)(2,1)}, bf16[2,384,384]{2,1,0:T(8,128)(2,1)}) custom-call(s32[1]{0:T(128)} %bitcast.place, bf16[1,384,384]{2,1,0:T(8,128)(2,1)S(1)} %copy-done.3, bf16[1,384,384]{2,1,0:T(8,128)(2,1)S(1)} %copy-done.4, bf16[1,384,384]{2,1,0:T(8,128)(2,1)S(1)} %copy-done.5, bf16[896,384]{1,0:T(8,128)(2,1)S(1)} %get-tuple-element.22.own, ...), custom_call_target="tpu_custom_call" | custom-call | tf_op jit(solution)/shard_map/interior/pallas_call | solution.py:484
  (35 shorter events, 0.4 us)
Async XLA Ops:
  1.9 3.6 %collective-permute-start.3 = (bf16[256,384]{1,0:T(8,128)(2,1)S(1)}, bf16[256,384]{1,0:T(8,128)(2,1)S(1)}, u32[]{:S(2)}, u32[]{:S(2)}) collective-permute-start(bf16[256,384]{1,0:T(8,128)(2,1)S(1)} %get-tuple-element.15.d_in), channel_id=1, source_target_pairs={{480,432},{32,16},{96,48},{160,144},{224,176},{288,272},{352,304},... | collective-permute-start | bytes 589832 | tf_op jit(solution)/shard_map/ppermute | solution.py:384
  2.6 3.6 %collective-permute-start.4 = (bf16[256,384]{1,0:T(8,128)(2,1)S(1)}, bf16[256,384]{1,0:T(8,128)(2,1)S(1)}, u32[]{:S(2)}, u32[]{:S(2)}) collective-permute-start(bf16[256,384]{1,0:T(8,128)(2,1)S(1)} %get-tuple-element.15.d_in), channel_id=1, source_target_pairs={{480,464},{32,496},{96,80},{160,112},{224,208},{288,240},{352,336}... | collective-permute-start | bytes 589832 | tf_op jit(solution)/shard_map/ppermute | solution.py:384
  3.3 5.8 %collective-permute-start.14 = (bf16[640,384]{1,0:T(8,128)(2,1)S(1)}, bf16[640,384]{1,0:T(8,128)(2,1)S(1)}, u32[]{:S(2)}, u32[]{:S(2)}) collective-permute-start(bf16[640,384]{1,0:T(8,128)(2,1)S(1)} %get-tuple-element.14), channel_id=1, source_target_pairs={{480,0},{32,64},{96,128},{160,192},{224,256},{288,320},{352,384},{... | collective-permute-start | bytes 1474568 | tf_op jit(solution)/shard_map/ppermute | solution.py:384
  4.0 33.2 %copy-start = (bf16[1,384,384]{2,1,0:T(8,128)(2,1)S(1)}, bf16[1,384,384]{2,1,0:T(8,128)(2,1)}, u32[]{:S(2)}) copy-start(bf16[1,384,384]{2,1,0:T(8,128)(2,1)} %inv.8) | copy-start | bytes 884740
  4.0 33.2 %copy-start.1 = (bf16[1,384,384]{2,1,0:T(8,128)(2,1)S(1)}, bf16[1,384,384]{2,1,0:T(8,128)(2,1)}, u32[]{:S(2)}) copy-start(bf16[1,384,384]{2,1,0:T(8,128)(2,1)} %low.8) | copy-start | bytes 884740
  4.0 33.2 %copy-start.2 = (bf16[1,384,384]{2,1,0:T(8,128)(2,1)S(1)}, bf16[1,384,384]{2,1,0:T(8,128)(2,1)}, u32[]{:S(2)}) copy-start(bf16[1,384,384]{2,1,0:T(8,128)(2,1)} %up.8) | copy-start | bytes 884740
  4.0 31.0 %collective-permute-start.16 = (bf16[1024,384]{1,0:T(8,128)(2,1)S(1)}, bf16[1024,384]{1,0:T(8,128)(2,1)S(1)}, u32[]{:S(2)}, u32[]{:S(2)}) collective-permute-start(bf16[1024,384]{1,0:T(8,128)(2,1)S(1)} %get-tuple-element.13.own_in), channel_id=1, source_target_pairs={{16,0},{144,128},{272,256},{400,384},{17,1},{145,129},{273,257},{4... | collective-permute-start | bytes 2359304 | tf_op jit(solution)/shard_map/ppermute | solution.py:384
  4.8 2.1 %collective-permute-start.10 = (bf16[256,384]{1,0:T(8,128)(2,1)S(1)}, bf16[256,384]{1,0:T(8,128)(2,1)S(1)}, u32[]{:S(2)}, u32[]{:S(2)}) collective-permute-start(bf16[256,384]{1,0:T(8,128)(2,1)S(1)} %get-tuple-element.15.d_in), channel_id=1, source_target_pairs={{480,472},{32,24},{96,88},{160,152},{224,216},{288,280},{352,344},... | collective-permute-start | bytes 589832 | tf_op jit(solution)/shard_map/ppermute | solution.py:384
  5.5 2.1 %collective-permute-start.15 = (bf16[256,384]{1,0:T(8,128)(2,1)S(1)}, bf16[256,384]{1,0:T(8,128)(2,1)S(1)}, u32[]{:S(2)}, u32[]{:S(2)}) collective-permute-start(bf16[256,384]{1,0:T(8,128)(2,1)S(1)} %get-tuple-element.15.d_in), channel_id=1, source_target_pairs={{480,448},{32,0},{96,64},{160,128},{224,192},{288,256},{352,320},{... | collective-permute-start | bytes 589832 | tf_op jit(solution)/shard_map/ppermute | solution.py:384
  6.2 3.6 %collective-permute-start.1 = (bf16[640,384]{1,0:T(8,128)(2,1)S(1)}, bf16[640,384]{1,0:T(8,128)(2,1)S(1)}, u32[]{:S(2)}, u32[]{:S(2)}) collective-permute-start(bf16[640,384]{1,0:T(8,128)(2,1)S(1)} %get-tuple-element.14), channel_id=1, source_target_pairs={{480,16},{32,48},{96,144},{160,176},{224,272},{288,304},{352,400},... | collective-permute-start | bytes 1474568 | tf_op jit(solution)/shard_map/ppermute | solution.py:384
  6.9 1.4 %collective-permute-start.9 = (bf16[256,384]{1,0:T(8,128)(2,1)S(1)}, bf16[256,384]{1,0:T(8,128)(2,1)S(1)}, u32[]{:S(2)}, u32[]{:S(2)}) collective-permute-start(bf16[256,384]{1,0:T(8,128)(2,1)S(1)} %get-tuple-element.15.d_in), channel_id=1, source_target_pairs={{480,488},{32,40},{96,104},{160,168},{224,232},{288,296},{352,360}... | collective-permute-start | bytes 589832 | tf_op jit(solution)/shard_map/ppermute | solution.py:384
  7.6 3.0 %collective-permute-start.2 = (bf16[640,384]{1,0:T(8,128)(2,1)S(1)}, bf16[640,384]{1,0:T(8,128)(2,1)S(1)}, u32[]{:S(2)}, u32[]{:S(2)}) collective-permute-start(bf16[640,384]{1,0:T(8,128)(2,1)S(1)} %get-tuple-element.14), channel_id=1, source_target_pairs={{480,496},{32,80},{96,112},{160,208},{224,240},{288,336},{352,368}... | collective-permute-start | bytes 1474568 | tf_op jit(solution)/shard_map/ppermute | solution.py:384
  8.3 27.4 %collective-permute-start.5 = (bf16[1024,384]{1,0:T(8,128)(2,1)S(1)}, bf16[1024,384]{1,0:T(8,128)(2,1)S(1)}, u32[]{:S(2)}, u32[]{:S(2)}) collective-permute-start(bf16[1024,384]{1,0:T(8,128)(2,1)S(1)} %get-tuple-element.13.own_in), channel_id=1, source_target_pairs={{0,16},{64,48},{128,144},{192,176},{256,272},{320,304},{384,400},{... | collective-permute-start | bytes 2359304 | tf_op jit(solution)/shard_map/ppermute | solution.py:384
  9.1 27.4 %collective-permute-start.6 = (bf16[1024,384]{1,0:T(8,128)(2,1)S(1)}, bf16[1024,384]{1,0:T(8,128)(2,1)S(1)}, u32[]{:S(2)}, u32[]{:S(2)}) collective-permute-start(bf16[1024,384]{1,0:T(8,128)(2,1)S(1)} %get-tuple-element.13.own_in), channel_id=1, source_target_pairs={{0,496},{64,80},{128,112},{192,208},{256,240},{320,336},{384,368},... | collective-permute-start | bytes 2359304 | tf_op jit(solution)/shard_map/ppermute | solution.py:384
  9.9 27.4 %collective-permute-start.17 = (bf16[1024,384]{1,0:T(8,128)(2,1)S(1)}, bf16[1024,384]{1,0:T(8,128)(2,1)S(1)}, u32[]{:S(2)}, u32[]{:S(2)}) collective-permute-start(bf16[1024,384]{1,0:T(8,128)(2,1)S(1)} %inputs.1), channel_id=1, source_target_pairs={{80,64},{208,192},{336,320},{464,448},{81,65},{209,193},{337,321},... | collective-permute-start | bytes 2359304 | tf_op jit(solution)/shard_map/ppermute | solution.py:384
  10.6 27.4 %collective-permute-start = (bf16[1024,384]{1,0:T(8,128)(2,1)S(1)}, bf16[1024,384]{1,0:T(8,128)(2,1)S(1)}, u32[]{:S(2)}, u32[]{:S(2)}) collective-permute-start(bf16[1024,384]{1,0:T(8,128)(2,1)S(1)} %get-tuple-element.13.own_in), channel_id=1, source_target_pairs={{484,480},{492,488},{500,496},{508,504},{4,0},{12,8},{20,16},{28,2... | collective-permute-start | bytes 2359304 | tf_op jit(solution)/shard_map/ppermute | solution.py:384
  35.0 3.7 %collective-permute-start.11 = (bf16[1024,384]{1,0:T(8,128)(2,1)S(1)}, bf16[1024,384]{1,0:T(8,128)(2,1)S(1)}, u32[]{:S(2)}, u32[]{:S(2)}) collective-permute-start(bf16[1024,384]{1,0:T(8,128)(2,1)S(1)} %get-tuple-element.13.own_in), channel_id=1, source_target_pairs={{488,480},{8,0},{40,32},{72,64},{104,96},{136,128},{168,160},{200,... | collective-permute-start | bytes 2359304 | tf_op jit(solution)/shard_map/ppermute | solution.py:384
  35.7 3.9 %collective-permute-start.12 = (bf16[1024,384]{1,0:T(8,128)(2,1)S(1)}, bf16[1024,384]{1,0:T(8,128)(2,1)S(1)}, u32[]{:S(2)}, u32[]{:S(2)}) collective-permute-start(bf16[1024,384]{1,0:T(8,128)(2,1)S(1)} %get-tuple-element.13.own_in), channel_id=1, source_target_pairs={{24,16},{88,80},{152,144},{216,208},{280,272},{344,336},{408,400},... | collective-permute-start | bytes 2359304 | tf_op jit(solution)/shard_map/ppermute | solution.py:384
  36.4 3.2 %collective-permute-start.13 = (bf16[1024,384]{1,0:T(8,128)(2,1)S(1)}, bf16[1024,384]{1,0:T(8,128)(2,1)S(1)}, u32[]{:S(2)}, u32[]{:S(2)}) collective-permute-start(bf16[1024,384]{1,0:T(8,128)(2,1)S(1)} %get-tuple-element.13.own_in), channel_id=1, source_target_pairs={{504,496},{56,48},{120,112},{184,176},{248,240},{312,304},{376,368... | collective-permute-start | bytes 2359304 | tf_op jit(solution)/shard_map/ppermute | solution.py:384
  37.2 2.4 %collective-permute-start.7 = (bf16[896,384]{1,0:T(8,128)(2,1)S(1)}, bf16[896,384]{1,0:T(8,128)(2,1)S(1)}, u32[]{:S(2)}, u32[]{:S(2)}) collective-permute-start(bf16[896,384]{1,0:T(8,128)(2,1)S(1)} %get-tuple-element.16.far_msg), channel_id=1, source_target_pairs={{496,504},{16,8},{48,56},{80,72},{112,120},{144,136},{176,184},{20... | collective-permute-start | bytes 2064392 | tf_op jit(solution)/shard_map/ppermute | solution.py:384
  38.0 1.6 %collective-permute-start.18 = (bf16[640,384]{1,0:T(8,128)(2,1)S(1)}, bf16[640,384]{1,0:T(8,128)(2,1)S(1)}, u32[]{:S(2)}, u32[]{:S(2)}) collective-permute-start(bf16[640,384]{1,0:T(8,128)(2,1)S(1)} %get-tuple-element.17.near_msg), channel_id=1, source_target_pairs={{496,480},{48,32},{112,96},{176,160},{240,224},{304,288},{368,352}... | collective-permute-start | bytes 1474568 | tf_op jit(solution)/shard_map/ppermute | solution.py:384
  38.7 1.0 %collective-permute-start.8 = (bf16[640,384]{1,0:T(8,128)(2,1)S(1)}, bf16[640,384]{1,0:T(8,128)(2,1)S(1)}, u32[]{:S(2)}, u32[]{:S(2)}) collective-permute-start(bf16[640,384]{1,0:T(8,128)(2,1)S(1)} %get-tuple-element.17.near_msg), channel_id=1, source_target_pairs={{496,488},{16,24},{48,40},{80,88},{112,104},{144,152},{176,168},{2... | collective-permute-start | bytes 1474568 | tf_op jit(solution)/shard_map/ppermute | solution.py:384
  39.7 30.0 %copy-start.3 = (bf16[1,384,384]{2,1,0:T(8,128)(2,1)S(1)}, bf16[1,384,384]{2,1,0:T(8,128)(2,1)}, u32[]{:S(2)}) copy-start(bf16[1,384,384]{2,1,0:T(8,128)(2,1)} %inv.9) | copy-start | bytes 884740
  40.0 29.7 %collective-permute-start.19 = (bf16[896,384]{1,0:T(8,128)(2,1)S(1)}, bf16[896,384]{1,0:T(8,128)(2,1)S(1)}, u32[]{:S(2)}, u32[]{:S(2)}) collective-permute-start(bf16[896,384]{1,0:T(8,128)(2,1)S(1)} %get-tuple-element.23), channel_id=1, source_target_pairs={{480,484},{488,492},{496,500},{504,508},{0,4},{8,12},{16,20},{24,2... | collective-permute-start | bytes 2064392 | tf_op jit(solution)/shard_map/ppermute | solution.py:384
  (2 other events, 59.9 us)
